TPU v7x, 32 devices: a whole 2x2x4 slice. The times are simulated.
32 devices in a mesh: fsdp: 4 (over z), adapter: 8 (over y, x, core).
Axes of the slice: x: 2, y: 2, z: 4, core: 2. Of those that a mesh axis runs over, the one named last changes fastest.
Arguments:
- tokens: bfloat16 [2048, 8192], P('adapter', 'fsdp'), may hold values from -6 to 6
- tenant: int32 [2048], P('adapter'), may hold values from 0 to 63, as said below
- send_list: int32 [8, 8, 128], P('adapter'), may hold values from -1 to 255, as said below
- base_weight: bfloat16 [8192, 2048], P('fsdp'), may hold values from -0.09375 to 0.09375
- down_weight: bfloat16 [64, 8192, 128], P('adapter', 'fsdp'), may hold values from -0.0625 to 0.0625
- up_projection_weight: bfloat16 [64, 64, 2048], P('adapter', None, 'fsdp'), may hold values from -0.75 to 0.75
- cotangent: bfloat16 [2048, 2048], P('adapter', 'fsdp'), may hold values from -3 to 3
Outputs:
- projected: bfloat16 [2048, 2048], P('adapter', 'fsdp')
- token_gradient: bfloat16 [2048, 8192], P('adapter', 'fsdp')
- down_weight_gradient: bfloat16 [64, 8192, 128], P('adapter', 'fsdp')
- up_weight_gradient: bfloat16 [64, 64, 2048], P('adapter', None, 'fsdp')
Inputs may be any that keep to these rules, and one draw needn't show every extreme that they name: `tenant`: adapter t belongs to owner t // 8. Among the 256 rows of one index of adapter at most 128 belong to the adapters of one owner, and one owner, the same for every index, has exactly 128 of them. send_list[i, o, :] lists in increasing order the rows (numbered within the 256 rows of index i of adapter) whose tenant belongs to owner o, then -1 in the slots left; every row stands in exactly one list.
All inputs are finite; a program needn't handle non-finite values.
Results may differ from a plain program's by a relative error of at most 0.005.
Values may be sent and summed in bfloat16 or wider, within the bound.
No kernel may reach another device: no remote copies, remote signals or barrier semaphores. Data moves between devices by JAX's collectives and lax.ppermute only.
A program may use at most 128 MiB of HBM per device.

v0:
```python
import jax
import jax.numpy as jnp
from jax import lax
from jax.sharding import PartitionSpec as P

KV = 1024


adapter_scale = 0.5


def down_partial(input_rows, weights_f, down_weight):
    low_all = jnp.einsum("sd,ldk->slk", input_rows, down_weight, preferred_element_type=jnp.float32)
    return jnp.sum(low_all * weights_f[:, :, None], axis=1)


def grad_partial(rows_dy, weights_f, up_projection_weight, selected_half):
    rank_size = up_projection_weight.shape[1]
    back_all = jnp.einsum(
        "sc,lrc->slr", rows_dy, up_projection_weight, preferred_element_type=jnp.float32
    )
    half_sum = jnp.sum(back_all * weights_f[:, :, None], axis=1)
    placed = jnp.zeros((rows_dy.shape[0], 2 * rank_size), jnp.float32)
    zero_idx = jnp.zeros((), jnp.int32)
    return lax.dynamic_update_slice(placed, half_sum, (zero_idx, selected_half * rank_size))


def forward_holder(low_rank, weight_table, up_projection_weight, selected_half):
    rank_size = up_projection_weight.shape[1]
    low_half = lax.dynamic_slice_in_dim(low_rank, selected_half * rank_size, rank_size, 1)
    broadcast_rows = low_half[:, None, :] * weight_table[:, :, None]
    adapter_update = adapter_scale * jnp.einsum(
        "slr,lrc->sc", broadcast_rows, up_projection_weight, preferred_element_type=jnp.float32
    )
    return (adapter_update.astype(jnp.bfloat16), broadcast_rows)


def backward_owner(back_low, weight_table, input_rows, rows_dy, broadcast_rows, down_weight):
    widened_rows = back_low[:, None, :] * weight_table[:, :, None]
    backward_update = adapter_scale * jnp.einsum(
        "wnr,nyr->wy", widened_rows, down_weight, preferred_element_type=jnp.float32
    )
    down_weight_gradient = adapter_scale * jnp.einsum(
        "wq,wmu->mqu", input_rows, widened_rows, preferred_element_type=jnp.float32
    )
    up_weight_gradient = adapter_scale * jnp.einsum(
        "slr,sc->lrc", broadcast_rows, rows_dy, preferred_element_type=jnp.float32
    )
    return (
        backward_update.astype(jnp.bfloat16),
        down_weight_gradient.astype(jnp.bfloat16),
        up_weight_gradient.astype(jnp.bfloat16),
    )


def shards(tokens, tenant, send_list, base_weight, down_weight, up_projection_weight, cotangent):
    rows_here = tokens.shape[0]
    width_here = tokens.shape[1]
    column_span = cotangent.shape[1]
    adapters_here = down_weight.shape[0]
    holder_list = send_list.shape[1]
    slot_capacity = send_list.shape[2]
    total_slots = holder_list * slot_capacity
    listed = send_list[0]
    present = listed >= 0
    safe_rows = jnp.where(present, listed, 0)
    local_ids = tenant % adapters_here
    picked_ids = local_ids[safe_rows]
    adapter_ids = jnp.arange(adapters_here, dtype=jnp.int32)
    selector = (
        (picked_ids[:, :, None] == adapter_ids[None, None, :]) & present[:, :, None]
    ).astype(jnp.bfloat16)
    send_x = tokens[safe_rows]
    send_dy = cotangent[safe_rows]
    drop_rows = jnp.where(present, listed, rows_here).reshape(total_slots)
    fsdp_pos = lax.axis_index("fsdp")
    selected_half = fsdp_pos * column_span // KV
    weight_cols = base_weight
    local_base_output = lax.psum_scatter(
        lax.dot_general(
            weight_cols, tokens, (((0,), (1,)), ((), ())), preferred_element_type=jnp.float32
        ),
        "fsdp",
        scatter_dimension=0,
        tiled=True,
    ).T
    weight_cols = base_weight
    input_frozen_part = lax.dot_general(
        lax.all_gather(cotangent, "fsdp", axis=1, tiled=True),
        weight_cols,
        (((1,), (1,)), ((), ())),
        preferred_element_type=jnp.float32,
    )
    recv_x, recv_sel = (
        lax.all_to_all(send_x, "adapter", split_axis=0, concat_axis=0, tiled=True),
        lax.all_to_all(selector, "adapter", split_axis=0, concat_axis=0, tiled=True),
    )
    input_rows = recv_x.reshape(total_slots, width_here)
    weight_table = recv_sel.reshape(total_slots, adapters_here)
    weights_f = weight_table.astype(jnp.float32)
    low_term = down_partial(input_rows, weights_f, down_weight)
    reduced_rank_sum = lax.psum(low_term, "fsdp")
    adapter_update, broadcast_rows = forward_holder(
        reduced_rank_sum.astype(jnp.bfloat16), weight_table, up_projection_weight, selected_half
    )
    got_delta = lax.all_to_all(
        adapter_update.reshape(holder_list, slot_capacity, column_span),
        "adapter",
        split_axis=0,
        concat_axis=0,
        tiled=True,
    )
    recv_dy = lax.all_to_all(send_dy, "adapter", split_axis=0, concat_axis=0, tiled=True)
    rows_dy = recv_dy.reshape(total_slots, column_span)
    back_sum = lax.psum(
        grad_partial(rows_dy, weights_f, up_projection_weight, selected_half), "fsdp"
    )
    backward_update, down_weight_gradient, up_weight_gradient = backward_owner(
        back_sum.astype(jnp.bfloat16),
        weight_table,
        input_rows,
        rows_dy,
        broadcast_rows,
        down_weight,
    )
    got_back = lax.all_to_all(
        backward_update.reshape(holder_list, slot_capacity, width_here),
        "adapter",
        split_axis=0,
        concat_axis=0,
        tiled=True,
    )
    adapter_columns = (
        jnp.zeros((rows_here, column_span), jnp.float32)
        .at[drop_rows]
        .add(got_delta.reshape(total_slots, column_span).astype(jnp.float32), mode="drop")
    )
    projected = (local_base_output + adapter_columns).astype(jnp.bfloat16)
    adapter_backward = (
        jnp.zeros((rows_here, width_here), jnp.float32)
        .at[drop_rows]
        .add(got_back.reshape(total_slots, width_here).astype(jnp.float32), mode="drop")
    )
    token_gradient = (input_frozen_part + adapter_backward).astype(jnp.bfloat16)
    return (projected, token_gradient, down_weight_gradient, up_weight_gradient)


def solution(mesh):
    in_specs = (
        P("adapter", "fsdp"),
        P("adapter"),
        P("adapter", None, None),
        P("fsdp", None),
        P("adapter", "fsdp", None),
        P("adapter", None, "fsdp"),
        P("adapter", "fsdp"),
    )
    out_specs = (
        P("adapter", "fsdp"),
        P("adapter", "fsdp"),
        P("adapter", "fsdp", None),
        P("adapter", None, "fsdp"),
    )
    return jax.shard_map(shards, mesh=mesh, in_specs=in_specs, out_specs=out_specs, check_vma=False)
```

profile of v0, /device:TPU:0, one launch (start us, length us, event | category | flops | bytes accessed | tf_op | source)
XLA Modules:
  0.0 267.3 jit_solution(12076343468223439721)
XLA Ops:
  7.2 0.0 copy-start
  7.2 0.0 copy-start.1
  7.2 0.8 fusion.29
  8.0 0.7 compare_bitcast_fusion
  8.7 0.7 and_select_fusion
  9.4 6.8 %gather_fusion.1 = s32[1024]{0:T(1024)S(1)} fusion(s32[256]{0:T(256)S(1)} %and_select_fusion, s32[1024]{0:T(1024)S(1)} %fusion.29), kind=kCustom, calls=%fused_computation.1 | custom fusion | bytes 12288 | tf_op jit(solution)/shard_map/gather | solution.py:68
  16.2 0.6 fusion.27
  16.8 5.2 %all-to-all-start.1 = ((bf16[8,128,8]{1,2,0:T(8,128)(2,1)}), bf16[8,128,8]{1,2,0:T(8,128)(2,1)S(1)}, u32[]{:S(2)}, u32[]{:S(2)}) async-start(bf16[8,128,8]{1,2,0:T(8,128)(2,1)} %fusion.27), calls=%async_computation.2 | async-start | bytes 32768 | tf_op jit(solution)/shard_map/all_to_all | solution.py:96
  22.0 0.0 copy-done.1
  22.0 5.1 %gather_fusion.2 = bf16[1024,512]{1,0:T(8,128)(2,1)} fusion(bf16[256,512]{1,0:T(8,128)(2,1)S(1)} %copy-done.1, s32[1024]{0:T(1024)S(1)} %fusion.29), kind=kCustom, calls=%fused_computation.2 | custom fusion | bytes 2101248 | tf_op jit(solution)/shard_map/gather | solution.py:74
  27.1 0.0 all-to-all-done.1
  27.1 4.2 %all-to-all-start.3 = ((bf16[8,128,512]{2,1,0:T(8,128)(2,1)}), bf16[8,128,512]{2,1,0:T(8,128)(2,1)S(1)}, u32[]{:S(2)}, u32[]{:S(2)}) async-start(bf16[8,128,512]{2,1,0:T(8,128)(2,1)} %bitcast.14), calls=%async_computation.4 | async-start | bytes 2097152 | tf_op jit(solution)/shard_map/all_to_all | solution.py:113
  31.3 0.0 copy-done
  31.3 6.0 %gather_fusion = bf16[1024,2048]{1,0:T(8,128)(2,1)} fusion(bf16[256,2048]{1,0:T(8,128)(2,1)S(1)} %copy-done, s32[1024]{0:T(1024)S(1)} %fusion.29), kind=kCustom, calls=%fused_computation | custom fusion | bytes 8392704 | tf_op jit(solution)/shard_map/gather | solution.py:73
  37.2 9.4 %all-to-all-done.3 = bf16[8,128,512]{2,1,0:T(8,128)(2,1)S(1)} async-done(((bf16[8,128,512]{2,1,0:T(8,128)(2,1)}), bf16[8,128,512]{2,1,0:T(8,128)(2,1)S(1)}, u32[]{:S(2)}, u32[]{:S(2)}) %all-to-all-start.3) | async-done | bytes 1048608 | tf_op jit(solution)/shard_map/all_to_all | solution.py:113
  46.7 4.6 %all-to-all-start = ((bf16[8,128,2048]{2,1,0:T(8,128)(2,1)}), bf16[8,128,2048]{2,1,0:T(8,128)(2,1)}, u32[]{:S(2)}, u32[]{:S(2)}) async-start(bf16[8,128,2048]{2,1,0:T(8,128)(2,1)} %bitcast.50), calls=%async_computation.1 | async-start | bytes 8388608 | tf_op jit(solution)/shard_map/all_to_all | solution.py:95
  51.3 0.0 all-gather.2.cloned.1.call-start
  51.3 0.7 all-gather.2.cloned.1.call-update
  52.0 0.0 copy-start.3
  52.0 0.0 reduce-scatter.2.cloned.1.call-start
  52.1 7.2 %fusion.31 = f32[2048,256]{1,0:T(8,128)} fusion(bf16[2048,2048]{1,0:T(8,128)(2,1)} %param.10, bf16[256,2048]{1,0:T(8,128)(2,1)S(1)} %copy-done), kind=kOutput, calls=%fused_computation.49 | convolution fusion | flops 2147483648 | bytes 11534336 | tf_op jit(solution)/shard_map/dot_general | solution.py:80
  59.3 0.0 reduce-scatter.2.cloned.1.call-update
  59.3 0.0 copy-done.3
  59.4 0.7 multiply_reduce_fusion.1
  60.2 40.2 %all-to-all-done = bf16[8,128,2048]{2,1,0:T(8,128)(2,1)} async-done(((bf16[8,128,2048]{2,1,0:T(8,128)(2,1)}), bf16[8,128,2048]{2,1,0:T(8,128)(2,1)}, u32[]{:S(2)}, u32[]{:S(2)}) %all-to-all-start) | async-done | bytes 4194336 | tf_op jit(solution)/shard_map/all_to_all | solution.py:95
  100.4 7.6 %multiply_reduce_fusion = f32[1024,128]{1,0:T(8,128)S(1)} fusion(bf16[1024,2048,1]{1,0,2:T(8,128)(2,1)} %bitcast.7, bf16[8,2048,128]{2,1,0:T(8,128)(2,1)} %param.11, f32[1024,8]{0,1:T(8,128)S(1)} %bitcast_convert_fusion), kind=kOutput, calls=%fused_computation.10 | convolution fusion | flops 4296933376 | bytes 8945664 | tf_op jit(solution)/shard_map/sd,ldk->slk/dot_general | solution.py:13
  107.9 56.5 %all-reduce.2 = (bf16[1024,128]{1,0:T(8,128)(2,1)S(1)}, bf16[1024,128]{0,1:T(8,128)(2,1)}) all-reduce(f32[1024,128]{1,0:T(8,128)S(1)} %multiply_reduce_fusion, f32[1024,128]{0,1:T(8,128)S(1)} %constant_dynamic-update-slice_fusion), channel_id=1, replica_groups=mesh['fsdp'=4,'adapter'=8] {'fsdp'}, use_global_device_ids=true, to_apply=%region_2.3 | all-reduce | flops 262144 | bytes 1572864 | tf_op jit(solution)/shard_map/psum | solution.py:102
  164.4 0.1 dynamic-slice_convert_fusion
  164.5 0.1 copy.17
  164.7 2.8 %fusion.8 = bf16[1024,512]{1,0:T(8,128)(2,1)} fusion(bf16[8,64,512]{2,1,0:T(8,128)(2,1)} %param.12, bf16[1024,8]{0,1:T(8,128)(2,1)S(1)} %bitcast.57, bf16[1024,64]{0,1:T(8,128)(2,1)S(1)} %copy.17), kind=kOutput, calls=%fused_computation.17 | convolution fusion | flops 538443776 | bytes 1720320 | tf_op jit(solution)/shard_map/slr,lrc->sc/dot_general | solution.py:32
  167.4 3.6 %all-to-all-start.2 = ((bf16[8,128,512]{2,1,0:T(8,128)(2,1)}), bf16[8,128,512]{2,1,0:T(8,128)(2,1)S(1)}, u32[]{:S(2)}, u32[]{:S(2)}) async-start(bf16[8,128,512]{2,1,0:T(8,128)(2,1)} %bitcast.55), calls=%async_computation.3 | async-start | bytes 2097152 | tf_op jit(solution)/shard_map/all_to_all | solution.py:106
  171.0 8.4 %fusion.2 = bf16[1024,2048]{1,0:T(8,128)(2,1)} fusion(bf16[8,2048,128]{2,1,0:T(8,128)(2,1)} %param.11, bf16[1024,8]{0,1:T(8,128)(2,1)S(1)} %bitcast.58, bf16[1024,128]{0,1:T(8,128)(2,1)} %get-tuple-element.17), kind=kOutput, calls=%fused_computation.8 | convolution fusion | flops 4300210176 | bytes 8667136 | tf_op jit(solution)/shard_map/wnr,nyr->wy/dot_general | solution.py:40
  179.4 7.0 %all-to-all-done.2 = bf16[8,128,512]{2,1,0:T(8,128)(2,1)S(1)} async-done(((bf16[8,128,512]{2,1,0:T(8,128)(2,1)}), bf16[8,128,512]{2,1,0:T(8,128)(2,1)S(1)}, u32[]{:S(2)}, u32[]{:S(2)}) %all-to-all-start.2) | async-done | bytes 1048608 | tf_op jit(solution)/shard_map/all_to_all | solution.py:106
  186.5 4.9 %all-to-all-start.4 = ((bf16[8,128,2048]{2,1,0:T(8,128)(2,1)}), bf16[8,128,2048]{2,1,0:T(8,128)(2,1)}, u32[]{:S(2)}, u32[]{:S(2)}) async-start(bf16[8,128,2048]{2,1,0:T(8,128)(2,1)} %bitcast.51), calls=%async_computation.5 | async-start | bytes 8388608 | tf_op jit(solution)/shard_map/all_to_all | solution.py:126
  191.3 0.0 copy-done.2
  191.4 0.0 all-gather.2.cloned.1.call-done
  191.4 0.0 copy-start.4
  191.4 7.4 %fusion.32 = f32[256,2048]{1,0:T(8,128)} fusion(bf16[256,2048]{1,0:T(8,128)(2,1)} %all-gather.2.cloned.1.call-done, bf16[2048,2048]{1,0:T(8,128)(2,1)} %param.10), kind=kOutput, calls=%fused_computation.50 | convolution fusion | flops 2147483648 | bytes 11534336 | tf_op jit(solution)/shard_map/dot_general | solution.py:88
  198.8 0.0 copy-done.4
  198.8 8.2 %fusion.3 = bf16[8,2048,128]{1,2,0:T(8,128)(2,1)} fusion(bf16[1024,2048,1]{1,0,2:T(8,128)(2,1)} %bitcast.7, bf16[1024,8]{0,1:T(8,128)(2,1)S(1)} %bitcast.59, bf16[1024,128]{0,1:T(8,128)(2,1)S(1)} %copy-done.4), kind=kOutput, calls=%fused_computation.11 | convolution fusion | flops 4300210176 | bytes 8667136 | tf_op jit(solution)/shard_map/wq,wmu->mqu/dot_general | solution.py:43
  207.1 6.4 %copy.20 = bf16[8,2048,128]{2,1,0:T(8,128)(2,1)} copy(bf16[8,2048,128]{1,2,0:T(8,128)(2,1)} %fusion.3) | data formatting | bytes 8388608
  213.5 1.5 fusion.15
  215.0 1.2 copy.18
  216.2 7.2 %scatter_custom_fusion = f32[256,512]{1,0:T(8,128)S(1)} fusion(f32[256,512]{1,0:T(8,128)S(1)} %copy.18, s32[1024]{0:T(1024)S(1)} %bitcast.63, bf16[1024,512]{1,0:T(8,128)(2,1)S(1)} %bitcast.52), kind=kCustom, calls=%fused_computation.14 | custom fusion | flops 1048576 | bytes 1572864 | tf_op jit(solution)/shard_map/scatter-add | solution.py:136
  223.4 0.7 convert_element_type.55
  224.1 16.1 %all-to-all-done.4 = bf16[8,128,2048]{2,1,0:T(8,128)(2,1)} async-done(((bf16[8,128,2048]{2,1,0:T(8,128)(2,1)}), bf16[8,128,2048]{2,1,0:T(8,128)(2,1)}, u32[]{:S(2)}, u32[]{:S(2)}) %all-to-all-start.4) | async-done | bytes 4194336 | tf_op jit(solution)/shard_map/all_to_all | solution.py:126
  240.3 17.5 %scatter_custom_fusion.1 = f32[256,2048]{1,0:T(8,128)} fusion(f32[256,2048]{1,0:T(8,128)} %fusion.32, s32[1024]{0:T(1024)S(1)} %bitcast.64, bf16[1024,2048]{1,0:T(8,128)(2,1)} %bitcast.24), kind=kCustom, calls=%fused_computation.5 | custom fusion | flops 4194304 | bytes 6291456 | tf_op jit(solution)/shard_map/scatter-add | solution.py:142
  257.8 2.7 %convert_element_type.60 = bf16[256,2048]{1,0:T(8,128)(2,1)} convert(f32[256,2048]{1,0:T(8,128)} %scatter_custom_fusion.1) | non-fusion elementwise | flops 524288 | bytes 3145728 | tf_op jit(solution)/shard_map/convert_element_type | solution.py:144
  (6 shorter events, 0.1 us)
Async XLA Ops:
  7.2 24.1 %copy-start = (bf16[256,2048]{1,0:T(8,128)(2,1)S(1)}, bf16[256,2048]{1,0:T(8,128)(2,1)}, u32[]{:S(2)}) copy-start(bf16[256,2048]{1,0:T(8,128)(2,1)} %param.7) | copy-start | bytes 3145732
  7.2 14.8 %copy-start.1 = (bf16[256,512]{1,0:T(8,128)(2,1)S(1)}, bf16[256,512]{1,0:T(8,128)(2,1)}, u32[]{:S(2)}) copy-start(bf16[256,512]{1,0:T(8,128)(2,1)} %param.13) | copy-start | bytes 786436
  16.8 10.3 %all-to-all-start.1 = ((bf16[8,128,8]{1,2,0:T(8,128)(2,1)}), bf16[8,128,8]{1,2,0:T(8,128)(2,1)S(1)}, u32[]{:S(2)}, u32[]{:S(2)}) async-start(bf16[8,128,8]{1,2,0:T(8,128)(2,1)} %fusion.27), calls=%async_computation.2 | async-start | bytes 32768 | tf_op jit(solution)/shard_map/all_to_all | solution.py:96
  27.1 19.6 %all-to-all-start.3 = ((bf16[8,128,512]{2,1,0:T(8,128)(2,1)}), bf16[8,128,512]{2,1,0:T(8,128)(2,1)S(1)}, u32[]{:S(2)}, u32[]{:S(2)}) async-start(bf16[8,128,512]{2,1,0:T(8,128)(2,1)} %bitcast.14), calls=%async_computation.4 | async-start | bytes 2097152 | tf_op jit(solution)/shard_map/all_to_all | solution.py:113
  46.7 53.7 %all-to-all-start = ((bf16[8,128,2048]{2,1,0:T(8,128)(2,1)}), bf16[8,128,2048]{2,1,0:T(8,128)(2,1)}, u32[]{:S(2)}, u32[]{:S(2)}) async-start(bf16[8,128,2048]{2,1,0:T(8,128)(2,1)} %bitcast.50), calls=%async_computation.1 | async-start | bytes 8388608 | tf_op jit(solution)/shard_map/all_to_all | solution.py:95
  51.3 140.1 %all-gather.2.cloned.1.call-start = ((), (), s32[]{:S(2)}) async-start(), calls=%async_computation.7 | async-start | bytes 1310720 | tf_op jit(solution)/shard_map/all_gather | solution.py:89
  52.0 7.3 %copy-start.3 = (bf16[8,64,512]{2,1,0:T(8,128)(2,1)S(1)}, bf16[8,64,512]{2,1,0:T(8,128)(2,1)}, u32[]{:S(2)}) copy-start(bf16[8,64,512]{2,1,0:T(8,128)(2,1)} %param.12) | copy-start | bytes 1572868
  52.0 163.0 %reduce-scatter.2.cloned.1.call-start = ((), (), s32[]{:S(2)}) async-start(), calls=%async_computation.6 | async-start | bytes 2621440 | tf_op jit(solution)/shard_map/reduce_scatter | solution.py:79
  167.4 19.0 %all-to-all-start.2 = ((bf16[8,128,512]{2,1,0:T(8,128)(2,1)}), bf16[8,128,512]{2,1,0:T(8,128)(2,1)S(1)}, u32[]{:S(2)}, u32[]{:S(2)}) async-start(bf16[8,128,512]{2,1,0:T(8,128)(2,1)} %bitcast.55), calls=%async_computation.3 | async-start | bytes 2097152 | tf_op jit(solution)/shard_map/all_to_all | solution.py:106
  186.5 4.9 %copy-start.2 = (s32[1,8,128]{2,1,0:T(8,128)S(1)}, s32[1,8,128]{2,1,0:T(8,128)}, u32[]{:S(2)}) copy-start(s32[1,8,128]{2,1,0:T(8,128)} %param.9) | copy-start | bytes 12292
  186.5 53.8 %all-to-all-start.4 = ((bf16[8,128,2048]{2,1,0:T(8,128)(2,1)}), bf16[8,128,2048]{2,1,0:T(8,128)(2,1)}, u32[]{:S(2)}, u32[]{:S(2)}) async-start(bf16[8,128,2048]{2,1,0:T(8,128)(2,1)} %bitcast.51), calls=%async_computation.5 | async-start | bytes 8388608 | tf_op jit(solution)/shard_map/all_to_all | solution.py:126
  191.4 7.5 %copy-start.4 = (bf16[1024,128]{0,1:T(8,128)(2,1)S(1)}, bf16[1024,128]{0,1:T(8,128)(2,1)}, u32[]{:S(2)}) copy-start(bf16[1024,128]{0,1:T(8,128)(2,1)} %get-tuple-element.17) | copy-start | bytes 786436
Sparse Core Ops, SparseCore 0:
  53.7 29.5 all-gather.1
  85.5 58.0 reduce-scatter.1
where the time goes:
time: 268 us; the launch traced here: 267 us
  waiting for transfers between devices  73.5 us (27%)
  blocking collectives  56.5 us (21%)
  matrix products  43.9 us (16%)
  other arithmetic  30.9 us (12%)
  local copies, waits for them, and re-layouts  25.9 us (10%)
  starting transfers between devices  22.5 us (8%)
  between operations  14.2 us (5%)
    psum x1, blocking collectives, shards(): reduced_rank_sum = lax.psum(low_term, 'fsdp')  56.5 us
    all_to_all x1, waiting for transfers between devices, shards(): lax.all_to_all(send_x, 'adapter', split_axis=0, concat_axis=0, tiled=True)  40.2 us
    scatter-add x1, other arithmetic, shards(): adapter_backward = jnp.zeros((rows_here, width_here), jnp.float32).at[dro...  17.5 us
    all_to_all x1, waiting for transfers between devices, shards(): lax.all_to_all(backward_update.reshape(holder_list, slot_capacity, width_...  16.1 us
    all_to_all x1, waiting for transfers between devices, shards(): lax.all_to_all(send_dy, 'adapter', split_axis=0, concat_axis=0, tiled=True)  9.44 us
    dot_general x1, matrix products, backward_owner(): jnp.einsum('wnr,nyr->wy', widened_rows, down_weight, preferred_element_ty...  8.41 us
    dot_general x1, matrix products, backward_owner(): jnp.einsum('wq,wmu->mqu', input_rows, widened_rows, preferred_element_typ...  8.22 us
    dot_general x1, matrix products, down_partial(): jnp.einsum('sd,ldk->slk', input_rows, down_weight, preferred_element_type...  7.56 us
  transfers between devices with their start and end apart: 7, of which 4 were waited for; matrix products, arithmetic and copies ran while one was open for 26% of the time, Pallas kernels for 0%

commit v1 on v0

--- a/solution.py
+++ b/solution.py
@@ -1,6 +1,8 @@
 import jax
 import jax.numpy as jnp
 from jax import lax
+from jax.experimental import pallas as pl
+from jax.experimental.pallas import tpu as pltpu
 from jax.sharding import PartitionSpec as P
 
 KV = 1024
@@ -53,7 +55,7 @@
     )
 
 
-def shards(tokens, tenant, send_list, base_weight, down_weight, up_projection_weight, cotangent):
+def shards_any(tokens, tenant, send_list, base_weight, down_weight, up_projection_weight, cotangent):
     rows_here = tokens.shape[0]
     width_here = tokens.shape[1]
     column_span = cotangent.shape[1]
@@ -144,6 +146,415 @@
     token_gradient = (input_frozen_part + adapter_backward).astype(jnp.bfloat16)
     return (projected, token_gradient, down_weight_gradient, up_weight_gradient)
 
+BF16 = jnp.bfloat16
+F32 = jnp.float32
+MIB = 1 << 20
+HINT_FLOPS, HINT_BYTES = 1 << 10, 1 << 10
+
+
+def contract(left, right, left_dim, right_dim):
+    return lax.dot_general(
+        left, right, (((left_dim,), (right_dim,)), ((), ())), preferred_element_type=F32
+    )
+
+
+def swap(value, axis, bits):
+    size = lax.axis_size(axis)
+    return lax.ppermute(value, axis, [(i, i ^ bits) for i in range(size)])
+
+
+def call(body, name, outs, args, *, grid=(), in_specs=None, out_specs=None, scratch=(), scalars=0, vmem=12, needs=(), passed=None):
+    given = len(args)
+    extra = [*needs] + ([passed] if passed is not None else [])
+    in_specs = list(in_specs) if in_specs is not None else [pl.BlockSpec()] * (given - scalars)
+    out_specs = list(out_specs) if out_specs is not None else [pl.BlockSpec()] * len(outs)
+    anywhere = pl.BlockSpec(memory_space=pl.ANY)
+    count = len(outs)
+    aliases = {}
+    if passed is not None:
+        outs = [*outs, shape(passed.shape, passed.dtype)]
+        out_specs.append(anywhere)
+        aliases = {given + len(extra) - 1: count}
+
+    def run(*refs):
+        kept = refs[:given] + refs[given + len(extra) : given + len(extra) + count]
+        body(*kept, *refs[given + len(extra) + len(outs) :])
+
+    spec = pltpu.PrefetchScalarGridSpec(
+        num_scalar_prefetch=scalars,
+        grid=grid,
+        in_specs=in_specs + [anywhere] * len(extra),
+        out_specs=out_specs,
+        scratch_shapes=list(scratch),
+    )
+    return pl.pallas_call(
+        run,
+        grid_spec=spec,
+        out_shape=outs,
+        name=name,
+        input_output_aliases=aliases,
+        cost_estimate=pl.CostEstimate(flops=HINT_FLOPS, bytes_accessed=HINT_BYTES, transcendentals=0),
+        compiler_params=pltpu.CompilerParams(vmem_limit_bytes=vmem * MIB),
+    )(*args, *extra)
+
+
+def tie(values, needs):
+    count, total = len(values), len(values) + len(needs)
+    anywhere = pl.BlockSpec(memory_space=pl.ANY)
+    return pl.pallas_call(
+        lambda *refs: None,
+        in_specs=[anywhere] * total,
+        out_specs=[anywhere] * count,
+        out_shape=[shape(v.shape, v.dtype) for v in values],
+        name="tie",
+        input_output_aliases={i: i for i in range(count)},
+        cost_estimate=pl.CostEstimate(flops=HINT_FLOPS, bytes_accessed=HINT_BYTES, transcendentals=0),
+        compiler_params=pltpu.CompilerParams(vmem_limit_bytes=MIB),
+    )(*values, *needs)
+
+
+def shape(dims, dtype=BF16):
+    return jax.ShapeDtypeStruct(dims, dtype)
+
+
+ORDER = (0, 1, 6, 7, 4, 5, 2, 3)
+
+
+def after(value, *others):
+    return lax.optimization_barrier((value, *others))[0]
+
+
+def back_body(holders, capacity, rank, local, *refs):
+    messages, up_ref = refs[:holders], refs[holders]
+    dy_ref, ids_ref, own_ref, mate_ref, part_ref = refs[holders + 1 :]
+    me = lax.axis_index("adapter")
+    rows = messages[0].shape[0] - 16
+    span = up_ref.shape[2]
+    owner = lax.broadcasted_iota(jnp.int32, (holders, capacity), 0)
+    row_id = lax.broadcasted_iota(jnp.int32, (rows, capacity), 0).astype(F32)
+    upper_lanes = (lax.broadcasted_iota(jnp.int32, (capacity, 2 * rank), 1) >= rank).astype(F32)
+    up = up_ref[...].reshape(local * rank, span)
+    for g in range(holders):
+        tail = messages[g][rows : rows + 16, :capacity].astype(F32)
+        lists, ids = tail[:holders], tail[holders:]
+        listed = jnp.sum(jnp.where(owner == me, lists, 0.0), axis=0, keepdims=True)
+        pick = (row_id == listed).astype(F32).astype(BF16)
+        own_ref[g] = pick
+        if g % 2 == 0:
+            other = jnp.sum(jnp.where(owner == (me ^ 1), lists, 0.0), axis=0, keepdims=True)
+            mate_ref[g // 2] = (row_id == other).astype(F32).astype(BF16)
+        column = ids.T
+        adapter = jnp.concatenate([column[:, j : j + 1] for j in range(rows // capacity)], axis=0)
+        adapter = jnp.broadcast_to(adapter + 1.0, (rows, capacity)).astype(BF16)
+        ids = contract(pick, adapter, 0, 0)
+        ids_ref[g] = ids
+        dy = contract(pick, messages[g][:rows, :], 0, 0).astype(BF16)
+        dy_ref[g] = dy
+        wide = contract(dy, up, 1, 1)
+        total = jnp.zeros((capacity, 2 * rank), F32)
+        for p in range(local // 2):
+            wanted = upper_lanes + (2 * p + 1.0)
+            total += jnp.where(ids == wanted, wide[:, 2 * rank * p : 2 * rank * (p + 1)], 0.0)
+        part_ref[g] = total[:, :rank] + total[:, rank:]
+
+
+def place_body(upper_ref, odd_ref):
+    place = lax.axis_index("fsdp")
+    upper_ref[...] = jnp.full(upper_ref.shape, (place >= lax.axis_size("fsdp") // 2).astype(F32))
+    odd_ref[...] = jnp.full(odd_ref.shape, (place & 1).astype(F32))
+
+
+def low_body(local, count, first, *refs):
+    blocks = refs[: 2 * count]
+    own_ref, ids_ref, down_ref, slots_ref, part_ref = refs[2 * count :]
+    half = blocks[0].shape[0]
+    capacity = own_ref.shape[2]
+    width = down_ref.shape[2]
+    for j in range(count):
+        picked = contract(own_ref[first + j, :half], blocks[2 * j][...], 0, 0)
+        picked += contract(own_ref[first + j, half:], blocks[2 * j + 1][...], 0, 0)
+        slots_ref[j * capacity : (j + 1) * capacity, :] = picked.astype(BF16)
+    ids = ids_ref[first : first + count].reshape(count * capacity, capacity)
+    total = jnp.zeros((count * capacity, width), F32)
+    for a in range(0, local, 2):
+        weights = jnp.concatenate([down_ref[a], down_ref[a + 1]], axis=1)
+        wide = contract(slots_ref[...], weights, 1, 0)
+        total += jnp.where(ids == a + 1.0, wide[:, :width], 0.0)
+        total += jnp.where(ids == a + 2.0, wide[:, width:], 0.0)
+    part_ref[...] = total
+
+
+def spread(low, ids, local):
+    low = low.astype(F32)
+    return jnp.concatenate([jnp.where(ids == a + 1.0, low, 0.0) for a in range(local)], axis=1).astype(BF16)
+
+
+def delta_body(local, low_ref, ids_ref, down_ref, odd_ref, even_ref, wide_ref):
+    slots = low_ref.shape[0]
+    holders, capacity, _ = ids_ref.shape
+
+    @pl.when(pl.program_id(0) == 0)
+    def _():
+        for g in range(holders):
+            at = (g % 2) * (slots // 2) + (g // 2) * capacity
+            wide_ref[pl.ds(at, capacity), :] = spread(
+                low_ref[g * capacity : (g + 1) * capacity, :], ids_ref[g], local
+            )
+
+    weights = jnp.concatenate([down_ref[a] for a in range(local)], axis=1)
+    half = slots // 2
+    for part, out_ref in ((1, odd_ref), (0, even_ref)):
+        out = (adapter_scale * contract(wide_ref[pl.ds(part * half, half), :], weights, 1, 1)).astype(BF16)
+        out_ref[...] = out.reshape(half // capacity, capacity, out.shape[1])
+
+
+def up_body(local, low_ref, ids_ref, up_ref, odd_ref, even_ref, wide_ref):
+    slots, rank = low_ref.shape
+    holders, capacity, _ = ids_ref.shape
+    low = low_ref[...].astype(F32)
+    low = jnp.concatenate([low, low], axis=1)
+    ids = ids_ref[...].reshape(slots, capacity)
+    upper_lanes = (lax.broadcasted_iota(jnp.int32, (slots, 2 * rank), 1) >= rank).astype(F32)
+    wide = jnp.concatenate(
+        [jnp.where(ids == upper_lanes + (2 * p + 1.0), low, 0.0) for p in range(local // 2)], axis=1
+    ).astype(BF16)
+    wide_ref[...] = wide
+    span = up_ref.shape[2]
+    up = up_ref[...].reshape(local * rank, span)
+    out = (adapter_scale * contract(wide, up, 1, 0)).astype(BF16)
+    for g in range(holders):
+        (odd_ref if g % 2 else even_ref)[g // 2] = out[g * capacity : (g + 1) * capacity]
+
+
+def expand_body(picks, own_ref, mate_ref, even_ref, got_ref, *out_refs):
+    for (p, first, count), out_ref in zip(picks, out_refs):
+        pick = jnp.concatenate(
+            [own_ref[2 * p][first : first + count], mate_ref[p][first : first + count]], axis=1
+        )
+        both = jnp.concatenate([even_ref[p], got_ref[p]], axis=0)
+        out_ref[...] = contract(pick, both, 1, 0).astype(BF16)
+
+
+def expand(name, start, pairs, picks, own, mate, even, got, step, needs=()):
+    rows, capacity = own.shape[1:]
+    width = even.shape[2]
+    step = min(width, step)
+    block = start // pairs
+    return call(
+        lambda *refs: expand_body(picks, *refs),
+        name,
+        [shape((count, width)) for _, _, count in picks],
+        [own, mate, even, got],
+        grid=(width // step,),
+        in_specs=[
+            pl.BlockSpec((2 * pairs, rows, capacity), lambda i: (block, 0, 0)),
+            pl.BlockSpec((pairs, rows, capacity), lambda i: (block, 0, 0)),
+            pl.BlockSpec((pairs, capacity, step), lambda i: (block, 0, i)),
+            pl.BlockSpec((pairs, capacity, step), lambda i: (block, 0, i)),
+        ],
+        out_specs=[pl.BlockSpec((count, step), lambda i: (0, i)) for _, _, count in picks],
+        needs=needs,
+    )
+
+
+def down_grad_body(local, pieces, *refs):
+    blocks = refs[:pieces]
+    low_ref, ids_ref, out_ref, wide_ref = refs[pieces:]
+    slots = low_ref.shape[0]
+
+    @pl.when(pl.program_id(0) == 0)
+    def _():
+        wide_ref[...] = spread(low_ref[...], ids_ref[...].reshape(slots, -1), local)
+
+    rows = jnp.concatenate([block[...] for block in blocks], axis=0)
+    out = (adapter_scale * contract(rows, wide_ref[...], 0, 0)).astype(BF16)
+    width = low_ref.shape[1]
+    for a in range(local):
+        out_ref[a] = out[:, a * width : (a + 1) * width]
+
+
+def shards(tokens, tenant, send_list, base_weight, down_weight, up_weight, cotangent):
+    rows, width = tokens.shape
+    span = cotangent.shape[1]
+    local, _, pair = down_weight.shape
+    rank = up_weight.shape[1]
+    holders, capacity = send_list.shape[1], send_list.shape[2]
+    slots = holders * capacity
+    fsdp = lax.axis_size("fsdp")
+    upper, odd_place = call(place_body, "place", [shape((8, 128), F32)] * 2, [], vmem=1)
+
+    def where(mask, yes, no):
+        mask = jnp.broadcast_to(mask[:1, :1], yes.shape)
+        return jnp.where(mask > 0.5, yes, no)
+    half = rows // 2
+    chunk = 512
+
+    extra = jnp.concatenate([send_list[0], (tenant % local).reshape(-1, capacity)], axis=0).astype(BF16)
+    extra = jnp.pad(extra, ((0, 16 - extra.shape[0]), (0, span - capacity)))
+    message = jnp.concatenate([cotangent, extra], axis=0)
+    near = {0: message}
+    for bits in (2, 4, 6):
+        near[bits] = swap(message, "adapter", bits)
+    top, bottom = tokens[:half], tokens[half:]
+    base_partial = jnp.dot(tokens, base_weight, preferred_element_type=F32).astype(BF16)
+    near[2], near[4], near[6], top = tie((near[2], near[4], near[6], top), (base_partial,))
+    messages = []
+    for bits in ORDER[::2]:
+        messages += [near[bits], swap(near[bits], "adapter", 1)]
+    far_dy = swap(cotangent, "fsdp", 2)
+    slots_dy, ids, own, mate, back_part = call(
+        lambda *refs: back_body(holders, capacity, rank, local, *refs),
+        "back_rows",
+        [
+            shape((holders, capacity, span)),
+            shape((holders, capacity, capacity), F32),
+            shape((holders, rows, capacity)),
+            shape((holders // 2, rows, capacity)),
+            shape((holders, capacity, rank), F32),
+        ],
+        [*messages, up_weight],
+    )
+    back_part = back_part.reshape(slots, rank)
+    flat_ids = ids.reshape(slots, capacity)
+
+    def low_rows(first, blocks, needs=()):
+        count = len(blocks)
+        return call(
+            lambda *refs: low_body(local, count, first, *refs),
+            "low_rows",
+            [shape((count * capacity, width)), shape((count * capacity, pair), F32)],
+            [*sum(blocks, ()), own, ids, down_weight],
+            vmem=16,
+            needs=needs,
+        )
+
+    def with_mates(*blocks):
+        out = []
+        for block in blocks:
+            out += [block, tuple(swap(piece, "adapter", 1) for piece in block)]
+        return out
+
+    got1 = swap(back_part.astype(BF16), "fsdp", 1)
+    x_top, y_top = swap(top, "adapter", 2), swap(top, "adapter", 4)
+    x_a, low_a = low_rows(0, with_mates((top, bottom)))
+    back_half = (back_part + got1.astype(F32)).astype(BF16)
+    (back_half,) = tie((back_half,), (x_top, y_top, low_a, far_dy))
+
+    back_other = swap(back_half, "fsdp", 2)
+    x_bottom, y_bottom = swap(bottom, "adapter", 2), swap(bottom, "adapter", 4)
+    next_dy = swap(cotangent, "fsdp", 1), swap(far_dy, "fsdp", 1)
+    back_low = where(
+        upper,
+        jnp.concatenate([back_other, back_half], axis=1),
+        jnp.concatenate([back_half, back_other], axis=1),
+    )
+    odd, even = call(
+        lambda *refs: delta_body(local, *refs),
+        "back_delta",
+        [shape((holders // 2, capacity, width))] * 2,
+        [back_low, ids, down_weight],
+        grid=(width // chunk,),
+        in_specs=[
+            pl.BlockSpec((slots, pair), lambda i: (0, 0)),
+            pl.BlockSpec((holders, capacity, capacity), lambda i: (0, 0, 0)),
+            pl.BlockSpec((local, chunk, pair), lambda i: (0, i, 0)),
+        ],
+        out_specs=[pl.BlockSpec((holders // 2, capacity, chunk), lambda i: (0, 0, i))] * 2,
+        scratch=[pltpu.VMEM((slots, local * pair), BF16)],
+        vmem=16,
+        needs=(x_bottom, y_bottom, *next_dy),
+    )
+
+    got = swap(odd, "adapter", 1)
+    diag = (swap(y_top, "adapter", 2), swap(x_bottom, "adapter", 4))
+    x_b, low_b = low_rows(4, with_mates((y_top, y_bottom), (x_top, x_bottom)))
+    x_c, low_c = low_rows(2, with_mates(diag))
+    low_part = jnp.concatenate([low_a, low_c, low_b], axis=0)
+    keep = where(upper, low_part[:, rank:], low_part[:, :rank])
+    give = where(upper, low_part[:, :rank], low_part[:, rank:]).astype(BF16)
+    diag_low, diag_high = expand(
+        "back_diag", 1, 1, ((0, 0, half), (0, half, half)), own, mate, even, got, 1024, needs=(give,)
+    )
+
+    low_in = swap(diag_low, "adapter", 2)
+    high_in = swap(diag_high, "adapter", 4)
+    got_low = swap(give, "fsdp", 2)
+    y_low, y_high, x_low, x_high = expand(
+        "back_near",
+        2,
+        2,
+        ((0, 0, half), (0, half, half), (1, 0, half), (1, half, half)),
+        own,
+        mate,
+        even,
+        got,
+        1024,
+    )
+    (down_grad,) = call(
+        lambda *refs: down_grad_body(local, 3, *refs),
+        "down_grad",
+        [shape((local, width, pair))],
+        [x_a, x_c, x_b, back_low, flat_ids],
+        grid=(width // 256,),
+        in_specs=[pl.BlockSpec((x.shape[0], 256), lambda i: (0, i)) for x in (x_a, x_c, x_b)]
+        + [pl.BlockSpec((slots, pair), lambda i: (0, 0)), pl.BlockSpec((slots, capacity), lambda i: (0, 0))],
+        out_specs=[pl.BlockSpec((local, 256, pair), lambda i: (0, i, 0))],
+        scratch=[pltpu.VMEM((slots, local * pair), BF16)],
+        vmem=16,
+    )
+    quarter = [base_partial[:, i * span : (i + 1) * span] for i in range(4)]
+    base_keep = [where(odd_place, quarter[1], quarter[0]), where(odd_place, quarter[3], quarter[2])]
+    base_give = [where(odd_place, quarter[0], quarter[1]), where(odd_place, quarter[2], quarter[3])]
+    base_got = swap(jnp.concatenate(base_give, axis=1), "fsdp", 1)
+    to_y, to_x = y_low + low_in, x_high + high_in
+    low_sum = keep + got_low.astype(F32)
+    (low_sent,) = tie((low_sum.astype(BF16),), (to_y, to_x, down_grad, base_got))
+
+    got2 = swap(low_sent, "fsdp", 1)
+    high_from_y = swap(y_high, "adapter", 4)
+    low_from_x = swap(x_low, "adapter", 2)
+    ordered = [
+        where(odd_place, b, a) for a, b in ((cotangent, next_dy[0]), (next_dy[0], cotangent))
+    ], [where(odd_place, b, a) for a, b in ((far_dy, next_dy[1]), (next_dy[1], far_dy))]
+    all_dy = jnp.concatenate(
+        [where(upper, ordered[1 - i][j], ordered[i][j]) for i in range(2) for j in range(2)], axis=1
+    )
+    input_base = contract(all_dy, base_weight, 1, 1)
+    (home,) = expand("back_home", 0, 1, ((0, 0, rows),), own, mate, even, got, 1024)
+    low_half = (low_sum + got2.astype(F32)).astype(BF16)
+    up_odd, up_even, wide_low = call(
+        lambda *refs: up_body(local, *refs),
+        "up_delta",
+        [shape((holders // 2, capacity, span))] * 2 + [shape((slots, local * rank))],
+        [low_half, ids, up_weight],
+        needs=(input_base, home, high_from_y, low_from_x),
+    )
+
+    low_from_y = swap(to_y, "adapter", 4)
+    high_from_x = swap(to_x, "adapter", 2)
+    base_sum = [
+        base_keep[i].astype(F32) + base_got[:, i * span : (i + 1) * span].astype(F32) for i in range(2)
+    ]
+    base_far = swap(where(upper, base_sum[0], base_sum[1]).astype(BF16), "fsdp", 2)
+    base_out = where(upper, base_sum[1], base_sum[0]) + base_far.astype(F32)
+    up_got = swap(up_odd, "adapter", 1)
+    add_home, add_diag, add_y, add_x = expand(
+        "up_rows", 0, 4, tuple((p, 0, rows) for p in range(4)), own, mate, up_even, up_got, 512
+    )
+    add_x = swap(add_x, "adapter", 2)
+    add_y = swap(add_y, "adapter", 4)
+    add_diag = swap(add_diag, "adapter", 6)
+    up_grad = adapter_scale * contract(wide_low, slots_dy.reshape(slots, span), 0, 0)
+    up_grad = up_grad.astype(BF16).reshape(local, rank, span)
+
+    projected = (base_out + (add_home + add_x + add_y + add_diag).astype(F32)).astype(BF16)
+    low_rows_out = home[:half] + low_from_x + low_from_y
+    high_rows_out = home[half:] + high_from_x + high_from_y
+    token_gradient = (
+        input_base + jnp.concatenate([low_rows_out, high_rows_out], axis=0).astype(F32)
+    ).astype(BF16)
+    return (projected, token_gradient, down_grad, up_grad)
+
 
 def solution(mesh):
     in_specs = (
@@ -161,4 +572,5 @@
         P("adapter", "fsdp", None),
         P("adapter", None, "fsdp"),
     )
-    return jax.shard_map(shards, mesh=mesh, in_specs=in_specs, out_specs=out_specs, check_vma=False)
+    program = shards if mesh.shape["adapter"] == 8 and mesh.shape["fsdp"] == 4 else shards_any
+    return jax.shard_map(program, mesh=mesh, in_specs=in_specs, out_specs=out_specs, check_vma=False)

time: 268 us -> 168 us (0.63)
  blocking collectives: 56.5 us -> 0 us
  matrix products: 43.9 us -> 10.9 us
  Pallas kernels: 0 us -> 28.1 us
  other arithmetic: 30.9 us -> 5.23 us
  local copies, waits for them, and re-layouts: 25.9 us -> 1.18 us
  starting transfers between devices: 22.5 us -> 40.5 us
  between operations: 14.2 us -> 2.34 us
  waiting for transfers between devices: 73.5 us -> 79.8 us
    ppermute x0 -> x41, waiting for transfers between devices: none -> 79.8 us  [swap(): return lax.ppermute(value, axis, [(i, i ^ bits) for i in range(size)])]
    all_to_all x5 -> x0, waiting for transfers between devices: 72.8 us -> none  [the longest x1 40.2 us: shards(): lax.all_to_all(send_x, 'adapter', split_axis=0, concat_axis=0, tiled=True)]
    psum x1 -> x0, blocking collectives: 56.5 us -> none  [shards(): reduced_rank_sum = lax.psum(low_term, 'fsdp')]
    ppermute x0 -> x41, starting transfers between devices: none -> 40.5 us  [swap(): return lax.ppermute(value, axis, [(i, i ^ bits) for i in range(size)])]
    dot_general x8 -> x3, matrix products: 43.9 us -> 10.9 us  [the longest x1 6.05 us: shards(): jnp.dot(tokens, base_weight, preferred_element_type=F32).astype(BF16)]
    pallas_call x0 -> x15, Pallas kernels: none -> 28.1 us  [the longest x12 28.1 us: call(): pl.pallas_call(run, grid_spec=spec, out_shape=outs, name=name, input_outp...]
    scatter-add x2 -> x0, other arithmetic: 24.7 us -> none  [the longest x1 17.5 us: shards(): adapter_backward = jnp.zeros((rows_here, width_here), jnp.float32).at[dro...]
    all_to_all x5 -> x0, starting transfers between devices: 22.4 us -> none  [the longest x1 5.17 us: shards(): lax.all_to_all(selector, 'adapter', split_axis=0, concat_axis=0, tiled=True)]
  transfers between devices with their start and end apart: 7 -> 41, of which waited for: 4 -> 18; matrix products, arithmetic and copies ran while one was open for 26% -> 6% of each run, Pallas kernels for 0% -> 12%
where the time goes in v1:
time: 168 us
  waiting for transfers between devices  79.8 us (48%)
  starting transfers between devices  40.5 us (24%)
  Pallas kernels  28.1 us (17%)
  matrix products  10.9 us (6%)
  other arithmetic  5.23 us (3%)
  between operations  2.34 us (1%)
    ppermute x41, waiting for transfers between devices, swap(): return lax.ppermute(value, axis, [(i, i ^ bits) for i in range(size)])  79.8 us
    ppermute x41, starting transfers between devices, swap(): return lax.ppermute(value, axis, [(i, i ^ bits) for i in range(size)])  40.5 us
    pallas_call x12, Pallas kernels, call(): pl.pallas_call(run, grid_spec=spec, out_shape=outs, name=name, input_outp...  28.1 us
    dot_general x1, matrix products, shards(): jnp.dot(tokens, base_weight, preferred_element_type=F32).astype(BF16)  6.05 us
    dot_general x2, matrix products, contract(): lax.dot_general(left, right, (((left_dim,), (right_dim,)), ((), ())), pre...  4.89 us
  transfers between devices with their start and end apart: 41, of which 18 were waited for; matrix products, arithmetic and copies ran while one was open for 6% of the time, Pallas kernels for 12%

profile of v1, /device:TPU:0, one launch (start us, length us, event | category | flops | bytes accessed | tf_op | source)
XLA Modules:
  0.0 168.1 jit_solution(16586111320454808946)
XLA Ops:
  2.0 1.0 pad_maximum_fusion.1.refs_0_
  3.0 4.0 %collective-permute-start.5 = (bf16[272,512]{1,0:T(8,128)(2,1)S(1)}, bf16[272,512]{1,0:T(8,128)(2,1)S(1)}, u32[]{:S(2)}, u32[]{:S(2)}) collective-permute-start(bf16[272,512]{1,0:T(8,128)(2,1)S(1)} %pad_maximum_fusion.1.refs_0_), channel_id=1, source_target_pairs={{0,6},{1,7},{2,4},{3,5},{4,2},{5,3},{6,0},{7,1},{8,14},{9,15},{10,... | collective-permute-start | bytes 835592 | tf_op jit(solution)/shard_map/ppermute | solution.py:163
  7.6 6.0 %convolution_convert_fusion.refs_4_ = bf16[256,2048]{1,0:T(8,128)(2,1)S(1)} fusion(bf16[256,2048]{1,0:T(8,128)(2,1)} %param.7, bf16[2048,2048]{1,0:T(8,128)(2,1)} %param.10), kind=kOutput, calls=%fused_computation | convolution fusion | flops 2148007936 | bytes 10485760 | tf_op jit(solution)/shard_map/dot_general | solution.py:399
  13.8 0.7 collective-permute-done.5.refs_2_
  14.5 5.1 %collective-permute-done.4.refs_1_ = bf16[272,512]{1,0:T(8,128)(2,1)S(1)} collective-permute-done((bf16[272,512]{1,0:T(8,128)(2,1)S(1)}, bf16[272,512]{1,0:T(8,128)(2,1)S(1)}, u32[]{:S(2)}, u32[]{:S(2)}) %collective-permute-start.4) | collective-permute-done | bytes 278560 | tf_op jit(solution)/shard_map/ppermute | solution.py:163
  20.9 1.5 collective-permute-start.20
  22.4 2.7 %collective-permute-start.25 = (bf16[256,512]{1,0:T(8,128)(2,1)S(1)}, bf16[256,512]{1,0:T(8,128)(2,1)S(1)}, u32[]{:S(2)}, u32[]{:S(2)}) collective-permute-start(bf16[256,512]{1,0:T(8,128)(2,1)S(1)} %copy-done.4), channel_id=1, source_target_pairs={{0,16},{8,24},{16,0},{24,8},{1,17},{9,25},{17,1},{25,9},{2,18},{10... | collective-permute-start | bytes 786440 | tf_op jit(solution)/shard_map/ppermute | solution.py:163
  25.1 0.8 collective-permute-start.11
  25.9 2.6 %back_rows.1 = (bf16[8,128,512]{2,1,0:T(8,128)(2,1)S(1)}, f32[8,128,128]{2,1,0:T(8,128)S(1)}, bf16[8,256,128]{2,1,0:T(8,128)(2,1)S(1)}, bf16[4,256,128]{2,1,0:T(8,128)(2,1)S(1)}, f32[8,128,64]{2,1,0:T(8,128)S(1)}) custom-call(bf16[272,512]{1,0:T(8,128)(2,1)S(1)} %pad_maximum_fusion.1.refs_0_, bf16[272,512]{1,0:T(8,128)(2,1)S(1)} %collective-permute-done.2.refs_1_, ...), custom_call_target="tpu_custom_call" | custom-call | flops 1024 | bytes 1024 | tf_op jit(solution)/shard_map/back_rows/pallas_call | solution.py:190
  28.5 9.2 %collective-permute-done.25.refs_4_ = bf16[256,512]{1,0:T(8,128)(2,1)S(1)} collective-permute-done((bf16[256,512]{1,0:T(8,128)(2,1)S(1)}, bf16[256,512]{1,0:T(8,128)(2,1)S(1)}, u32[]{:S(2)}, u32[]{:S(2)}) %collective-permute-start.25) | collective-permute-done | bytes 262176 | tf_op jit(solution)/shard_map/ppermute | solution.py:163
  38.4 0.7 collective-permute-start.17
  39.1 6.5 %collective-permute-done.24 = bf16[1024,64]{1,0:T(8,128)(2,1)S(1)} collective-permute-done((bf16[1024,64]{1,0:T(8,128)(2,1)S(1)}, bf16[1024,64]{1,0:T(8,128)(2,1)S(1)}, u32[]{:S(2)}, u32[]{:S(2)}) %collective-permute-start.24) | collective-permute-done | bytes 131104 | tf_op jit(solution)/shard_map/ppermute | solution.py:163
  45.7 1.4 collective-permute-start.27
  47.8 1.8 %low_rows.3 = (bf16[256,2048]{1,0:T(8,128)(2,1)S(1)}, f32[256,128]{1,0:T(8,128)S(1)}) custom-call(bf16[128,2048]{1,0:T(8,128)(2,1)S(1)} %get-tuple-element.43.refs_0_, bf16[128,2048]{1,0:T(8,128)(2,1)S(1)} %get-tuple-element.74.refs_1_, bf16[128,2048]{1,0:T(8,128)(2,1)S(1)} %collective-permute-done.9.refs_2_, ...), custom_call_target="tpu_custom_call" | custom-call | flops 1024 | bytes 1024 | tf_op jit(solution)/shard_map/low_rows/pallas_call | solution.py:190
  49.7 3.1 %collective-permute-start.26 = (bf16[1024,64]{1,0:T(8,128)(2,1)S(1)}, bf16[1024,64]{1,0:T(8,128)(2,1)S(1)}, u32[]{:S(2)}, u32[]{:S(2)}) collective-permute-start(bf16[1024,64]{1,0:T(8,128)(2,1)S(1)} %tie.4), channel_id=1, source_target_pairs={{0,16},{8,24},{16,0},{24,8},{1,17},{9,25},{17,1},{25,9},{2,18},{10... | collective-permute-start | bytes 393224 | tf_op jit(solution)/shard_map/ppermute | solution.py:163
  54.0 9.0 %collective-permute-done.26 = bf16[1024,64]{1,0:T(8,128)(2,1)S(1)} collective-permute-done((bf16[1024,64]{1,0:T(8,128)(2,1)S(1)}, bf16[1024,64]{1,0:T(8,128)(2,1)S(1)}, u32[]{:S(2)}, u32[]{:S(2)}) %collective-permute-start.26) | collective-permute-done | bytes 131104 | tf_op jit(solution)/shard_map/ppermute | solution.py:163
  63.8 6.1 %back_delta.1 = (bf16[4,128,2048]{2,1,0:T(8,128)(2,1)S(1)}, bf16[4,128,2048]{2,1,0:T(8,128)(2,1)S(1)}) custom-call(bf16[1024,128]{1,0:T(8,128)(2,1)S(1)} %maximum_select_fusion.refs_0_.refs_3_, f32[8,128,128]{2,1,0:T(8,128)S(1)} %get-tuple-element.44.refs_5_.refs_9_.refs_1_, bf16[8,2048,128]{2,1,0:T(8,128)(2,1)S(1)} %copy-done, ...), custom_call_target="tpu_custom_call" | custom-call | flops 1024 | bytes 1024 | tf_op jit(solution)/shard_map/back_delta/pallas_call | solution.py:190
  70.6 1.7 collective-permute-start.14
  72.7 2.1 %collective-permute-done.19.refs_3_ = bf16[128,2048]{1,0:T(8,128)(2,1)S(1)} collective-permute-done((bf16[128,2048]{1,0:T(8,128)(2,1)S(1)}, bf16[128,2048]{1,0:T(8,128)(2,1)S(1)}, u32[]{:S(2)}, u32[]{:S(2)}) %collective-permute-start.19) | collective-permute-done | bytes 524320 | tf_op jit(solution)/shard_map/ppermute | solution.py:163
  75.8 9.1 %collective-permute-done.14.refs_1_ = bf16[128,2048]{1,0:T(8,128)(2,1)S(1)} collective-permute-done((bf16[128,2048]{1,0:T(8,128)(2,1)S(1)}, bf16[128,2048]{1,0:T(8,128)(2,1)S(1)}, u32[]{:S(2)}, u32[]{:S(2)}) %collective-permute-start.14) | collective-permute-done | bytes 524320 | tf_op jit(solution)/shard_map/ppermute | solution.py:163
  84.8 1.4 collective-permute-done.12.refs_0_
  87.5 3.4 %low_rows.5 = (bf16[512,2048]{1,0:T(8,128)(2,1)S(1)}, f32[512,128]{1,0:T(8,128)S(1)}) custom-call(bf16[128,2048]{1,0:T(8,128)(2,1)S(1)} %collective-permute-done.11.refs_0_.refs_2_, bf16[128,2048]{1,0:T(8,128)(2,1)S(1)} %collective-permute-done.17.refs_1_.refs_4_, bf16[128,2048]{1,0:T(8,128)(2,1)S(1)} %collective-permute-done.18.refs_2_, ...), custom_call_target="tpu_custom_call" | custom-call | flops 1024 | bytes 1024 | tf_op jit(solution)/shard_map/low_rows/pallas_call | solution.py:190
  91.0 1.8 %low_rows.4 = (bf16[256,2048]{1,0:T(8,128)(2,1)S(1)}, f32[256,128]{1,0:T(8,128)S(1)}) custom-call(bf16[128,2048]{1,0:T(8,128)(2,1)S(1)} %collective-permute-done.12.refs_0_, bf16[128,2048]{1,0:T(8,128)(2,1)S(1)} %collective-permute-done.14.refs_1_, bf16[128,2048]{1,0:T(8,128)(2,1)S(1)} %collective-permute-done.15.refs_2_, ...), custom_call_target="tpu_custom_call" | custom-call | flops 1024 | bytes 1024 | tf_op jit(solution)/shard_map/low_rows/pallas_call | solution.py:190
  93.0 0.8 back_diag.1
  93.8 0.9 collective-permute-start.30
  94.7 1.2 collective-permute-start.31
  96.0 4.1 %collective-permute-start = (bf16[256,1024]{1,0:T(8,128)(2,1)S(1)}, bf16[256,1024]{1,0:T(8,128)(2,1)S(1)}, u32[]{:S(2)}, u32[]{:S(2)}) collective-permute-start(bf16[256,1024]{1,0:T(8,128)(2,1)S(1)} %pad_maximum_fusion), channel_id=1, source_target_pairs={{0,8},{8,0},{16,24},{24,16},{1,9},{9,1},{17,25},{25,17},{2,10},{10... | collective-permute-start | bytes 1572872 | tf_op jit(solution)/shard_map/ppermute | solution.py:163
  100.1 0.9 collective-permute-start.23
  101.0 7.8 %down_grad.1.refs_3_ = bf16[8,2048,128]{2,1,0:T(8,128)(2,1)} custom-call(bf16[256,2048]{1,0:T(8,128)(2,1)S(1)} %get-tuple-element.55.refs_0_, bf16[256,2048]{1,0:T(8,128)(2,1)S(1)} %get-tuple-element.56.refs_1_, bf16[512,2048]{1,0:T(8,128)(2,1)S(1)} %get-tuple-element.57.refs_2_, bf16[1024,128]{1,0:T(8,128)(2,1)S(1)} %maximum_select_fusion.refs_0_.refs_3_, ...), custom_call_target="tpu_custom_call" | custom-call | flops 1024 | bytes 1024 | tf_op jit(solution)/shard_map/down_grad/pallas_call | solution.py:190
  108.8 8.2 %collective-permute-done.23 = bf16[1024,64]{1,0:T(8,128)(2,1)S(1)} collective-permute-done((bf16[1024,64]{1,0:T(8,128)(2,1)S(1)}, bf16[1024,64]{1,0:T(8,128)(2,1)S(1)}, u32[]{:S(2)}, u32[]{:S(2)}) %collective-permute-start.23) | collective-permute-done | bytes 131104 | tf_op jit(solution)/shard_map/ppermute | solution.py:163
  117.3 1.3 back_near.1
  119.2 1.3 collective-permute-start.34
  120.6 0.8 collective-permute-start.40
  121.6 1.5 collective-permute-start.39
  123.1 1.7 collective-permute-start.32
  124.8 1.0 back_home.1.refs_4_
  125.8 3.7 %collective-permute-done.32 = bf16[1024,64]{1,0:T(8,128)(2,1)S(1)} collective-permute-done((bf16[1024,64]{1,0:T(8,128)(2,1)S(1)}, bf16[1024,64]{1,0:T(8,128)(2,1)S(1)}, u32[]{:S(2)}, u32[]{:S(2)}) %collective-permute-start.32) | collective-permute-done | bytes 131104 | tf_op jit(solution)/shard_map/ppermute | solution.py:163
  129.7 3.7 %collective-permute-done.33.refs_5_ = bf16[128,2048]{1,0:T(8,128)(2,1)S(1)} collective-permute-done((bf16[128,2048]{1,0:T(8,128)(2,1)S(1)}, bf16[128,2048]{1,0:T(8,128)(2,1)S(1)}, u32[]{:S(2)}, u32[]{:S(2)}) %collective-permute-start.33) | collective-permute-done | bytes 524320 | tf_op jit(solution)/shard_map/ppermute | solution.py:163
  134.1 8.8 %collective-permute-done.40 = bf16[128,2048]{1,0:T(8,128)(2,1)S(1)} collective-permute-done((bf16[128,2048]{1,0:T(8,128)(2,1)S(1)}, bf16[128,2048]{1,0:T(8,128)(2,1)S(1)}, u32[]{:S(2)}, u32[]{:S(2)}) %collective-permute-start.40) | collective-permute-done | bytes 524320 | tf_op jit(solution)/shard_map/ppermute | solution.py:163
  143.2 3.3 %add_convert_fusion = (bf16[256,2048]{1,0:T(8,128)(2,1)}, f32[256,2048]{1,0:T(8,128)S(1)}) fusion(bf16[128,2048]{1,0:T(8,128)(2,1)S(1)} %get-tuple-element.69, bf16[128,2048]{1,0:T(8,128)(2,1)S(1)} %get-tuple-element.68, bf16[2048,2048]{1,0:T(8,128)(2,1)S(1)} %bitcast.22, bf16[256,512]{1,0:T(8,128)(2,1)S(1)} %get-tuple-element.73, ...), kind=kOutput, calls=%fused_computation.1 | convolution fusion | flops 2154823680 | bytes 13631488 | tf_op jit(solution)/shard_map/dot_general | solution.py:156
  146.5 1.0 up_delta.1
  147.8 3.4 %collective-permute-start.1 = (bf16[256,512]{1,0:T(8,128)(2,1)S(1)}, bf16[256,512]{1,0:T(8,128)(2,1)S(1)}, u32[]{:S(2)}, u32[]{:S(2)}) collective-permute-start(bf16[256,512]{1,0:T(8,128)(2,1)S(1)} %select_convert_fusion.1), channel_id=1, source_target_pairs={{0,16},{8,24},{16,0},{24,8},{1,17},{9,25},{17,1},{25,9},{2,18},{10... | collective-permute-start | bytes 786440 | tf_op jit(solution)/shard_map/ppermute | solution.py:163
  151.7 1.5 collective-permute-start.36
  153.6 1.7 collective-permute-start.38
  155.3 1.5 fusion
  156.8 7.0 %collective-permute-done.1 = bf16[256,512]{1,0:T(8,128)(2,1)S(1)} collective-permute-done((bf16[256,512]{1,0:T(8,128)(2,1)S(1)}, bf16[256,512]{1,0:T(8,128)(2,1)S(1)}, u32[]{:S(2)}, u32[]{:S(2)}) %collective-permute-start.1) | collective-permute-done | bytes 262176 | tf_op jit(solution)/shard_map/ppermute | solution.py:163
  163.8 3.2 %collective-permute-done.37 = bf16[256,512]{1,0:T(8,128)(2,1)S(1)} collective-permute-done((bf16[256,512]{1,0:T(8,128)(2,1)S(1)}, bf16[256,512]{1,0:T(8,128)(2,1)S(1)}, u32[]{:S(2)}, u32[]{:S(2)}) %collective-permute-start.37) | collective-permute-done | bytes 262176 | tf_op jit(solution)/shard_map/ppermute | solution.py:163
  167.0 1.1 add_convert_fusion.1
  (91 shorter events, 12.6 us)
Async XLA Ops:
  3.0 10.7 %copy-start.3 = (bf16[256,2048]{1,0:T(8,128)(2,1)S(1)}, bf16[256,2048]{1,0:T(8,128)(2,1)}, u32[]{:S(2)}) copy-start(bf16[256,2048]{1,0:T(8,128)(2,1)} %param.7) | copy-start | bytes 3145732
  3.0 11.5 %collective-permute-start.5 = (bf16[272,512]{1,0:T(8,128)(2,1)S(1)}, bf16[272,512]{1,0:T(8,128)(2,1)S(1)}, u32[]{:S(2)}, u32[]{:S(2)}) collective-permute-start(bf16[272,512]{1,0:T(8,128)(2,1)S(1)} %pad_maximum_fusion.1.refs_0_), channel_id=1, source_target_pairs={{0,6},{1,7},{2,4},{3,5},{4,2},{5,3},{6,0},{7,1},{8,14},{9,15},{10,... | collective-permute-start | bytes 835592 | tf_op jit(solution)/shard_map/ppermute | solution.py:163
  7.0 12.6 %collective-permute-start.4 = (bf16[272,512]{1,0:T(8,128)(2,1)S(1)}, bf16[272,512]{1,0:T(8,128)(2,1)S(1)}, u32[]{:S(2)}, u32[]{:S(2)}) collective-permute-start(bf16[272,512]{1,0:T(8,128)(2,1)S(1)} %pad_maximum_fusion.1.refs_0_), channel_id=1, source_target_pairs={{0,4},{1,5},{2,6},{3,7},{4,0},{5,1},{6,2},{7,3},{8,12},{9,13},{10,... | collective-permute-start | bytes 835592 | tf_op jit(solution)/shard_map/ppermute | solution.py:163
  7.5 12.4 %collective-permute-start.3 = (bf16[272,512]{1,0:T(8,128)(2,1)S(1)}, bf16[272,512]{1,0:T(8,128)(2,1)S(1)}, u32[]{:S(2)}, u32[]{:S(2)}) collective-permute-start(bf16[272,512]{1,0:T(8,128)(2,1)S(1)} %pad_maximum_fusion.1.refs_0_), channel_id=1, source_target_pairs={{0,2},{1,3},{2,0},{3,1},{4,6},{5,7},{6,4},{7,5},{8,10},{9,11},{10,... | collective-permute-start | bytes 835592 | tf_op jit(solution)/shard_map/ppermute | solution.py:163
  7.6 13.3 %collective-permute-start.2 = (bf16[272,512]{1,0:T(8,128)(2,1)S(1)}, bf16[272,512]{1,0:T(8,128)(2,1)S(1)}, u32[]{:S(2)}, u32[]{:S(2)}) collective-permute-start(bf16[272,512]{1,0:T(8,128)(2,1)S(1)} %pad_maximum_fusion.1.refs_0_), channel_id=1, source_target_pairs={{0,1},{1,0},{2,3},{3,2},{4,5},{5,4},{6,7},{7,6},{8,9},{9,8},{10,11... | collective-permute-start | bytes 835592 | tf_op jit(solution)/shard_map/ppermute | solution.py:163
  13.7 8.7 %copy-start.4 = (bf16[256,512]{1,0:T(8,128)(2,1)S(1)}, bf16[256,512]{1,0:T(8,128)(2,1)}, u32[]{:S(2)}) copy-start(bf16[256,512]{1,0:T(8,128)(2,1)} %param.13) | copy-start | bytes 786436
  13.7 12.2 %copy-start.2 = (bf16[8,64,512]{2,1,0:T(8,128)(2,1)S(1)}, bf16[8,64,512]{2,1,0:T(8,128)(2,1)}, u32[]{:S(2)}) copy-start(bf16[8,64,512]{2,1,0:T(8,128)(2,1)} %refs_2_.3) | copy-start | bytes 1572868
  19.9 2.5 %collective-permute-start.6 = (bf16[272,512]{1,0:T(8,128)(2,1)S(1)}, bf16[272,512]{1,0:T(8,128)(2,1)S(1)}, u32[]{:S(2)}, u32[]{:S(2)}) collective-permute-start(bf16[272,512]{1,0:T(8,128)(2,1)S(1)} %get-tuple-element.38.refs_2_), channel_id=1, source_target_pairs={{0,1},{1,0},{2,3},{3,2},{4,5},{5,4},{6,7},{7,6},{8,9},{9,8},{10,11... | collective-permute-start | bytes 835592 | tf_op jit(solution)/shard_map/ppermute | solution.py:163
  19.9 2.5 %collective-permute-start.7 = (bf16[272,512]{1,0:T(8,128)(2,1)S(1)}, bf16[272,512]{1,0:T(8,128)(2,1)S(1)}, u32[]{:S(2)}, u32[]{:S(2)}) collective-permute-start(bf16[272,512]{1,0:T(8,128)(2,1)S(1)} %get-tuple-element.39.refs_4_), channel_id=1, source_target_pairs={{0,1},{1,0},{2,3},{3,2},{4,5},{5,4},{6,7},{7,6},{8,9},{9,8},{10,11... | collective-permute-start | bytes 835592 | tf_op jit(solution)/shard_map/ppermute | solution.py:163
  20.4 4.7 %collective-permute-start.8 = (bf16[272,512]{1,0:T(8,128)(2,1)S(1)}, bf16[272,512]{1,0:T(8,128)(2,1)S(1)}, u32[]{:S(2)}, u32[]{:S(2)}) collective-permute-start(bf16[272,512]{1,0:T(8,128)(2,1)S(1)} %get-tuple-element.40.refs_6_), channel_id=1, source_target_pairs={{0,1},{1,0},{2,3},{3,2},{4,5},{5,4},{6,7},{7,6},{8,9},{9,8},{10,11... | collective-permute-start | bytes 835592 | tf_op jit(solution)/shard_map/ppermute | solution.py:163
  20.4 18.0 %collective-permute-start.10 = (bf16[128,2048]{1,0:T(8,128)(2,1)S(1)}, bf16[128,2048]{1,0:T(8,128)(2,1)S(1)}, u32[]{:S(2)}, u32[]{:S(2)}) collective-permute-start(bf16[128,2048]{1,0:T(8,128)(2,1)S(1)} %get-tuple-element.74.refs_1_), channel_id=1, source_target_pairs={{0,1},{1,0},{2,3},{3,2},{4,5},{5,4},{6,7},{7,6},{8,9},{9,8},{10,11... | collective-permute-start | bytes 1572872 | tf_op jit(solution)/shard_map/ppermute | solution.py:163
  20.9 26.9 %copy-start = (bf16[8,2048,128]{2,1,0:T(8,128)(2,1)S(1)}, bf16[8,2048,128]{2,1,0:T(8,128)(2,1)}, u32[]{:S(2)}) copy-start(bf16[8,2048,128]{2,1,0:T(8,128)(2,1)} %refs_2_.2) | copy-start | bytes 12582916
  20.9 24.8 %collective-permute-start.20 = (bf16[128,2048]{1,0:T(8,128)(2,1)S(1)}, bf16[128,2048]{1,0:T(8,128)(2,1)S(1)}, u32[]{:S(2)}, u32[]{:S(2)}) collective-permute-start(bf16[128,2048]{1,0:T(8,128)(2,1)S(1)} %get-tuple-element.43.refs_0_), channel_id=1, source_target_pairs={{0,2},{1,3},{2,0},{3,1},{4,6},{5,7},{6,4},{7,5},{8,10},{9,11},{10,... | collective-permute-start | bytes 1572872 | tf_op jit(solution)/shard_map/ppermute | solution.py:163
  22.4 24.7 %collective-permute-start.9 = (bf16[128,2048]{1,0:T(8,128)(2,1)S(1)}, bf16[128,2048]{1,0:T(8,128)(2,1)S(1)}, u32[]{:S(2)}, u32[]{:S(2)}) collective-permute-start(bf16[128,2048]{1,0:T(8,128)(2,1)S(1)} %get-tuple-element.43.refs_0_), channel_id=1, source_target_pairs={{0,1},{1,0},{2,3},{3,2},{4,5},{5,4},{6,7},{7,6},{8,9},{9,8},{10,11... | collective-permute-start | bytes 1572872 | tf_op jit(solution)/shard_map/ppermute | solution.py:163
  22.4 15.2 %collective-permute-start.25 = (bf16[256,512]{1,0:T(8,128)(2,1)S(1)}, bf16[256,512]{1,0:T(8,128)(2,1)S(1)}, u32[]{:S(2)}, u32[]{:S(2)}) collective-permute-start(bf16[256,512]{1,0:T(8,128)(2,1)S(1)} %copy-done.4), channel_id=1, source_target_pairs={{0,16},{8,24},{16,0},{24,8},{1,17},{9,25},{17,1},{25,9},{2,18},{10... | collective-permute-start | bytes 786440 | tf_op jit(solution)/shard_map/ppermute | solution.py:163
  25.1 24.6 %collective-permute-start.11 = (bf16[128,2048]{1,0:T(8,128)(2,1)S(1)}, bf16[128,2048]{1,0:T(8,128)(2,1)S(1)}, u32[]{:S(2)}, u32[]{:S(2)}) collective-permute-start(bf16[128,2048]{1,0:T(8,128)(2,1)S(1)} %get-tuple-element.43.refs_0_), channel_id=1, source_target_pairs={{0,4},{1,5},{2,6},{3,7},{4,0},{5,1},{6,2},{7,3},{8,12},{9,13},{10,... | collective-permute-start | bytes 1572872 | tf_op jit(solution)/shard_map/ppermute | solution.py:163
  37.7 7.9 %collective-permute-start.24 = (bf16[1024,64]{1,0:T(8,128)(2,1)S(1)}, bf16[1024,64]{1,0:T(8,128)(2,1)S(1)}, u32[]{:S(2)}, u32[]{:S(2)}) collective-permute-start(bf16[1024,64]{1,0:T(8,128)(2,1)S(1)} %bitcast_convert_fusion), channel_id=1, source_target_pairs={{0,8},{8,0},{16,24},{24,16},{1,9},{9,1},{17,25},{25,17},{2,10},{10... | collective-permute-start | bytes 393224 | tf_op jit(solution)/shard_map/ppermute | solution.py:163
  38.4 25.4 %collective-permute-start.17 = (bf16[128,2048]{1,0:T(8,128)(2,1)S(1)}, bf16[128,2048]{1,0:T(8,128)(2,1)S(1)}, u32[]{:S(2)}, u32[]{:S(2)}) collective-permute-start(bf16[128,2048]{1,0:T(8,128)(2,1)S(1)} %get-tuple-element.74.refs_1_), channel_id=1, source_target_pairs={{0,4},{1,5},{2,6},{3,7},{4,0},{5,1},{6,2},{7,3},{8,12},{9,13},{10,... | collective-permute-start | bytes 1572872 | tf_op jit(solution)/shard_map/ppermute | solution.py:163
  45.5 18.2 %collective-permute-start.13 = (bf16[128,2048]{1,0:T(8,128)(2,1)S(1)}, bf16[128,2048]{1,0:T(8,128)(2,1)S(1)}, u32[]{:S(2)}, u32[]{:S(2)}) collective-permute-start(bf16[128,2048]{1,0:T(8,128)(2,1)S(1)} %get-tuple-element.74.refs_1_), channel_id=1, source_target_pairs={{0,2},{1,3},{2,0},{3,1},{4,6},{5,7},{6,4},{7,5},{8,10},{9,11},{10,... | collective-permute-start | bytes 1572872 | tf_op jit(solution)/shard_map/ppermute | solution.py:163
  45.7 17.6 %collective-permute-start.27 = (bf16[256,512]{1,0:T(8,128)(2,1)S(1)}, bf16[256,512]{1,0:T(8,128)(2,1)S(1)}, u32[]{:S(2)}, u32[]{:S(2)}) collective-permute-start(bf16[256,512]{1,0:T(8,128)(2,1)S(1)} %copy-done.4), channel_id=1, source_target_pairs={{0,8},{8,0},{16,24},{24,16},{1,9},{9,1},{17,25},{25,17},{2,10},{10... | collective-permute-start | bytes 786440 | tf_op jit(solution)/shard_map/ppermute | solution.py:163
  47.1 16.6 %collective-permute-start.28 = (bf16[256,512]{1,0:T(8,128)(2,1)S(1)}, bf16[256,512]{1,0:T(8,128)(2,1)S(1)}, u32[]{:S(2)}, u32[]{:S(2)}) collective-permute-start(bf16[256,512]{1,0:T(8,128)(2,1)S(1)} %collective-permute-done.25.refs_4_), channel_id=1, source_target_pairs={{0,8},{8,0},{16,24},{24,16},{1,9},{9,1},{17,25},{25,17},{2,10},{10... | collective-permute-start | bytes 786440 | tf_op jit(solution)/shard_map/ppermute | solution.py:163
  49.7 13.3 %collective-permute-start.26 = (bf16[1024,64]{1,0:T(8,128)(2,1)S(1)}, bf16[1024,64]{1,0:T(8,128)(2,1)S(1)}, u32[]{:S(2)}, u32[]{:S(2)}) collective-permute-start(bf16[1024,64]{1,0:T(8,128)(2,1)S(1)} %tie.4), channel_id=1, source_target_pairs={{0,16},{8,24},{16,0},{24,8},{1,17},{9,25},{17,1},{25,9},{2,18},{10... | collective-permute-start | bytes 393224 | tf_op jit(solution)/shard_map/ppermute | solution.py:163
  69.9 23.1 %collective-permute-start.29 = (bf16[4,128,2048]{2,1,0:T(8,128)(2,1)S(1)}, bf16[4,128,2048]{2,1,0:T(8,128)(2,1)S(1)}, u32[]{:S(2)}, u32[]{:S(2)}) collective-permute-start(bf16[4,128,2048]{2,1,0:T(8,128)(2,1)S(1)} %get-tuple-element.50), channel_id=1, source_target_pairs={{0,1},{1,0},{2,3},{3,2},{4,5},{5,4},{6,7},{7,6},{8,9},{9,8},{10,11... | collective-permute-start | bytes 6291464 | tf_op jit(solution)/shard_map/ppermute | solution.py:163
  70.0 4.9 %collective-permute-start.19 = (bf16[128,2048]{1,0:T(8,128)(2,1)S(1)}, bf16[128,2048]{1,0:T(8,128)(2,1)S(1)}, u32[]{:S(2)}, u32[]{:S(2)}) collective-permute-start(bf16[128,2048]{1,0:T(8,128)(2,1)S(1)} %collective-permute-done.17.refs_1_.refs_4_), channel_id=1, source_target_pairs={{0,1},{1,0},{2,3},{3,2},{4,5},{5,4},{6,7},{7,6},{8,9},{9,8},{10,11... | collective-permute-start | bytes 1572872 | tf_op jit(solution)/shard_map/ppermute | solution.py:163
  70.5 5.1 %collective-permute-start.22 = (bf16[128,2048]{1,0:T(8,128)(2,1)S(1)}, bf16[128,2048]{1,0:T(8,128)(2,1)S(1)}, u32[]{:S(2)}, u32[]{:S(2)}) collective-permute-start(bf16[128,2048]{1,0:T(8,128)(2,1)S(1)} %collective-permute-done.13.refs_5_.refs_3_), channel_id=1, source_target_pairs={{0,1},{1,0},{2,3},{3,2},{4,5},{5,4},{6,7},{7,6},{8,9},{9,8},{10,11... | collective-permute-start | bytes 1572872 | tf_op jit(solution)/shard_map/ppermute | solution.py:163
  70.6 14.3 %collective-permute-start.14 = (bf16[128,2048]{1,0:T(8,128)(2,1)S(1)}, bf16[128,2048]{1,0:T(8,128)(2,1)S(1)}, u32[]{:S(2)}, u32[]{:S(2)}) collective-permute-start(bf16[128,2048]{1,0:T(8,128)(2,1)S(1)} %collective-permute-done.13.refs_5_.refs_3_), channel_id=1, source_target_pairs={{0,4},{1,5},{2,6},{3,7},{4,0},{5,1},{6,2},{7,3},{8,12},{9,13},{10,... | collective-permute-start | bytes 1572872 | tf_op jit(solution)/shard_map/ppermute | solution.py:163
  72.2 14.0 %collective-permute-start.12 = (bf16[128,2048]{1,0:T(8,128)(2,1)S(1)}, bf16[128,2048]{1,0:T(8,128)(2,1)S(1)}, u32[]{:S(2)}, u32[]{:S(2)}) collective-permute-start(bf16[128,2048]{1,0:T(8,128)(2,1)S(1)} %collective-permute-done.11.refs_0_.refs_2_), channel_id=1, source_target_pairs={{0,2},{1,3},{2,0},{3,1},{4,6},{5,7},{6,4},{7,5},{8,10},{9,11},{10,... | collective-permute-start | bytes 1572872 | tf_op jit(solution)/shard_map/ppermute | solution.py:163
  74.9 12.6 %collective-permute-start.21 = (bf16[128,2048]{1,0:T(8,128)(2,1)S(1)}, bf16[128,2048]{1,0:T(8,128)(2,1)S(1)}, u32[]{:S(2)}, u32[]{:S(2)}) collective-permute-start(bf16[128,2048]{1,0:T(8,128)(2,1)S(1)} %collective-permute-done.20.refs_4_.refs_1_), channel_id=1, source_target_pairs={{0,1},{1,0},{2,3},{3,2},{4,5},{5,4},{6,7},{7,6},{8,9},{9,8},{10,11... | collective-permute-start | bytes 1572872 | tf_op jit(solution)/shard_map/ppermute | solution.py:163
  75.6 11.9 %collective-permute-start.18 = (bf16[128,2048]{1,0:T(8,128)(2,1)S(1)}, bf16[128,2048]{1,0:T(8,128)(2,1)S(1)}, u32[]{:S(2)}, u32[]{:S(2)}) collective-permute-start(bf16[128,2048]{1,0:T(8,128)(2,1)S(1)} %collective-permute-done.11.refs_0_.refs_2_), channel_id=1, source_target_pairs={{0,1},{1,0},{2,3},{3,2},{4,5},{5,4},{6,7},{7,6},{8,9},{9,8},{10,11... | collective-permute-start | bytes 1572872 | tf_op jit(solution)/shard_map/ppermute | solution.py:163
  84.8 6.1 %collective-permute-start.16 = (bf16[128,2048]{1,0:T(8,128)(2,1)S(1)}, bf16[128,2048]{1,0:T(8,128)(2,1)S(1)}, u32[]{:S(2)}, u32[]{:S(2)}) collective-permute-start(bf16[128,2048]{1,0:T(8,128)(2,1)S(1)} %collective-permute-done.14.refs_1_), channel_id=1, source_target_pairs={{0,1},{1,0},{2,3},{3,2},{4,5},{5,4},{6,7},{7,6},{8,9},{9,8},{10,11... | collective-permute-start | bytes 1572872 | tf_op jit(solution)/shard_map/ppermute | solution.py:163
  86.2 4.7 %collective-permute-start.15 = (bf16[128,2048]{1,0:T(8,128)(2,1)S(1)}, bf16[128,2048]{1,0:T(8,128)(2,1)S(1)}, u32[]{:S(2)}, u32[]{:S(2)}) collective-permute-start(bf16[128,2048]{1,0:T(8,128)(2,1)S(1)} %collective-permute-done.12.refs_0_), channel_id=1, source_target_pairs={{0,1},{1,0},{2,3},{3,2},{4,5},{5,4},{6,7},{7,6},{8,9},{9,8},{10,11... | collective-permute-start | bytes 1572872 | tf_op jit(solution)/shard_map/ppermute | solution.py:163
  93.8 27.6 %collective-permute-start.30 = (bf16[128,2048]{1,0:T(8,128)(2,1)S(1)}, bf16[128,2048]{1,0:T(8,128)(2,1)S(1)}, u32[]{:S(2)}, u32[]{:S(2)}) collective-permute-start(bf16[128,2048]{1,0:T(8,128)(2,1)S(1)} %get-tuple-element.52), channel_id=1, source_target_pairs={{0,2},{1,3},{2,0},{3,1},{4,6},{5,7},{6,4},{7,5},{8,10},{9,11},{10,... | collective-permute-start | bytes 1572872 | tf_op jit(solution)/shard_map/ppermute | solution.py:163
  94.7 25.8 %collective-permute-start.31 = (bf16[128,2048]{1,0:T(8,128)(2,1)S(1)}, bf16[128,2048]{1,0:T(8,128)(2,1)S(1)}, u32[]{:S(2)}, u32[]{:S(2)}) collective-permute-start(bf16[128,2048]{1,0:T(8,128)(2,1)S(1)} %get-tuple-element.54), channel_id=1, source_target_pairs={{0,4},{1,5},{2,6},{3,7},{4,0},{5,1},{6,2},{7,3},{8,12},{9,13},{10,... | collective-permute-start | bytes 1572872 | tf_op jit(solution)/shard_map/ppermute | solution.py:163
  96.0 27.0 %collective-permute-start = (bf16[256,1024]{1,0:T(8,128)(2,1)S(1)}, bf16[256,1024]{1,0:T(8,128)(2,1)S(1)}, u32[]{:S(2)}, u32[]{:S(2)}) collective-permute-start(bf16[256,1024]{1,0:T(8,128)(2,1)S(1)} %pad_maximum_fusion), channel_id=1, source_target_pairs={{0,8},{8,0},{16,24},{24,16},{1,9},{9,1},{17,25},{25,17},{2,10},{10... | collective-permute-start | bytes 1572872 | tf_op jit(solution)/shard_map/ppermute | solution.py:163
  100.1 16.9 %collective-permute-start.23 = (bf16[1024,64]{1,0:T(8,128)(2,1)S(1)}, bf16[1024,64]{1,0:T(8,128)(2,1)S(1)}, u32[]{:S(2)}, u32[]{:S(2)}) collective-permute-start(bf16[1024,64]{1,0:T(8,128)(2,1)S(1)} %select_convert_fusion.refs_4_), channel_id=1, source_target_pairs={{0,16},{8,24},{16,0},{24,8},{1,17},{9,25},{17,1},{25,9},{2,18},{10... | collective-permute-start | bytes 393224 | tf_op jit(solution)/shard_map/ppermute | solution.py:163
  117.2 5.8 %copy-start.1 = (bf16[8,2048,128]{2,1,0:T(8,128)(2,1)S(1)}, bf16[8,2048,128]{2,1,0:T(8,128)(2,1)}, u32[]{:S(2)}) copy-start(bf16[8,2048,128]{2,1,0:T(8,128)(2,1)} %down_grad.1.refs_3_) | copy-start | bytes 12582916
  118.5 14.9 %collective-permute-start.33 = (bf16[128,2048]{1,0:T(8,128)(2,1)S(1)}, bf16[128,2048]{1,0:T(8,128)(2,1)S(1)}, u32[]{:S(2)}, u32[]{:S(2)}) collective-permute-start(bf16[128,2048]{1,0:T(8,128)(2,1)S(1)} %get-tuple-element.58), channel_id=1, source_target_pairs={{0,4},{1,5},{2,6},{3,7},{4,0},{5,1},{6,2},{7,3},{8,12},{9,13},{10,... | collective-permute-start | bytes 1572872 | tf_op jit(solution)/shard_map/ppermute | solution.py:163
  119.2 14.9 %collective-permute-start.34 = (bf16[128,2048]{1,0:T(8,128)(2,1)S(1)}, bf16[128,2048]{1,0:T(8,128)(2,1)S(1)}, u32[]{:S(2)}, u32[]{:S(2)}) collective-permute-start(bf16[128,2048]{1,0:T(8,128)(2,1)S(1)} %get-tuple-element.59), channel_id=1, source_target_pairs={{0,2},{1,3},{2,0},{3,1},{4,6},{5,7},{6,4},{7,5},{8,10},{9,11},{10,... | collective-permute-start | bytes 1572872 | tf_op jit(solution)/shard_map/ppermute | solution.py:163
  120.6 22.3 %collective-permute-start.40 = (bf16[128,2048]{1,0:T(8,128)(2,1)S(1)}, bf16[128,2048]{1,0:T(8,128)(2,1)S(1)}, u32[]{:S(2)}, u32[]{:S(2)}) collective-permute-start(bf16[128,2048]{1,0:T(8,128)(2,1)S(1)} %add.66.refs_2_), channel_id=1, source_target_pairs={{0,2},{1,3},{2,0},{3,1},{4,6},{5,7},{6,4},{7,5},{8,10},{9,11},{10,... | collective-permute-start | bytes 1572872 | tf_op jit(solution)/shard_map/ppermute | solution.py:163
  121.6 21.4 %collective-permute-start.39 = (bf16[128,2048]{1,0:T(8,128)(2,1)S(1)}, bf16[128,2048]{1,0:T(8,128)(2,1)S(1)}, u32[]{:S(2)}, u32[]{:S(2)}) collective-permute-start(bf16[128,2048]{1,0:T(8,128)(2,1)S(1)} %add.65.refs_1_), channel_id=1, source_target_pairs={{0,4},{1,5},{2,6},{3,7},{4,0},{5,1},{6,2},{7,3},{8,12},{9,13},{10,... | collective-permute-start | bytes 1572872 | tf_op jit(solution)/shard_map/ppermute | solution.py:163
  123.0 20.1 %slice-start = ((s8[8388608]{0:T(1024)(128)(4,1)}), s8[4194304]{0:T(1024)(128)(4,1)S(1)}, s32[]{:S(2)}) async-start(s8[8388608]{0:T(1024)(128)(4,1)} %bitcast.21), calls=%async_computation | async-start | bytes 8388608
  123.1 6.4 %collective-permute-start.32 = (bf16[1024,64]{1,0:T(8,128)(2,1)S(1)}, bf16[1024,64]{1,0:T(8,128)(2,1)S(1)}, u32[]{:S(2)}, u32[]{:S(2)}) collective-permute-start(bf16[1024,64]{1,0:T(8,128)(2,1)S(1)} %tie.5), channel_id=1, source_target_pairs={{0,8},{8,0},{16,24},{24,16},{1,9},{9,1},{17,25},{25,17},{2,10},{10... | collective-permute-start | bytes 393224 | tf_op jit(solution)/shard_map/ppermute | solution.py:163
  124.8 18.4 %slice-start.1 = ((s8[8388608]{0:T(1024)(128)(4,1)}), s8[4194304]{0:T(1024)(128)(4,1)S(1)}, s32[]{:S(2)}) async-start(s8[8388608]{0:T(1024)(128)(4,1)} %bitcast.21), calls=%async_computation.1 | async-start | bytes 8388608
  147.5 3.7 %collective-permute-start.35 = (bf16[4,128,512]{2,1,0:T(8,128)(2,1)S(1)}, bf16[4,128,512]{2,1,0:T(8,128)(2,1)S(1)}, u32[]{:S(2)}, u32[]{:S(2)}) collective-permute-start(bf16[4,128,512]{2,1,0:T(8,128)(2,1)S(1)} %get-tuple-element.61), channel_id=1, source_target_pairs={{0,1},{1,0},{2,3},{3,2},{4,5},{5,4},{6,7},{7,6},{8,9},{9,8},{10,11... | collective-permute-start | bytes 1572872 | tf_op jit(solution)/shard_map/ppermute | solution.py:163
  147.8 16.0 %collective-permute-start.1 = (bf16[256,512]{1,0:T(8,128)(2,1)S(1)}, bf16[256,512]{1,0:T(8,128)(2,1)S(1)}, u32[]{:S(2)}, u32[]{:S(2)}) collective-permute-start(bf16[256,512]{1,0:T(8,128)(2,1)S(1)} %select_convert_fusion.1), channel_id=1, source_target_pairs={{0,16},{8,24},{16,0},{24,8},{1,17},{9,25},{17,1},{25,9},{2,18},{10... | collective-permute-start | bytes 786440 | tf_op jit(solution)/shard_map/ppermute | solution.py:163
  151.7 12.1 %collective-permute-start.36 = (bf16[256,512]{1,0:T(8,128)(2,1)S(1)}, bf16[256,512]{1,0:T(8,128)(2,1)S(1)}, u32[]{:S(2)}, u32[]{:S(2)}) collective-permute-start(bf16[256,512]{1,0:T(8,128)(2,1)S(1)} %get-tuple-element.63), channel_id=1, source_target_pairs={{0,2},{1,3},{2,0},{3,1},{4,6},{5,7},{6,4},{7,5},{8,10},{9,11},{10,... | collective-permute-start | bytes 786440 | tf_op jit(solution)/shard_map/ppermute | solution.py:163
  153.2 13.8 %collective-permute-start.37 = (bf16[256,512]{1,0:T(8,128)(2,1)S(1)}, bf16[256,512]{1,0:T(8,128)(2,1)S(1)}, u32[]{:S(2)}, u32[]{:S(2)}) collective-permute-start(bf16[256,512]{1,0:T(8,128)(2,1)S(1)} %get-tuple-element.64), channel_id=1, source_target_pairs={{0,4},{1,5},{2,6},{3,7},{4,0},{5,1},{6,2},{7,3},{8,12},{9,13},{10,... | collective-permute-start | bytes 786440 | tf_op jit(solution)/shard_map/ppermute | solution.py:163
  153.6 13.4 %collective-permute-start.38 = (bf16[256,512]{1,0:T(8,128)(2,1)S(1)}, bf16[256,512]{1,0:T(8,128)(2,1)S(1)}, u32[]{:S(2)}, u32[]{:S(2)}) collective-permute-start(bf16[256,512]{1,0:T(8,128)(2,1)S(1)} %get-tuple-element.65), channel_id=1, source_target_pairs={{0,6},{1,7},{2,4},{3,5},{4,2},{5,3},{6,0},{7,1},{8,14},{9,15},{10,... | collective-permute-start | bytes 786440 | tf_op jit(solution)/shard_map/ppermute | solution.py:163

commit v2 on v1

--- a/solution.py
+++ b/solution.py
@@ -163,7 +163,7 @@
     return lax.ppermute(value, axis, [(i, i ^ bits) for i in range(size)])
 
 
-def call(body, name, outs, args, *, grid=(), in_specs=None, out_specs=None, scratch=(), scalars=0, vmem=12, needs=(), passed=None):
+def call(body, name, outs, args, *, grid=(), in_specs=None, out_specs=None, scratch=(), scalars=0, vmem=12, needs=(), passed=None, hint=1):
     given = len(args)
     extra = [*needs] + ([passed] if passed is not None else [])
     in_specs = list(in_specs) if in_specs is not None else [pl.BlockSpec()] * (given - scalars)
@@ -193,7 +193,9 @@
         out_shape=outs,
         name=name,
         input_output_aliases=aliases,
-        cost_estimate=pl.CostEstimate(flops=HINT_FLOPS, bytes_accessed=HINT_BYTES, transcendentals=0),
+        cost_estimate=pl.CostEstimate(
+            flops=HINT_FLOPS * hint, bytes_accessed=HINT_BYTES * hint, transcendentals=0
+        ),
         compiler_params=pltpu.CompilerParams(vmem_limit_bytes=vmem * MIB),
     )(*args, *extra)
 
@@ -258,6 +260,17 @@
         part_ref[g] = total[:, :rank] + total[:, rank:]
 
 
+def message_body(local, dy_ref, lists_ref, tenant_ref, out_ref):
+    rows, span = dy_ref.shape
+    _, holders, capacity = lists_ref.shape
+    count = tenant_ref.shape[0]
+    out_ref[:rows, :] = dy_ref[...]
+    ids = lax.rem(tenant_ref[...], local).astype(F32)
+    tail = jnp.concatenate([lists_ref[0].astype(F32), ids, jnp.zeros((16 - holders - count, capacity), F32)], axis=0)
+    tail = jnp.concatenate([tail, jnp.zeros((16, span - capacity), F32)], axis=1)
+    out_ref[rows:, :] = tail.astype(BF16)
+
+
 def place_body(upper_ref, odd_ref):
     place = lax.axis_index("fsdp")
     upper_ref[...] = jnp.full(upper_ref.shape, (place >= lax.axis_size("fsdp") // 2).astype(F32))
@@ -265,14 +278,15 @@
 
 
 def low_body(local, count, first, *refs):
-    blocks = refs[: 2 * count]
-    own_ref, ids_ref, down_ref, slots_ref, part_ref = refs[2 * count :]
-    half = blocks[0].shape[0]
+    own_ref, ids_ref, down_ref, slots_ref, part_ref = refs[-5:]
+    pieces = (len(refs) - 5) // count
+    rows = own_ref.shape[1] // pieces
     capacity = own_ref.shape[2]
     width = down_ref.shape[2]
     for j in range(count):
-        picked = contract(own_ref[first + j, :half], blocks[2 * j][...], 0, 0)
-        picked += contract(own_ref[first + j, half:], blocks[2 * j + 1][...], 0, 0)
+        picked = contract(own_ref[first + j, :rows], refs[pieces * j][...], 0, 0)
+        for i in range(1, pieces):
+            picked += contract(own_ref[first + j, i * rows : (i + 1) * rows], refs[pieces * j + i][...], 0, 0)
         slots_ref[j * capacity : (j + 1) * capacity, :] = picked.astype(BF16)
     ids = ids_ref[first : first + count].reshape(count * capacity, capacity)
     total = jnp.zeros((count * capacity, width), F32)
@@ -359,7 +373,8 @@
 
 def down_grad_body(local, pieces, *refs):
     blocks = refs[:pieces]
-    low_ref, ids_ref, out_ref, wide_ref = refs[pieces:]
+    low_ref, ids_ref, out_ref, made_ref, wide_ref = refs[pieces:]
+    made_ref[...] = jnp.zeros_like(made_ref)
     slots = low_ref.shape[0]
 
     @pl.when(pl.program_id(0) == 0)
@@ -389,19 +404,22 @@
     half = rows // 2
     chunk = 512
 
-    extra = jnp.concatenate([send_list[0], (tenant % local).reshape(-1, capacity)], axis=0).astype(BF16)
-    extra = jnp.pad(extra, ((0, 16 - extra.shape[0]), (0, span - capacity)))
-    message = jnp.concatenate([cotangent, extra], axis=0)
+    (message,) = call(
+        lambda *refs: message_body(local, *refs),
+        "message",
+        [shape((rows + 16, span))],
+        [cotangent, send_list, tenant.reshape(-1, capacity)],
+    )
     near = {0: message}
     for bits in (2, 4, 6):
         near[bits] = swap(message, "adapter", bits)
     top, bottom = tokens[:half], tokens[half:]
     base_partial = jnp.dot(tokens, base_weight, preferred_element_type=F32).astype(BF16)
-    near[2], near[4], near[6], top = tie((near[2], near[4], near[6], top), (base_partial,))
+    far_dy = swap(cotangent, "fsdp", 2)
+    near[2], near[4], near[6], top = tie((near[2], near[4], near[6], top), (base_partial, far_dy))
     messages = []
     for bits in ORDER[::2]:
         messages += [near[bits], swap(near[bits], "adapter", 1)]
-    far_dy = swap(cotangent, "fsdp", 2)
     slots_dy, ids, own, mate, back_part = call(
         lambda *refs: back_body(holders, capacity, rank, local, *refs),
         "back_rows",
@@ -436,13 +454,12 @@
 
     got1 = swap(back_part.astype(BF16), "fsdp", 1)
     x_top, y_top = swap(top, "adapter", 2), swap(top, "adapter", 4)
-    x_a, low_a = low_rows(0, with_mates((top, bottom)))
+    x_a, low_a = low_rows(0, with_mates((tokens,)))
     back_half = (back_part + got1.astype(F32)).astype(BF16)
-    (back_half,) = tie((back_half,), (x_top, y_top, low_a, far_dy))
+    (back_half,) = tie((back_half,), (x_top, y_top, low_a))
 
     back_other = swap(back_half, "fsdp", 2)
     x_bottom, y_bottom = swap(bottom, "adapter", 2), swap(bottom, "adapter", 4)
-    next_dy = swap(cotangent, "fsdp", 1), swap(far_dy, "fsdp", 1)
     back_low = where(
         upper,
         jnp.concatenate([back_other, back_half], axis=1),
@@ -462,23 +479,16 @@
         out_specs=[pl.BlockSpec((holders // 2, capacity, chunk), lambda i: (0, 0, i))] * 2,
         scratch=[pltpu.VMEM((slots, local * pair), BF16)],
         vmem=16,
-        needs=(x_bottom, y_bottom, *next_dy),
+        needs=(x_bottom, y_bottom),
+        hint=1 << 14,
     )
 
     got = swap(odd, "adapter", 1)
     diag = (swap(y_top, "adapter", 2), swap(x_bottom, "adapter", 4))
     x_b, low_b = low_rows(4, with_mates((y_top, y_bottom), (x_top, x_bottom)))
-    x_c, low_c = low_rows(2, with_mates(diag))
-    low_part = jnp.concatenate([low_a, low_c, low_b], axis=0)
-    keep = where(upper, low_part[:, rank:], low_part[:, :rank])
-    give = where(upper, low_part[:, :rank], low_part[:, rank:]).astype(BF16)
     diag_low, diag_high = expand(
-        "back_diag", 1, 1, ((0, 0, half), (0, half, half)), own, mate, even, got, 1024, needs=(give,)
-    )
-
-    low_in = swap(diag_low, "adapter", 2)
-    high_in = swap(diag_high, "adapter", 4)
-    got_low = swap(give, "fsdp", 2)
+        "back_diag", 1, 1, ((0, 0, half), (0, half, half)), own, mate, even, got, 1024
+    )
     y_low, y_high, x_low, x_high = expand(
         "back_near",
         2,
@@ -490,29 +500,45 @@
         got,
         1024,
     )
-    (down_grad,) = call(
+    *diag, base_partial = tie((*diag, base_partial), (low_b, diag_low, y_low))
+
+    low_in = swap(diag_low, "adapter", 2)
+    high_in = swap(diag_high, "adapter", 4)
+    quarter = [base_partial[:, i * span : (i + 1) * span] for i in range(4)]
+    base_keep = [where(odd_place, quarter[1], quarter[0]), where(odd_place, quarter[3], quarter[2])]
+    base_give = [where(odd_place, quarter[0], quarter[1]), where(odd_place, quarter[2], quarter[3])]
+    base_got = swap(jnp.concatenate(base_give, axis=1), "fsdp", 1)
+    x_c, low_c = low_rows(2, with_mates(tuple(diag)))
+    low_part = jnp.concatenate([low_a, low_c, low_b], axis=0)
+    keep = where(upper, low_part[:, rank:], low_part[:, :rank])
+    give = where(upper, low_part[:, :rank], low_part[:, rank:]).astype(BF16)
+    to_y, to_x = y_low + low_in, x_high + high_in
+    give, y_high, x_low = tie((give, y_high, x_low), (to_y, to_x))
+
+    got_low = swap(give, "fsdp", 2)
+    next_dy = swap(jnp.stack([cotangent, far_dy]), "fsdp", 1)
+    high_from_y = swap(y_high, "adapter", 4)
+    low_from_x = swap(x_low, "adapter", 2)
+    down_grad, made = call(
         lambda *refs: down_grad_body(local, 3, *refs),
         "down_grad",
-        [shape((local, width, pair))],
+        [shape((local, width, pair)), shape((8, 128), F32)],
         [x_a, x_c, x_b, back_low, flat_ids],
         grid=(width // 256,),
         in_specs=[pl.BlockSpec((x.shape[0], 256), lambda i: (0, i)) for x in (x_a, x_c, x_b)]
         + [pl.BlockSpec((slots, pair), lambda i: (0, 0)), pl.BlockSpec((slots, capacity), lambda i: (0, 0))],
-        out_specs=[pl.BlockSpec((local, 256, pair), lambda i: (0, i, 0))],
+        out_specs=[pl.BlockSpec((local, 256, pair), lambda i: (0, i, 0)), pl.BlockSpec((8, 128), lambda i: (0, 0))],
         scratch=[pltpu.VMEM((slots, local * pair), BF16)],
         vmem=16,
     )
-    quarter = [base_partial[:, i * span : (i + 1) * span] for i in range(4)]
-    base_keep = [where(odd_place, quarter[1], quarter[0]), where(odd_place, quarter[3], quarter[2])]
-    base_give = [where(odd_place, quarter[0], quarter[1]), where(odd_place, quarter[2], quarter[3])]
-    base_got = swap(jnp.concatenate(base_give, axis=1), "fsdp", 1)
-    to_y, to_x = y_low + low_in, x_high + high_in
     low_sum = keep + got_low.astype(F32)
-    (low_sent,) = tie((low_sum.astype(BF16),), (to_y, to_x, down_grad, base_got))
+    low_sent, base_got, to_y, to_x = tie(
+        (low_sum.astype(BF16), base_got, to_y, to_x), (made, next_dy, high_from_y, low_from_x)
+    )
 
     got2 = swap(low_sent, "fsdp", 1)
-    high_from_y = swap(y_high, "adapter", 4)
-    low_from_x = swap(x_low, "adapter", 2)
+    low_from_y = swap(to_y, "adapter", 4)
+    high_from_x = swap(to_x, "adapter", 2)
     ordered = [
         where(odd_place, b, a) for a, b in ((cotangent, next_dy[0]), (next_dy[0], cotangent))
     ], [where(odd_place, b, a) for a, b in ((far_dy, next_dy[1]), (next_dy[1], far_dy))]
@@ -521,22 +547,21 @@
     )
     input_base = contract(all_dy, base_weight, 1, 1)
     (home,) = expand("back_home", 0, 1, ((0, 0, rows),), own, mate, even, got, 1024)
-    low_half = (low_sum + got2.astype(F32)).astype(BF16)
-    up_odd, up_even, wide_low = call(
-        lambda *refs: up_body(local, *refs),
-        "up_delta",
-        [shape((holders // 2, capacity, span))] * 2 + [shape((slots, local * rank))],
-        [low_half, ids, up_weight],
-        needs=(input_base, home, high_from_y, low_from_x),
-    )
-
-    low_from_y = swap(to_y, "adapter", 4)
-    high_from_x = swap(to_x, "adapter", 2)
     base_sum = [
         base_keep[i].astype(F32) + base_got[:, i * span : (i + 1) * span].astype(F32) for i in range(2)
     ]
     base_far = swap(where(upper, base_sum[0], base_sum[1]).astype(BF16), "fsdp", 2)
     base_out = where(upper, base_sum[1], base_sum[0]) + base_far.astype(F32)
+    low_half = (low_sum + got2.astype(F32)).astype(BF16)
+    up_odd, up_even, wide_low, input_base = call(
+        lambda *refs: up_body(local, *refs),
+        "up_delta",
+        [shape((holders // 2, capacity, span))] * 2 + [shape((slots, local * rank))],
+        [low_half, ids, up_weight],
+        needs=(home, low_from_y, high_from_x, base_far),
+        passed=input_base,
+    )
+
     up_got = swap(up_odd, "adapter", 1)
     add_home, add_diag, add_y, add_x = expand(
         "up_rows", 0, 4, tuple((p, 0, rows) for p in range(4)), own, mate, up_even, up_got, 512

time: 168 us -> 150 us (0.89)
  waiting for transfers between devices: 79.8 us -> 63.9 us
  starting transfers between devices: 40.5 us -> 36.3 us
    ppermute x41 -> x39, waiting for transfers between devices: 79.8 us -> 63.9 us  [swap(): return lax.ppermute(value, axis, [(i, i ^ bits) for i in range(size)])]
    ppermute x41 -> x39, starting transfers between devices: 40.5 us -> 36.3 us  [swap(): return lax.ppermute(value, axis, [(i, i ^ bits) for i in range(size)])]
    pallas_call x12 -> x13, Pallas kernels: 28.1 us -> 28.9 us  [call(): pl.pallas_call(run, grid_spec=spec, out_shape=outs, name=name, input_outp...]
  transfers between devices with their start and end apart: 41 -> 39, of which waited for: 18 -> 19; matrix products, arithmetic and copies ran while one was open for 6% -> 11% of each run, Pallas kernels for 12% -> 13%
where the time goes in v2:
time: 150 us
  waiting for transfers between devices  63.9 us (43%)
  starting transfers between devices  36.3 us (24%)
  Pallas kernels  28.9 us (19%)
  matrix products  9.93 us (7%)
  other arithmetic  6.01 us (4%)
  local copies, waits for them, and re-layouts  2.54 us (2%)
  between operations  2.33 us (2%)
    ppermute x39, waiting for transfers between devices, swap(): return lax.ppermute(value, axis, [(i, i ^ bits) for i in range(size)])  63.9 us
    ppermute x39, starting transfers between devices, swap(): return lax.ppermute(value, axis, [(i, i ^ bits) for i in range(size)])  36.3 us
    pallas_call x13, Pallas kernels, call(): pl.pallas_call(run, grid_spec=spec, out_shape=outs, name=name, input_outp...  28.9 us
    dot_general x1, matrix products, shards(): jnp.dot(tokens, base_weight, preferred_element_type=F32).astype(BF16)  6.05 us
    dot_general x2, matrix products, contract(): lax.dot_general(left, right, (((left_dim,), (right_dim,)), ((), ())), pre...  3.89 us
  transfers between devices with their start and end apart: 39, of which 19 were waited for; matrix products, arithmetic and copies ran while one was open for 11% of the time, Pallas kernels for 13%

profile of v2, /device:TPU:0, one launch (start us, length us, event | category | flops | bytes accessed | tf_op | source)
XLA Modules:
  0.0 149.9 jit_solution(1110388249230121733)
XLA Ops:
  2.0 1.0 message.1.refs_0_
  3.0 3.0 %collective-permute-start = (bf16[272,512]{1,0:T(8,128)(2,1)S(1)}, bf16[272,512]{1,0:T(8,128)(2,1)S(1)}, u32[]{:S(2)}, u32[]{:S(2)}) collective-permute-start(bf16[272,512]{1,0:T(8,128)(2,1)S(1)} %message.1.refs_0_), channel_id=1, source_target_pairs={{0,2},{1,3},{2,0},{3,1},{4,6},{5,7},{6,4},{7,5},{8,10},{9,11},{10,... | collective-permute-start | bytes 835592 | tf_op jit(solution)/shard_map/ppermute | solution.py:163
  6.0 1.5 %collective-permute-start.1 = (bf16[272,512]{1,0:T(8,128)(2,1)S(1)}, bf16[272,512]{1,0:T(8,128)(2,1)S(1)}, u32[]{:S(2)}, u32[]{:S(2)}) collective-permute-start(bf16[272,512]{1,0:T(8,128)(2,1)S(1)} %message.1.refs_0_), channel_id=1, source_target_pairs={{0,4},{1,5},{2,6},{3,7},{4,0},{5,1},{6,2},{7,3},{8,12},{9,13},{10,... | collective-permute-start | bytes 835592 | tf_op jit(solution)/shard_map/ppermute | solution.py:163
  7.5 3.0 %collective-permute-start.3 = (bf16[256,512]{1,0:T(8,128)(2,1)}, bf16[256,512]{1,0:T(8,128)(2,1)S(1)}, u32[]{:S(2)}, u32[]{:S(2)}) collective-permute-start(bf16[256,512]{1,0:T(8,128)(2,1)} %refs_0_.2), channel_id=1, source_target_pairs={{0,16},{8,24},{16,0},{24,8},{1,17},{9,25},{17,1},{25,9},{2,18},{10... | collective-permute-start | bytes 786440 | tf_op jit(solution)/shard_map/ppermute | solution.py:163
  10.6 6.0 %convolution_convert_fusion.refs_4_.refs_2_ = bf16[256,2048]{1,0:T(8,128)(2,1)S(1)} fusion(bf16[256,2048]{1,0:T(8,128)(2,1)} %refs_0_.3, bf16[2048,2048]{1,0:T(8,128)(2,1)} %param.10), kind=kOutput, calls=%fused_computation | convolution fusion | flops 2148007936 | bytes 10485760 | tf_op jit(solution)/shard_map/dot_general | solution.py:417
  16.7 5.1 %collective-permute-done.3.refs_5_ = bf16[256,512]{1,0:T(8,128)(2,1)S(1)} collective-permute-done((bf16[256,512]{1,0:T(8,128)(2,1)}, bf16[256,512]{1,0:T(8,128)(2,1)S(1)}, u32[]{:S(2)}, u32[]{:S(2)}) %collective-permute-start.3) | collective-permute-done | bytes 262176 | tf_op jit(solution)/shard_map/ppermute | solution.py:163
  23.4 1.6 %collective-permute-start.4 = (bf16[128,2048]{1,0:T(8,128)(2,1)S(1)}, bf16[128,2048]{1,0:T(8,128)(2,1)S(1)}, u32[]{:S(2)}, u32[]{:S(2)}) collective-permute-start(bf16[128,2048]{1,0:T(8,128)(2,1)S(1)} %get-tuple-element.51), channel_id=1, source_target_pairs={{0,4},{1,5},{2,6},{3,7},{4,0},{5,1},{6,2},{7,3},{8,12},{9,13},{10,... | collective-permute-start | bytes 1572872 | tf_op jit(solution)/shard_map/ppermute | solution.py:163
  25.0 1.5 collective-permute-start.11
  26.5 2.5 %back_rows.1 = (bf16[8,128,512]{2,1,0:T(8,128)(2,1)S(1)}, f32[8,128,128]{2,1,0:T(8,128)S(1)}, bf16[8,256,128]{2,1,0:T(8,128)(2,1)S(1)}, bf16[4,256,128]{2,1,0:T(8,128)(2,1)S(1)}, f32[8,128,64]{2,1,0:T(8,128)S(1)}) custom-call(bf16[272,512]{1,0:T(8,128)(2,1)S(1)} %message.1.refs_0_, bf16[272,512]{1,0:T(8,128)(2,1)S(1)} %collective-permute-done.14.refs_1_, ...), custom_call_target="tpu_custom_call" | custom-call | flops 1024 | bytes 1024 | tf_op jit(solution)/shard_map/back_rows/pallas_call | solution.py:190
  30.5 6.5 %collective-permute-done.18 = bf16[1024,64]{1,0:T(8,128)(2,1)S(1)} collective-permute-done((bf16[1024,64]{1,0:T(8,128)(2,1)S(1)}, bf16[1024,64]{1,0:T(8,128)(2,1)S(1)}, u32[]{:S(2)}, u32[]{:S(2)}) %collective-permute-start.18) | collective-permute-done | bytes 131104 | tf_op jit(solution)/shard_map/ppermute | solution.py:163
  37.8 1.6 %low_rows.4 = (bf16[256,2048]{1,0:T(8,128)(2,1)S(1)}, f32[256,128]{1,0:T(8,128)S(1)}) custom-call(bf16[256,2048]{1,0:T(8,128)(2,1)S(1)} %copy-done.1, bf16[256,2048]{1,0:T(8,128)(2,1)S(1)} %collective-permute-done.19.refs_1_, bf16[8,256,128]{2,1,0:T(8,128)(2,1)S(1)} %get-tuple-element.55.refs_8_.refs_2_.refs_0_.refs_4_, ...), custom_call_target="tpu_custom_call" | custom-call | flops 1024 | bytes 1024 | tf_op jit(solution)/shard_map/low_rows/pallas_call | solution.py:190
  39.8 1.9 %collective-permute-start.20 = (bf16[1024,64]{1,0:T(8,128)(2,1)S(1)}, bf16[1024,64]{1,0:T(8,128)(2,1)S(1)}, u32[]{:S(2)}, u32[]{:S(2)}) collective-permute-start(bf16[1024,64]{1,0:T(8,128)(2,1)S(1)} %tie.6), channel_id=1, source_target_pairs={{0,16},{8,24},{16,0},{24,8},{1,17},{9,25},{17,1},{25,9},{2,18},{10... | collective-permute-start | bytes 393224 | tf_op jit(solution)/shard_map/ppermute | solution.py:163
  42.9 9.9 %collective-permute-done.20 = bf16[1024,64]{1,0:T(8,128)(2,1)S(1)} collective-permute-done((bf16[1024,64]{1,0:T(8,128)(2,1)S(1)}, bf16[1024,64]{1,0:T(8,128)(2,1)S(1)}, u32[]{:S(2)}, u32[]{:S(2)}) %collective-permute-start.20) | collective-permute-done | bytes 131104 | tf_op jit(solution)/shard_map/ppermute | solution.py:163
  53.1 6.3 %back_delta.1 = (bf16[4,128,2048]{2,1,0:T(8,128)(2,1)S(1)}, bf16[4,128,2048]{2,1,0:T(8,128)(2,1)S(1)}) custom-call(bf16[1024,128]{1,0:T(8,128)(2,1)S(1)} %maximum_select_fusion.refs_0_.refs_3_, f32[8,128,128]{2,1,0:T(8,128)S(1)} %get-tuple-element.56.refs_9_.refs_3_.refs_1_.refs_5_, bf16[8,2048,128]{2,1,0:T(8,128)(2,1)S(1)} %copy-done, ...), custom_call_target="tpu_custom_call" | custom-call | flops 16777216 | bytes 16777216 | tf_op jit(solution)/shard_map/back_delta/pallas_call | solution.py:190
  60.6 3.8 %collective-permute-done.13.refs_7_ = bf16[128,2048]{1,0:T(8,128)(2,1)S(1)} collective-permute-done((bf16[128,2048]{1,0:T(8,128)(2,1)S(1)}, bf16[128,2048]{1,0:T(8,128)(2,1)S(1)}, u32[]{:S(2)}, u32[]{:S(2)}) %collective-permute-start.13) | collective-permute-done | bytes 524320 | tf_op jit(solution)/shard_map/ppermute | solution.py:163
  64.4 1.0 collective-permute-start.7
  65.4 1.2 collective-permute-start.5
  67.9 3.4 %low_rows.3 = (bf16[512,2048]{1,0:T(8,128)(2,1)S(1)}, f32[512,128]{1,0:T(8,128)S(1)}) custom-call(bf16[128,2048]{1,0:T(8,128)(2,1)S(1)} %collective-permute-done.4.refs_0_.refs_2_, bf16[128,2048]{1,0:T(8,128)(2,1)S(1)} %collective-permute-done.8.refs_1_.refs_4_, bf16[128,2048]{1,0:T(8,128)(2,1)S(1)} %collective-permute-done.9.refs_2_, ...), custom_call_target="tpu_custom_call" | custom-call | flops 1024 | bytes 1024 | tf_op jit(solution)/shard_map/low_rows/pallas_call | solution.py:190
  73.0 1.2 back_near.1
  74.2 4.2 %collective-permute-done.7.refs_1_ = bf16[128,2048]{1,0:T(8,128)(2,1)S(1)} collective-permute-done((bf16[128,2048]{1,0:T(8,128)(2,1)S(1)}, bf16[128,2048]{1,0:T(8,128)(2,1)S(1)}, u32[]{:S(2)}, u32[]{:S(2)}) %collective-permute-start.7) | collective-permute-done | bytes 524320 | tf_op jit(solution)/shard_map/ppermute | solution.py:163
  78.4 1.9 %collective-permute-done.5.refs_0_ = bf16[128,2048]{1,0:T(8,128)(2,1)S(1)} collective-permute-done((bf16[128,2048]{1,0:T(8,128)(2,1)S(1)}, bf16[128,2048]{1,0:T(8,128)(2,1)S(1)}, u32[]{:S(2)}, u32[]{:S(2)}) %collective-permute-start.5) | collective-permute-done | bytes 524320 | tf_op jit(solution)/shard_map/ppermute | solution.py:163
  80.8 1.0 collective-permute-start.25
  81.8 1.0 pad_maximum_fusion.1
  83.6 1.4 collective-permute-start.27
  85.1 1.8 %low_rows.5 = (bf16[256,2048]{1,0:T(8,128)(2,1)S(1)}, f32[256,128]{1,0:T(8,128)S(1)}) custom-call(bf16[128,2048]{1,0:T(8,128)(2,1)S(1)} %get-tuple-element.66.refs_0_, bf16[128,2048]{1,0:T(8,128)(2,1)S(1)} %get-tuple-element.67.refs_1_, bf16[128,2048]{1,0:T(8,128)(2,1)S(1)} %collective-permute-done.22.refs_2_, ...), custom_call_target="tpu_custom_call" | custom-call | flops 1024 | bytes 1024 | tf_op jit(solution)/shard_map/low_rows/pallas_call | solution.py:190
  86.9 3.5 %collective-permute-done.24 = bf16[128,2048]{1,0:T(8,128)(2,1)S(1)} collective-permute-done((bf16[128,2048]{1,0:T(8,128)(2,1)S(1)}, bf16[128,2048]{1,0:T(8,128)(2,1)S(1)}, u32[]{:S(2)}, u32[]{:S(2)}) %collective-permute-start.24) | collective-permute-done | bytes 524320 | tf_op jit(solution)/shard_map/ppermute | solution.py:163
  90.5 4.1 %collective-permute-done.25 = bf16[128,2048]{1,0:T(8,128)(2,1)S(1)} collective-permute-done((bf16[128,2048]{1,0:T(8,128)(2,1)S(1)}, bf16[128,2048]{1,0:T(8,128)(2,1)S(1)}, u32[]{:S(2)}, u32[]{:S(2)}) %collective-permute-start.25) | collective-permute-done | bytes 524320 | tf_op jit(solution)/shard_map/ppermute | solution.py:163
  94.9 1.1 collective-permute-start.29
  96.0 1.5 %collective-permute-start.30 = (bf16[128,2048]{1,0:T(8,128)(2,1)S(1)}, bf16[128,2048]{1,0:T(8,128)(2,1)S(1)}, u32[]{:S(2)}, u32[]{:S(2)}) collective-permute-start(bf16[128,2048]{1,0:T(8,128)(2,1)S(1)} %get-tuple-element.79), channel_id=1, source_target_pairs={{0,2},{1,3},{2,0},{3,1},{4,6},{5,7},{6,4},{7,5},{8,10},{9,11},{10,... | collective-permute-start | bytes 1572872 | tf_op jit(solution)/shard_map/ppermute | solution.py:163
  97.7 1.0 broadcast_select_fusion.11
  98.7 7.8 %down_grad.1 = (bf16[8,2048,128]{2,1,0:T(8,128)(2,1)}, f32[8,128]{1,0:T(8,128)S(1)}) custom-call(bf16[256,2048]{1,0:T(8,128)(2,1)S(1)} %get-tuple-element.74.refs_0_, bf16[256,2048]{1,0:T(8,128)(2,1)S(1)} %get-tuple-element.75.refs_1_, bf16[512,2048]{1,0:T(8,128)(2,1)S(1)} %get-tuple-element.76.refs_2_, ...), custom_call_target="tpu_custom_call" | custom-call | flops 1024 | bytes 1024 | tf_op jit(solution)/shard_map/down_grad/pallas_call | solution.py:190
  106.5 4.9 %collective-permute-done.26 = bf16[1024,64]{1,0:T(8,128)(2,1)S(1)} collective-permute-done((bf16[1024,64]{1,0:T(8,128)(2,1)S(1)}, bf16[1024,64]{1,0:T(8,128)(2,1)S(1)}, u32[]{:S(2)}, u32[]{:S(2)}) %collective-permute-start.26) | collective-permute-done | bytes 131104 | tf_op jit(solution)/shard_map/ppermute | solution.py:163
  111.6 1.6 %collective-permute-done.27.refs_1_ = bf16[256,1024]{1,0:T(8,128)(2,1)S(1)} collective-permute-done((bf16[256,1024]{1,0:T(8,128)(2,1)S(1)}, bf16[256,1024]{1,0:T(8,128)(2,1)S(1)}, u32[]{:S(2)}, u32[]{:S(2)}) %collective-permute-start.27) | collective-permute-done | bytes 524320 | tf_op jit(solution)/shard_map/ppermute | solution.py:163
  113.2 2.6 %collective-permute-start.32 = (bf16[1024,64]{1,0:T(8,128)(2,1)S(1)}, bf16[1024,64]{1,0:T(8,128)(2,1)S(1)}, u32[]{:S(2)}, u32[]{:S(2)}) collective-permute-start(bf16[1024,64]{1,0:T(8,128)(2,1)S(1)} %get-tuple-element.81), channel_id=1, source_target_pairs={{0,8},{8,0},{16,24},{24,16},{1,9},{9,1},{17,25},{25,17},{2,10},{10... | collective-permute-start | bytes 393224 | tf_op jit(solution)/shard_map/ppermute | solution.py:163
  116.1 1.6 %collective-permute-start.31 = (bf16[256,512]{1,0:T(8,128)(2,1)S(1)}, bf16[256,512]{1,0:T(8,128)(2,1)S(1)}, u32[]{:S(2)}, u32[]{:S(2)}) collective-permute-start(bf16[256,512]{1,0:T(8,128)(2,1)S(1)} %select_convert_fusion), channel_id=1, source_target_pairs={{0,16},{8,24},{16,0},{24,8},{1,17},{9,25},{17,1},{25,9},{2,18},{10... | collective-permute-start | bytes 786440 | tf_op jit(solution)/shard_map/ppermute | solution.py:163
  117.6 1.0 collective-permute-start.33
  118.6 1.2 collective-permute-start.34
  119.9 2.4 %fusion.1.refs_7_ = f32[256,2048]{1,0:T(8,128)S(1)} fusion(bf16[2048,2048]{1,0:T(8,128)(2,1)S(1)} %bitcast.51, bf16[256,512]{1,0:T(8,128)(2,1)S(1)} %get-tuple-element.99, bf16[256,512]{1,0:T(8,128)(2,1)S(1)} %get-tuple-element.98, bf16[256,512]{1,0:T(8,128)(2,1)S(1)} %get-tuple-element.97, bf16[256,512]{1,0:T(8,128)(2,1)S(1)} %get-tuple-element.96), kind=kOutput, calls=%fused_computation.4 | convolution fusion | flops 2151677952 | bytes 11534336 | tf_op jit(solution)/shard_map/dot_general | solution.py:156
  122.2 1.0 back_home.1.refs_3_
  123.2 1.9 %collective-permute-done.32 = bf16[1024,64]{1,0:T(8,128)(2,1)S(1)} collective-permute-done((bf16[1024,64]{1,0:T(8,128)(2,1)S(1)}, bf16[1024,64]{1,0:T(8,128)(2,1)S(1)}, u32[]{:S(2)}, u32[]{:S(2)}) %collective-permute-start.32) | collective-permute-done | bytes 131104 | tf_op jit(solution)/shard_map/ppermute | solution.py:163
  125.3 4.4 %collective-permute-done.31.refs_6_ = bf16[256,512]{1,0:T(8,128)(2,1)S(1)} collective-permute-done((bf16[256,512]{1,0:T(8,128)(2,1)S(1)}, bf16[256,512]{1,0:T(8,128)(2,1)S(1)}, u32[]{:S(2)}, u32[]{:S(2)}) %collective-permute-start.31) | collective-permute-done | bytes 262176 | tf_op jit(solution)/shard_map/ppermute | solution.py:163
  131.7 1.3 add_convert_fusion
  133.8 1.3 collective-permute-start.36
  135.1 1.3 collective-permute-start.37
  137.4 1.5 %fusion = bf16[512,512]{1,0:T(8,128)(2,1)} fusion(bf16[1024,512]{1,0:T(8,128)(2,1)S(1)} %get-tuple-element.92, bf16[1024,512]{1,0:T(8,128)(2,1)S(1)} %bitcast.49), kind=kOutput, calls=%fused_computation.3 | convolution fusion | flops 537395200 | bytes 2621440 | tf_op jit(solution)/shard_map/dot_general | solution.py:156
  138.9 4.1 %collective-permute-done.36 = bf16[256,512]{1,0:T(8,128)(2,1)S(1)} collective-permute-done((bf16[256,512]{1,0:T(8,128)(2,1)S(1)}, bf16[256,512]{1,0:T(8,128)(2,1)S(1)}, u32[]{:S(2)}, u32[]{:S(2)}) %collective-permute-start.36) | collective-permute-done | bytes 262176 | tf_op jit(solution)/shard_map/ppermute | solution.py:163
  143.1 5.7 %collective-permute-done.37 = bf16[256,512]{1,0:T(8,128)(2,1)S(1)} collective-permute-done((bf16[256,512]{1,0:T(8,128)(2,1)S(1)}, bf16[256,512]{1,0:T(8,128)(2,1)S(1)}, u32[]{:S(2)}, u32[]{:S(2)}) %collective-permute-start.37) | collective-permute-done | bytes 262176 | tf_op jit(solution)/shard_map/ppermute | solution.py:163
  148.8 1.1 add_convert_fusion.1
  (88 shorter events, 16.2 us)
Async XLA Ops:
  0.6 0.7 copy-start.3
  1.3 0.7 copy-start.4
  3.0 13.7 %copy-start.1 = (bf16[256,2048]{1,0:T(8,128)(2,1)S(1)}, bf16[256,2048]{1,0:T(8,128)(2,1)}, u32[]{:S(2)}) copy-start(bf16[256,2048]{1,0:T(8,128)(2,1)} %refs_0_.3) | copy-start | bytes 3145732
  3.0 18.9 %collective-permute-start = (bf16[272,512]{1,0:T(8,128)(2,1)S(1)}, bf16[272,512]{1,0:T(8,128)(2,1)S(1)}, u32[]{:S(2)}, u32[]{:S(2)}) collective-permute-start(bf16[272,512]{1,0:T(8,128)(2,1)S(1)} %message.1.refs_0_), channel_id=1, source_target_pairs={{0,2},{1,3},{2,0},{3,1},{4,6},{5,7},{6,4},{7,5},{8,10},{9,11},{10,... | collective-permute-start | bytes 835592 | tf_op jit(solution)/shard_map/ppermute | solution.py:163
  6.0 15.9 %collective-permute-start.1 = (bf16[272,512]{1,0:T(8,128)(2,1)S(1)}, bf16[272,512]{1,0:T(8,128)(2,1)S(1)}, u32[]{:S(2)}, u32[]{:S(2)}) collective-permute-start(bf16[272,512]{1,0:T(8,128)(2,1)S(1)} %message.1.refs_0_), channel_id=1, source_target_pairs={{0,4},{1,5},{2,6},{3,7},{4,0},{5,1},{6,2},{7,3},{8,12},{9,13},{10,... | collective-permute-start | bytes 835592 | tf_op jit(solution)/shard_map/ppermute | solution.py:163
  7.5 14.4 %collective-permute-start.2 = (bf16[272,512]{1,0:T(8,128)(2,1)S(1)}, bf16[272,512]{1,0:T(8,128)(2,1)S(1)}, u32[]{:S(2)}, u32[]{:S(2)}) collective-permute-start(bf16[272,512]{1,0:T(8,128)(2,1)S(1)} %message.1.refs_0_), channel_id=1, source_target_pairs={{0,6},{1,7},{2,4},{3,5},{4,2},{5,3},{6,0},{7,1},{8,14},{9,15},{10,... | collective-permute-start | bytes 835592 | tf_op jit(solution)/shard_map/ppermute | solution.py:163
  7.5 14.3 %collective-permute-start.3 = (bf16[256,512]{1,0:T(8,128)(2,1)}, bf16[256,512]{1,0:T(8,128)(2,1)S(1)}, u32[]{:S(2)}, u32[]{:S(2)}) collective-permute-start(bf16[256,512]{1,0:T(8,128)(2,1)} %refs_0_.2), channel_id=1, source_target_pairs={{0,16},{8,24},{16,0},{24,8},{1,17},{9,25},{17,1},{25,9},{2,18},{10... | collective-permute-start | bytes 786440 | tf_op jit(solution)/shard_map/ppermute | solution.py:163
  10.6 27.2 %collective-permute-start.19 = (bf16[256,2048]{1,0:T(8,128)(2,1)}, bf16[256,2048]{1,0:T(8,128)(2,1)S(1)}, u32[]{:S(2)}, u32[]{:S(2)}) collective-permute-start(bf16[256,2048]{1,0:T(8,128)(2,1)} %refs_0_.3), channel_id=1, source_target_pairs={{0,1},{1,0},{2,3},{3,2},{4,5},{5,4},{6,7},{7,6},{8,9},{9,8},{10,11... | collective-permute-start | bytes 3145736 | tf_op jit(solution)/shard_map/ppermute | solution.py:163
  16.6 9.9 %copy-start.2 = (bf16[8,64,512]{2,1,0:T(8,128)(2,1)S(1)}, bf16[8,64,512]{2,1,0:T(8,128)(2,1)}, u32[]{:S(2)}) copy-start(bf16[8,64,512]{2,1,0:T(8,128)(2,1)} %refs_2_.3) | copy-start | bytes 1572868
  21.9 1.6 %collective-permute-start.14 = (bf16[272,512]{1,0:T(8,128)(2,1)S(1)}, bf16[272,512]{1,0:T(8,128)(2,1)S(1)}, u32[]{:S(2)}, u32[]{:S(2)}) collective-permute-start(bf16[272,512]{1,0:T(8,128)(2,1)S(1)} %message.1.refs_0_), channel_id=1, source_target_pairs={{0,1},{1,0},{2,3},{3,2},{4,5},{5,4},{6,7},{7,6},{8,9},{9,8},{10,11... | collective-permute-start | bytes 835592 | tf_op jit(solution)/shard_map/ppermute | solution.py:163
  21.9 3.1 %collective-permute-start.15 = (bf16[272,512]{1,0:T(8,128)(2,1)S(1)}, bf16[272,512]{1,0:T(8,128)(2,1)S(1)}, u32[]{:S(2)}, u32[]{:S(2)}) collective-permute-start(bf16[272,512]{1,0:T(8,128)(2,1)S(1)} %get-tuple-element.52.refs_2_), channel_id=1, source_target_pairs={{0,1},{1,0},{2,3},{3,2},{4,5},{5,4},{6,7},{7,6},{8,9},{9,8},{10,11... | collective-permute-start | bytes 835592 | tf_op jit(solution)/shard_map/ppermute | solution.py:163
  22.5 4.0 %collective-permute-start.16 = (bf16[272,512]{1,0:T(8,128)(2,1)S(1)}, bf16[272,512]{1,0:T(8,128)(2,1)S(1)}, u32[]{:S(2)}, u32[]{:S(2)}) collective-permute-start(bf16[272,512]{1,0:T(8,128)(2,1)S(1)} %get-tuple-element.53.refs_4_), channel_id=1, source_target_pairs={{0,1},{1,0},{2,3},{3,2},{4,5},{5,4},{6,7},{7,6},{8,9},{9,8},{10,11... | collective-permute-start | bytes 835592 | tf_op jit(solution)/shard_map/ppermute | solution.py:163
  22.5 4.0 %collective-permute-start.17 = (bf16[272,512]{1,0:T(8,128)(2,1)S(1)}, bf16[272,512]{1,0:T(8,128)(2,1)S(1)}, u32[]{:S(2)}, u32[]{:S(2)}) collective-permute-start(bf16[272,512]{1,0:T(8,128)(2,1)S(1)} %get-tuple-element.54.refs_6_), channel_id=1, source_target_pairs={{0,1},{1,0},{2,3},{3,2},{4,5},{5,4},{6,7},{7,6},{8,9},{9,8},{10,11... | collective-permute-start | bytes 835592 | tf_op jit(solution)/shard_map/ppermute | solution.py:163
  23.4 14.3 %copy-start = (bf16[8,2048,128]{2,1,0:T(8,128)(2,1)S(1)}, bf16[8,2048,128]{2,1,0:T(8,128)(2,1)}, u32[]{:S(2)}) copy-start(bf16[8,2048,128]{2,1,0:T(8,128)(2,1)} %refs_6_.1) | copy-start | bytes 12582916
  23.4 15.9 %collective-permute-start.4 = (bf16[128,2048]{1,0:T(8,128)(2,1)S(1)}, bf16[128,2048]{1,0:T(8,128)(2,1)S(1)}, u32[]{:S(2)}, u32[]{:S(2)}) collective-permute-start(bf16[128,2048]{1,0:T(8,128)(2,1)S(1)} %get-tuple-element.51), channel_id=1, source_target_pairs={{0,4},{1,5},{2,6},{3,7},{4,0},{5,1},{6,2},{7,3},{8,12},{9,13},{10,... | collective-permute-start | bytes 1572872 | tf_op jit(solution)/shard_map/ppermute | solution.py:163
  25.0 14.8 %collective-permute-start.11 = (bf16[128,2048]{1,0:T(8,128)(2,1)S(1)}, bf16[128,2048]{1,0:T(8,128)(2,1)S(1)}, u32[]{:S(2)}, u32[]{:S(2)}) collective-permute-start(bf16[128,2048]{1,0:T(8,128)(2,1)S(1)} %get-tuple-element.51), channel_id=1, source_target_pairs={{0,2},{1,3},{2,0},{3,1},{4,6},{5,7},{6,4},{7,5},{8,10},{9,11},{10,... | collective-permute-start | bytes 1572872 | tf_op jit(solution)/shard_map/ppermute | solution.py:163
  29.1 7.9 %collective-permute-start.18 = (bf16[1024,64]{1,0:T(8,128)(2,1)S(1)}, bf16[1024,64]{1,0:T(8,128)(2,1)S(1)}, u32[]{:S(2)}, u32[]{:S(2)}) collective-permute-start(bf16[1024,64]{1,0:T(8,128)(2,1)S(1)} %bitcast_convert_fusion), channel_id=1, source_target_pairs={{0,8},{8,0},{16,24},{24,16},{1,9},{9,1},{17,25},{25,17},{2,10},{10... | collective-permute-start | bytes 393224 | tf_op jit(solution)/shard_map/ppermute | solution.py:163
  29.9 23.1 %collective-permute-start.6 = (bf16[128,2048]{1,0:T(8,128)(2,1)S(1)}, bf16[128,2048]{1,0:T(8,128)(2,1)S(1)}, u32[]{:S(2)}, u32[]{:S(2)}) collective-permute-start(bf16[128,2048]{1,0:T(8,128)(2,1)S(1)} %get-tuple-element.102), channel_id=1, source_target_pairs={{0,2},{1,3},{2,0},{3,1},{4,6},{5,7},{6,4},{7,5},{8,10},{9,11},{10,... | collective-permute-start | bytes 1572872 | tf_op jit(solution)/shard_map/ppermute | solution.py:163
  37.0 16.1 %collective-permute-start.8 = (bf16[128,2048]{1,0:T(8,128)(2,1)S(1)}, bf16[128,2048]{1,0:T(8,128)(2,1)S(1)}, u32[]{:S(2)}, u32[]{:S(2)}) collective-permute-start(bf16[128,2048]{1,0:T(8,128)(2,1)S(1)} %get-tuple-element.102), channel_id=1, source_target_pairs={{0,4},{1,5},{2,6},{3,7},{4,0},{5,1},{6,2},{7,3},{8,12},{9,13},{10,... | collective-permute-start | bytes 1572872 | tf_op jit(solution)/shard_map/ppermute | solution.py:163
  39.8 13.0 %collective-permute-start.20 = (bf16[1024,64]{1,0:T(8,128)(2,1)S(1)}, bf16[1024,64]{1,0:T(8,128)(2,1)S(1)}, u32[]{:S(2)}, u32[]{:S(2)}) collective-permute-start(bf16[1024,64]{1,0:T(8,128)(2,1)S(1)} %tie.6), channel_id=1, source_target_pairs={{0,16},{8,24},{16,0},{24,8},{1,17},{9,25},{17,1},{25,9},{2,18},{10... | collective-permute-start | bytes 393224 | tf_op jit(solution)/shard_map/ppermute | solution.py:163
  59.4 11.9 %collective-permute-start.21 = (bf16[4,128,2048]{2,1,0:T(8,128)(2,1)S(1)}, bf16[4,128,2048]{2,1,0:T(8,128)(2,1)S(1)}, u32[]{:S(2)}, u32[]{:S(2)}) collective-permute-start(bf16[4,128,2048]{2,1,0:T(8,128)(2,1)S(1)} %get-tuple-element.62), channel_id=1, source_target_pairs={{0,1},{1,0},{2,3},{3,2},{4,5},{5,4},{6,7},{7,6},{8,9},{9,8},{10,11... | collective-permute-start | bytes 6291464 | tf_op jit(solution)/shard_map/ppermute | solution.py:163
  59.5 4.9 %collective-permute-start.13 = (bf16[128,2048]{1,0:T(8,128)(2,1)S(1)}, bf16[128,2048]{1,0:T(8,128)(2,1)S(1)}, u32[]{:S(2)}, u32[]{:S(2)}) collective-permute-start(bf16[128,2048]{1,0:T(8,128)(2,1)S(1)} %collective-permute-done.6.refs_5_.refs_3_), channel_id=1, source_target_pairs={{0,1},{1,0},{2,3},{3,2},{4,5},{5,4},{6,7},{7,6},{8,9},{9,8},{10,11... | collective-permute-start | bytes 1572872 | tf_op jit(solution)/shard_map/ppermute | solution.py:163
  60.0 5.4 %collective-permute-start.10 = (bf16[128,2048]{1,0:T(8,128)(2,1)S(1)}, bf16[128,2048]{1,0:T(8,128)(2,1)S(1)}, u32[]{:S(2)}, u32[]{:S(2)}) collective-permute-start(bf16[128,2048]{1,0:T(8,128)(2,1)S(1)} %collective-permute-done.8.refs_1_.refs_4_), channel_id=1, source_target_pairs={{0,1},{1,0},{2,3},{3,2},{4,5},{5,4},{6,7},{7,6},{8,9},{9,8},{10,11... | collective-permute-start | bytes 1572872 | tf_op jit(solution)/shard_map/ppermute | solution.py:163
  60.1 7.8 %collective-permute-start.9 = (bf16[128,2048]{1,0:T(8,128)(2,1)S(1)}, bf16[128,2048]{1,0:T(8,128)(2,1)S(1)}, u32[]{:S(2)}, u32[]{:S(2)}) collective-permute-start(bf16[128,2048]{1,0:T(8,128)(2,1)S(1)} %collective-permute-done.4.refs_0_.refs_2_), channel_id=1, source_target_pairs={{0,1},{1,0},{2,3},{3,2},{4,5},{5,4},{6,7},{7,6},{8,9},{9,8},{10,11... | collective-permute-start | bytes 1572872 | tf_op jit(solution)/shard_map/ppermute | solution.py:163
  60.5 7.3 %collective-permute-start.12 = (bf16[128,2048]{1,0:T(8,128)(2,1)S(1)}, bf16[128,2048]{1,0:T(8,128)(2,1)S(1)}, u32[]{:S(2)}, u32[]{:S(2)}) collective-permute-start(bf16[128,2048]{1,0:T(8,128)(2,1)S(1)} %collective-permute-done.11.refs_4_.refs_1_), channel_id=1, source_target_pairs={{0,1},{1,0},{2,3},{3,2},{4,5},{5,4},{6,7},{7,6},{8,9},{9,8},{10,11... | collective-permute-start | bytes 1572872 | tf_op jit(solution)/shard_map/ppermute | solution.py:163
  64.4 14.0 %collective-permute-start.7 = (bf16[128,2048]{1,0:T(8,128)(2,1)S(1)}, bf16[128,2048]{1,0:T(8,128)(2,1)S(1)}, u32[]{:S(2)}, u32[]{:S(2)}) collective-permute-start(bf16[128,2048]{1,0:T(8,128)(2,1)S(1)} %collective-permute-done.6.refs_5_.refs_3_), channel_id=1, source_target_pairs={{0,4},{1,5},{2,6},{3,7},{4,0},{5,1},{6,2},{7,3},{8,12},{9,13},{10,... | collective-permute-start | bytes 1572872 | tf_op jit(solution)/shard_map/ppermute | solution.py:163
  65.4 14.8 %collective-permute-start.5 = (bf16[128,2048]{1,0:T(8,128)(2,1)S(1)}, bf16[128,2048]{1,0:T(8,128)(2,1)S(1)}, u32[]{:S(2)}, u32[]{:S(2)}) collective-permute-start(bf16[128,2048]{1,0:T(8,128)(2,1)S(1)} %collective-permute-done.4.refs_0_.refs_2_), channel_id=1, source_target_pairs={{0,2},{1,3},{2,0},{3,1},{4,6},{5,7},{6,4},{7,5},{8,10},{9,11},{10,... | collective-permute-start | bytes 1572872 | tf_op jit(solution)/shard_map/ppermute | solution.py:163
  72.1 18.2 %collective-permute-start.24 = (bf16[128,2048]{1,0:T(8,128)(2,1)S(1)}, bf16[128,2048]{1,0:T(8,128)(2,1)S(1)}, u32[]{:S(2)}, u32[]{:S(2)}) collective-permute-start(bf16[128,2048]{1,0:T(8,128)(2,1)S(1)} %get-tuple-element.63.refs_4_), channel_id=1, source_target_pairs={{0,2},{1,3},{2,0},{3,1},{4,6},{5,7},{6,4},{7,5},{8,10},{9,11},{10,... | collective-permute-start | bytes 1572872 | tf_op jit(solution)/shard_map/ppermute | solution.py:163
  80.2 3.4 %collective-permute-start.22 = (bf16[128,2048]{1,0:T(8,128)(2,1)S(1)}, bf16[128,2048]{1,0:T(8,128)(2,1)S(1)}, u32[]{:S(2)}, u32[]{:S(2)}) collective-permute-start(bf16[128,2048]{1,0:T(8,128)(2,1)S(1)} %get-tuple-element.66.refs_0_), channel_id=1, source_target_pairs={{0,1},{1,0},{2,3},{3,2},{4,5},{5,4},{6,7},{7,6},{8,9},{9,8},{10,11... | collective-permute-start | bytes 1572872 | tf_op jit(solution)/shard_map/ppermute | solution.py:163
  80.2 4.8 %collective-permute-start.23 = (bf16[128,2048]{1,0:T(8,128)(2,1)S(1)}, bf16[128,2048]{1,0:T(8,128)(2,1)S(1)}, u32[]{:S(2)}, u32[]{:S(2)}) collective-permute-start(bf16[128,2048]{1,0:T(8,128)(2,1)S(1)} %get-tuple-element.67.refs_1_), channel_id=1, source_target_pairs={{0,1},{1,0},{2,3},{3,2},{4,5},{5,4},{6,7},{7,6},{8,9},{9,8},{10,11... | collective-permute-start | bytes 1572872 | tf_op jit(solution)/shard_map/ppermute | solution.py:163
  80.8 13.8 %collective-permute-start.25 = (bf16[128,2048]{1,0:T(8,128)(2,1)S(1)}, bf16[128,2048]{1,0:T(8,128)(2,1)S(1)}, u32[]{:S(2)}, u32[]{:S(2)}) collective-permute-start(bf16[128,2048]{1,0:T(8,128)(2,1)S(1)} %get-tuple-element.72), channel_id=1, source_target_pairs={{0,4},{1,5},{2,6},{3,7},{4,0},{5,1},{6,2},{7,3},{8,12},{9,13},{10,... | collective-permute-start | bytes 1572872 | tf_op jit(solution)/shard_map/ppermute | solution.py:163
  82.8 14.9 %collective-permute-start.28 = (bf16[2,256,512]{2,1,0:T(8,128)(2,1)S(1)}, bf16[2,256,512]{2,1,0:T(8,128)(2,1)S(1)}, u32[]{:S(2)}, u32[]{:S(2)}) collective-permute-start(bf16[2,256,512]{2,1,0:T(8,128)(2,1)S(1)} %pad_maximum_fusion.1), channel_id=1, source_target_pairs={{0,8},{8,0},{16,24},{24,16},{1,9},{9,1},{17,25},{25,17},{2,10},{10... | collective-permute-start | bytes 1572872 | tf_op jit(solution)/shard_map/ppermute | solution.py:163
  83.6 29.6 %collective-permute-start.27 = (bf16[256,1024]{1,0:T(8,128)(2,1)S(1)}, bf16[256,1024]{1,0:T(8,128)(2,1)S(1)}, u32[]{:S(2)}, u32[]{:S(2)}) collective-permute-start(bf16[256,1024]{1,0:T(8,128)(2,1)S(1)} %pad_maximum_fusion), channel_id=1, source_target_pairs={{0,8},{8,0},{16,24},{24,16},{1,9},{9,1},{17,25},{25,17},{2,10},{10... | collective-permute-start | bytes 1572872 | tf_op jit(solution)/shard_map/ppermute | solution.py:163
  94.9 24.9 %slice-start = ((s8[8388608]{0:T(1024)(128)(4,1)}), s8[4194304]{0:T(1024)(128)(4,1)S(1)}, s32[]{:S(2)}) async-start(s8[8388608]{0:T(1024)(128)(4,1)} %bitcast.50), calls=%async_computation | async-start | bytes 8388608
  94.9 18.3 %collective-permute-start.29 = (bf16[128,2048]{1,0:T(8,128)(2,1)S(1)}, bf16[128,2048]{1,0:T(8,128)(2,1)S(1)}, u32[]{:S(2)}, u32[]{:S(2)}) collective-permute-start(bf16[128,2048]{1,0:T(8,128)(2,1)S(1)} %get-tuple-element.78), channel_id=1, source_target_pairs={{0,4},{1,5},{2,6},{3,7},{4,0},{5,1},{6,2},{7,3},{8,12},{9,13},{10,... | collective-permute-start | bytes 1572872 | tf_op jit(solution)/shard_map/ppermute | solution.py:163
  96.0 17.2 %collective-permute-start.30 = (bf16[128,2048]{1,0:T(8,128)(2,1)S(1)}, bf16[128,2048]{1,0:T(8,128)(2,1)S(1)}, u32[]{:S(2)}, u32[]{:S(2)}) collective-permute-start(bf16[128,2048]{1,0:T(8,128)(2,1)S(1)} %get-tuple-element.79), channel_id=1, source_target_pairs={{0,2},{1,3},{2,0},{3,1},{4,6},{5,7},{6,4},{7,5},{8,10},{9,11},{10,... | collective-permute-start | bytes 1572872 | tf_op jit(solution)/shard_map/ppermute | solution.py:163
  97.5 13.9 %collective-permute-start.26 = (bf16[1024,64]{1,0:T(8,128)(2,1)S(1)}, bf16[1024,64]{1,0:T(8,128)(2,1)S(1)}, u32[]{:S(2)}, u32[]{:S(2)}) collective-permute-start(bf16[1024,64]{1,0:T(8,128)(2,1)S(1)} %get-tuple-element.73), channel_id=1, source_target_pairs={{0,16},{8,24},{16,0},{24,8},{1,17},{9,25},{17,1},{25,9},{2,18},{10... | collective-permute-start | bytes 393224 | tf_op jit(solution)/shard_map/ppermute | solution.py:163
  98.7 21.2 %slice-start.1 = ((s8[8388608]{0:T(1024)(128)(4,1)}), s8[4194304]{0:T(1024)(128)(4,1)S(1)}, s32[]{:S(2)}) async-start(s8[8388608]{0:T(1024)(128)(4,1)} %bitcast.50), calls=%async_computation.1 | async-start | bytes 8388608
  113.2 11.9 %collective-permute-start.32 = (bf16[1024,64]{1,0:T(8,128)(2,1)S(1)}, bf16[1024,64]{1,0:T(8,128)(2,1)S(1)}, u32[]{:S(2)}, u32[]{:S(2)}) collective-permute-start(bf16[1024,64]{1,0:T(8,128)(2,1)S(1)} %get-tuple-element.81), channel_id=1, source_target_pairs={{0,8},{8,0},{16,24},{24,16},{1,9},{9,1},{17,25},{25,17},{2,10},{10... | collective-permute-start | bytes 393224 | tf_op jit(solution)/shard_map/ppermute | solution.py:163
  116.1 13.7 %collective-permute-start.31 = (bf16[256,512]{1,0:T(8,128)(2,1)S(1)}, bf16[256,512]{1,0:T(8,128)(2,1)S(1)}, u32[]{:S(2)}, u32[]{:S(2)}) collective-permute-start(bf16[256,512]{1,0:T(8,128)(2,1)S(1)} %select_convert_fusion), channel_id=1, source_target_pairs={{0,16},{8,24},{16,0},{24,8},{1,17},{9,25},{17,1},{25,9},{2,18},{10... | collective-permute-start | bytes 786440 | tf_op jit(solution)/shard_map/ppermute | solution.py:163
  117.6 12.2 %collective-permute-start.33 = (bf16[128,2048]{1,0:T(8,128)(2,1)S(1)}, bf16[128,2048]{1,0:T(8,128)(2,1)S(1)}, u32[]{:S(2)}, u32[]{:S(2)}) collective-permute-start(bf16[128,2048]{1,0:T(8,128)(2,1)S(1)} %get-tuple-element.82), channel_id=1, source_target_pairs={{0,4},{1,5},{2,6},{3,7},{4,0},{5,1},{6,2},{7,3},{8,12},{9,13},{10,... | collective-permute-start | bytes 1572872 | tf_op jit(solution)/shard_map/ppermute | solution.py:163
  118.6 11.8 %collective-permute-start.34 = (bf16[128,2048]{1,0:T(8,128)(2,1)S(1)}, bf16[128,2048]{1,0:T(8,128)(2,1)S(1)}, u32[]{:S(2)}, u32[]{:S(2)}) collective-permute-start(bf16[128,2048]{1,0:T(8,128)(2,1)S(1)} %get-tuple-element.83), channel_id=1, source_target_pairs={{0,2},{1,3},{2,0},{3,1},{4,6},{5,7},{6,4},{7,5},{8,10},{9,11},{10,... | collective-permute-start | bytes 1572872 | tf_op jit(solution)/shard_map/ppermute | solution.py:163
  131.4 2.0 %collective-permute-start.35 = (bf16[4,128,512]{2,1,0:T(8,128)(2,1)S(1)}, bf16[4,128,512]{2,1,0:T(8,128)(2,1)S(1)}, u32[]{:S(2)}, u32[]{:S(2)}) collective-permute-start(bf16[4,128,512]{2,1,0:T(8,128)(2,1)S(1)} %get-tuple-element.85), channel_id=1, source_target_pairs={{0,1},{1,0},{2,3},{3,2},{4,5},{5,4},{6,7},{7,6},{8,9},{9,8},{10,11... | collective-permute-start | bytes 1572872 | tf_op jit(solution)/shard_map/ppermute | solution.py:163
  133.8 9.2 %collective-permute-start.36 = (bf16[256,512]{1,0:T(8,128)(2,1)S(1)}, bf16[256,512]{1,0:T(8,128)(2,1)S(1)}, u32[]{:S(2)}, u32[]{:S(2)}) collective-permute-start(bf16[256,512]{1,0:T(8,128)(2,1)S(1)} %get-tuple-element.87), channel_id=1, source_target_pairs={{0,2},{1,3},{2,0},{3,1},{4,6},{5,7},{6,4},{7,5},{8,10},{9,11},{10,... | collective-permute-start | bytes 786440 | tf_op jit(solution)/shard_map/ppermute | solution.py:163
  135.1 13.7 %collective-permute-start.37 = (bf16[256,512]{1,0:T(8,128)(2,1)S(1)}, bf16[256,512]{1,0:T(8,128)(2,1)S(1)}, u32[]{:S(2)}, u32[]{:S(2)}) collective-permute-start(bf16[256,512]{1,0:T(8,128)(2,1)S(1)} %get-tuple-element.88), channel_id=1, source_target_pairs={{0,4},{1,5},{2,6},{3,7},{4,0},{5,1},{6,2},{7,3},{8,12},{9,13},{10,... | collective-permute-start | bytes 786440 | tf_op jit(solution)/shard_map/ppermute | solution.py:163
  136.4 12.4 %collective-permute-start.38 = (bf16[256,512]{1,0:T(8,128)(2,1)S(1)}, bf16[256,512]{1,0:T(8,128)(2,1)S(1)}, u32[]{:S(2)}, u32[]{:S(2)}) collective-permute-start(bf16[256,512]{1,0:T(8,128)(2,1)S(1)} %get-tuple-element.89), channel_id=1, source_target_pairs={{0,6},{1,7},{2,4},{3,5},{4,2},{5,3},{6,0},{7,1},{8,14},{9,15},{10,... | collective-permute-start | bytes 786440 | tf_op jit(solution)/shard_map/ppermute | solution.py:163

commit v3 on v2

--- a/solution.py
+++ b/solution.py
@@ -163,18 +163,16 @@
     return lax.ppermute(value, axis, [(i, i ^ bits) for i in range(size)])
 
 
-def call(body, name, outs, args, *, grid=(), in_specs=None, out_specs=None, scratch=(), scalars=0, vmem=12, needs=(), passed=None, hint=1):
+def call(body, name, outs, args, *, grid=(), in_specs=None, out_specs=None, scratch=(), scalars=0, vmem=12, needs=(), passed=(), hint=1):
     given = len(args)
-    extra = [*needs] + ([passed] if passed is not None else [])
+    extra = [*needs, *passed]
     in_specs = list(in_specs) if in_specs is not None else [pl.BlockSpec()] * (given - scalars)
     out_specs = list(out_specs) if out_specs is not None else [pl.BlockSpec()] * len(outs)
     anywhere = pl.BlockSpec(memory_space=pl.ANY)
     count = len(outs)
-    aliases = {}
-    if passed is not None:
-        outs = [*outs, shape(passed.shape, passed.dtype)]
-        out_specs.append(anywhere)
-        aliases = {given + len(extra) - 1: count}
+    outs = [*outs, *(shape(p.shape, p.dtype) for p in passed)]
+    out_specs += [anywhere] * len(passed)
+    aliases = {given + len(needs) + i: count + i for i in range(len(passed))}
 
     def run(*refs):
         kept = refs[:given] + refs[given + len(extra) : given + len(extra) + count]
@@ -236,6 +234,7 @@
     row_id = lax.broadcasted_iota(jnp.int32, (rows, capacity), 0).astype(F32)
     upper_lanes = (lax.broadcasted_iota(jnp.int32, (capacity, 2 * rank), 1) >= rank).astype(F32)
     up = up_ref[...].reshape(local * rank, span)
+    parts = []
     for g in range(holders):
         tail = messages[g][rows : rows + 16, :capacity].astype(F32)
         lists, ids = tail[:holders], tail[holders:]
@@ -257,7 +256,9 @@
         for p in range(local // 2):
             wanted = upper_lanes + (2 * p + 1.0)
             total += jnp.where(ids == wanted, wide[:, 2 * rank * p : 2 * rank * (p + 1)], 0.0)
-        part_ref[g] = total[:, :rank] + total[:, rank:]
+        parts.append(total[:, :rank] + total[:, rank:])
+    for g in range(holders // 2):
+        part_ref[g] = jnp.concatenate([parts[g], parts[g + holders // 2]], axis=1)
 
 
 def message_body(local, dy_ref, lists_ref, tenant_ref, out_ref):
@@ -277,16 +278,18 @@
     odd_ref[...] = jnp.full(odd_ref.shape, (place & 1).astype(F32))
 
 
-def low_body(local, count, first, *refs):
+def low_body(local, count, first, starts, *refs):
     own_ref, ids_ref, down_ref, slots_ref, part_ref = refs[-5:]
     pieces = (len(refs) - 5) // count
     rows = own_ref.shape[1] // pieces
     capacity = own_ref.shape[2]
     width = down_ref.shape[2]
     for j in range(count):
-        picked = contract(own_ref[first + j, :rows], refs[pieces * j][...], 0, 0)
-        for i in range(1, pieces):
-            picked += contract(own_ref[first + j, i * rows : (i + 1) * rows], refs[pieces * j + i][...], 0, 0)
+        picked = 0.0
+        for i in range(pieces):
+            at = starts[pieces * j + i]
+            piece = refs[pieces * j + i][at : at + rows, :]
+            picked += contract(own_ref[first + j, i * rows : (i + 1) * rows], piece, 0, 0)
         slots_ref[j * capacity : (j + 1) * capacity, :] = picked.astype(BF16)
     ids = ids_ref[first : first + count].reshape(count * capacity, capacity)
     total = jnp.zeros((count * capacity, width), F32)
@@ -303,30 +306,28 @@
     return jnp.concatenate([jnp.where(ids == a + 1.0, low, 0.0) for a in range(local)], axis=1).astype(BF16)
 
 
-def delta_body(local, low_ref, ids_ref, down_ref, odd_ref, even_ref, wide_ref):
-    slots = low_ref.shape[0]
+def delta_body(local, part, low_ref, ids_ref, down_ref, out_ref, wide_ref):
     holders, capacity, _ = ids_ref.shape
 
     @pl.when(pl.program_id(0) == 0)
     def _():
-        for g in range(holders):
-            at = (g % 2) * (slots // 2) + (g // 2) * capacity
-            wide_ref[pl.ds(at, capacity), :] = spread(
+        for i, g in enumerate(range(part, holders, 2)):
+            wide_ref[i * capacity : (i + 1) * capacity, :] = spread(
                 low_ref[g * capacity : (g + 1) * capacity, :], ids_ref[g], local
             )
 
     weights = jnp.concatenate([down_ref[a] for a in range(local)], axis=1)
-    half = slots // 2
-    for part, out_ref in ((1, odd_ref), (0, even_ref)):
-        out = (adapter_scale * contract(wide_ref[pl.ds(part * half, half), :], weights, 1, 1)).astype(BF16)
-        out_ref[...] = out.reshape(half // capacity, capacity, out.shape[1])
+    out = (adapter_scale * contract(wide_ref[...], weights, 1, 1)).astype(BF16)
+    out_ref[...] = out.reshape(out_ref.shape)
 
 
 def up_body(local, low_ref, ids_ref, up_ref, odd_ref, even_ref, wide_ref):
-    slots, rank = low_ref.shape
+    slots, rank = 2 * low_ref.shape[0], low_ref.shape[1] // 2
     holders, capacity, _ = ids_ref.shape
-    low = low_ref[...].astype(F32)
-    low = jnp.concatenate([low, low], axis=1)
+    packed = low_ref[...].astype(F32)
+    low = jnp.concatenate(
+        [jnp.concatenate([packed[:, i : i + rank]] * 2, axis=1) for i in (0, rank)], axis=0
+    )
     ids = ids_ref[...].reshape(slots, capacity)
     upper_lanes = (lax.broadcasted_iota(jnp.int32, (slots, 2 * rank), 1) >= rank).astype(F32)
     wide = jnp.concatenate(
@@ -396,10 +397,10 @@
     holders, capacity = send_list.shape[1], send_list.shape[2]
     slots = holders * capacity
     fsdp = lax.axis_size("fsdp")
-    upper, odd_place = call(place_body, "place", [shape((8, 128), F32)] * 2, [], vmem=1)
+    upper, odd_place = call(place_body, "place", [shape((1, 1), F32)] * 2, [], vmem=1)
 
     def where(mask, yes, no):
-        mask = jnp.broadcast_to(mask[:1, :1], yes.shape)
+        mask = jnp.broadcast_to(mask, yes.shape)
         return jnp.where(mask > 0.5, yes, no)
     half = rows // 2
     chunk = 512
@@ -408,15 +409,21 @@
         lambda *refs: message_body(local, *refs),
         "message",
         [shape((rows + 16, span))],
-        [cotangent, send_list, tenant.reshape(-1, capacity)],
+        [pltpu.with_memory_space_constraint(a, pltpu.HBM) for a in (cotangent, send_list, tenant.reshape(-1, capacity))],
+        grid=(1,),
+        in_specs=[
+            pl.BlockSpec(cotangent.shape, lambda i: (0, 0)),
+            pl.BlockSpec(send_list.shape, lambda i: (0, 0, 0)),
+            pl.BlockSpec((rows // capacity, capacity), lambda i: (0, 0)),
+        ],
+        out_specs=[pl.BlockSpec((rows + 16, span), lambda i: (0, 0))],
     )
     near = {0: message}
     for bits in (2, 4, 6):
         near[bits] = swap(message, "adapter", bits)
     top, bottom = tokens[:half], tokens[half:]
     base_partial = jnp.dot(tokens, base_weight, preferred_element_type=F32).astype(BF16)
-    far_dy = swap(cotangent, "fsdp", 2)
-    near[2], near[4], near[6], top = tie((near[2], near[4], near[6], top), (base_partial, far_dy))
+    near[2], near[4], near[6], top = tie((near[2], near[4], near[6], top), (base_partial,))
     messages = []
     for bits in ORDER[::2]:
         messages += [near[bits], swap(near[bits], "adapter", 1)]
@@ -428,20 +435,22 @@
             shape((holders, capacity, capacity), F32),
             shape((holders, rows, capacity)),
             shape((holders // 2, rows, capacity)),
-            shape((holders, capacity, rank), F32),
+            shape((holders // 2, capacity, 2 * rank), F32),
         ],
         [*messages, up_weight],
     )
-    back_part = back_part.reshape(slots, rank)
+    back_part = back_part.reshape(slots // 2, 2 * rank)
     flat_ids = ids.reshape(slots, capacity)
 
     def low_rows(first, blocks, needs=()):
         count = len(blocks)
+        pieces = sum(blocks, ())
+        starts = [p[1] * half if isinstance(p, tuple) else 0 for p in pieces]
         return call(
-            lambda *refs: low_body(local, count, first, *refs),
+            lambda *refs: low_body(local, count, first, starts, *refs),
             "low_rows",
             [shape((count * capacity, width)), shape((count * capacity, pair), F32)],
-            [*sum(blocks, ()), own, ids, down_weight],
+            [p[0] if isinstance(p, tuple) else p for p in pieces] + [own, ids, down_weight],
             vmem=16,
             needs=needs,
         )
@@ -457,35 +466,59 @@
     x_a, low_a = low_rows(0, with_mates((tokens,)))
     back_half = (back_part + got1.astype(F32)).astype(BF16)
     (back_half,) = tie((back_half,), (x_top, y_top, low_a))
+    (base_partial,) = tie((base_partial,), (got1,))
 
     back_other = swap(back_half, "fsdp", 2)
     x_bottom, y_bottom = swap(bottom, "adapter", 2), swap(bottom, "adapter", 4)
-    back_low = where(
-        upper,
-        jnp.concatenate([back_other, back_half], axis=1),
-        jnp.concatenate([back_half, back_other], axis=1),
-    )
-    odd, even = call(
-        lambda *refs: delta_body(local, *refs),
-        "back_delta",
-        [shape((holders // 2, capacity, width))] * 2,
-        [back_low, ids, down_weight],
-        grid=(width // chunk,),
-        in_specs=[
-            pl.BlockSpec((slots, pair), lambda i: (0, 0)),
-            pl.BlockSpec((holders, capacity, capacity), lambda i: (0, 0, 0)),
-            pl.BlockSpec((local, chunk, pair), lambda i: (0, i, 0)),
+    top_mates = swap(jnp.concatenate([y_top, x_top], axis=0), "adapter", 1)
+    quarter = [base_partial[:, i * span : (i + 1) * span] for i in range(4)]
+    base_keep = [where(odd_place, quarter[1], quarter[0]), where(odd_place, quarter[3], quarter[2])]
+    base_give = [where(odd_place, quarter[0], quarter[1]), where(odd_place, quarter[2], quarter[3])]
+    base_got = swap(jnp.concatenate(base_give, axis=1), "fsdp", 1)
+    lower_half, upper_half = where(upper, back_other, back_half), where(upper, back_half, back_other)
+    back_low = jnp.concatenate(
+        [
+            jnp.concatenate([lower_half[:, i : i + rank], upper_half[:, i : i + rank]], axis=1)
+            for i in (0, rank)
         ],
-        out_specs=[pl.BlockSpec((holders // 2, capacity, chunk), lambda i: (0, 0, i))] * 2,
-        scratch=[pltpu.VMEM((slots, local * pair), BF16)],
-        vmem=16,
-        needs=(x_bottom, y_bottom),
-        hint=1 << 14,
-    )
+        axis=0,
+    )
+
+    def back_delta(part, needs):
+        (out,) = call(
+            lambda *refs: delta_body(local, part, *refs),
+            "back_delta",
+            [shape((holders // 2, capacity, width))],
+            [back_low, ids, down_weight],
+            grid=(width // chunk,),
+            in_specs=[
+                pl.BlockSpec((slots, pair), lambda i: (0, 0)),
+                pl.BlockSpec((holders, capacity, capacity), lambda i: (0, 0, 0)),
+                pl.BlockSpec((local, chunk, pair), lambda i: (0, i, 0)),
+            ],
+            out_specs=[pl.BlockSpec((holders // 2, capacity, chunk), lambda i: (0, 0, i))],
+            scratch=[pltpu.VMEM((slots // 2, local * pair), BF16)],
+            vmem=16,
+            needs=needs,
+        )
+        return out
+
+    odd = back_delta(1, (x_bottom, y_bottom, top_mates, base_got))
+    even = back_delta(0, (odd,))
 
     got = swap(odd, "adapter", 1)
     diag = (swap(y_top, "adapter", 2), swap(x_bottom, "adapter", 4))
-    x_b, low_b = low_rows(4, with_mates((y_top, y_bottom), (x_top, x_bottom)))
+    far_dy = swap(cotangent, "fsdp", 2)
+    bottom_mates = swap(jnp.concatenate([y_bottom, x_bottom], axis=0), "adapter", 1)
+    x_b, low_b = low_rows(
+        4,
+        [
+            (y_top, y_bottom),
+            ((top_mates, 0), (bottom_mates, 0)),
+            (x_top, x_bottom),
+            ((top_mates, 1), (bottom_mates, 1)),
+        ],
+    )
     diag_low, diag_high = expand(
         "back_diag", 1, 1, ((0, 0, half), (0, half, half)), own, mate, even, got, 1024
     )
@@ -500,25 +533,20 @@
         got,
         1024,
     )
-    *diag, base_partial = tie((*diag, base_partial), (low_b, diag_low, y_low))
+    *diag, far_dy = tie((*diag, far_dy), (low_b, diag_low, y_low))
 
     low_in = swap(diag_low, "adapter", 2)
     high_in = swap(diag_high, "adapter", 4)
-    quarter = [base_partial[:, i * span : (i + 1) * span] for i in range(4)]
-    base_keep = [where(odd_place, quarter[1], quarter[0]), where(odd_place, quarter[3], quarter[2])]
-    base_give = [where(odd_place, quarter[0], quarter[1]), where(odd_place, quarter[2], quarter[3])]
-    base_got = swap(jnp.concatenate(base_give, axis=1), "fsdp", 1)
     x_c, low_c = low_rows(2, with_mates(tuple(diag)))
     low_part = jnp.concatenate([low_a, low_c, low_b], axis=0)
-    keep = where(upper, low_part[:, rank:], low_part[:, :rank])
-    give = where(upper, low_part[:, :rank], low_part[:, rank:]).astype(BF16)
+    halves = [
+        jnp.concatenate([low_part[: slots // 2, i : i + rank], low_part[slots // 2 :, i : i + rank]], axis=1)
+        for i in (0, rank)
+    ]
+    keep, give = where(upper, halves[1], halves[0]), where(upper, halves[0], halves[1]).astype(BF16)
     to_y, to_x = y_low + low_in, x_high + high_in
-    give, y_high, x_low = tie((give, y_high, x_low), (to_y, to_x))
-
     got_low = swap(give, "fsdp", 2)
     next_dy = swap(jnp.stack([cotangent, far_dy]), "fsdp", 1)
-    high_from_y = swap(y_high, "adapter", 4)
-    low_from_x = swap(x_low, "adapter", 2)
     down_grad, made = call(
         lambda *refs: down_grad_body(local, 3, *refs),
         "down_grad",
@@ -532,13 +560,13 @@
         vmem=16,
     )
     low_sum = keep + got_low.astype(F32)
-    low_sent, base_got, to_y, to_x = tie(
-        (low_sum.astype(BF16), base_got, to_y, to_x), (made, next_dy, high_from_y, low_from_x)
+    low_sent, base_got, y_high, x_low = tie(
+        (low_sum.astype(BF16), base_got, y_high, x_low), (to_y, to_x, next_dy)
     )
 
     got2 = swap(low_sent, "fsdp", 1)
-    low_from_y = swap(to_y, "adapter", 4)
-    high_from_x = swap(to_x, "adapter", 2)
+    high_from_y = swap(y_high, "adapter", 4)
+    low_from_x = swap(x_low, "adapter", 2)
     ordered = [
         where(odd_place, b, a) for a, b in ((cotangent, next_dy[0]), (next_dy[0], cotangent))
     ], [where(odd_place, b, a) for a, b in ((far_dy, next_dy[1]), (next_dy[1], far_dy))]
@@ -553,15 +581,17 @@
     base_far = swap(where(upper, base_sum[0], base_sum[1]).astype(BF16), "fsdp", 2)
     base_out = where(upper, base_sum[1], base_sum[0]) + base_far.astype(F32)
     low_half = (low_sum + got2.astype(F32)).astype(BF16)
-    up_odd, up_even, wide_low, input_base = call(
+    up_odd, up_even, wide_low, to_y, to_x, input_base = call(
         lambda *refs: up_body(local, *refs),
         "up_delta",
         [shape((holders // 2, capacity, span))] * 2 + [shape((slots, local * rank))],
         [low_half, ids, up_weight],
-        needs=(home, low_from_y, high_from_x, base_far),
-        passed=input_base,
-    )
-
+        needs=(home, high_from_y, low_from_x, base_far, made),
+        passed=(to_y, to_x, input_base),
+    )
+
+    low_from_y = swap(to_y, "adapter", 4)
+    high_from_x = swap(to_x, "adapter", 2)
     up_got = swap(up_odd, "adapter", 1)
     add_home, add_diag, add_y, add_x = expand(
         "up_rows", 0, 4, tuple((p, 0, rows) for p in range(4)), own, mate, up_even, up_got, 512

time: 150 us -> 140 us (0.933)
  waiting for transfers between devices: 63.9 us -> 57.7 us
  other arithmetic: 6.01 us -> 4.01 us
  local copies, waits for them, and re-layouts: 2.54 us -> 0.54 us
  Pallas kernels: 28.9 us -> 30.4 us
    ppermute x39 -> x37, waiting for transfers between devices: 63.9 us -> 57.7 us  [swap(): return lax.ppermute(value, axis, [(i, i ^ bits) for i in range(size)])]
    pallas_call x13 -> x14, Pallas kernels: 28.9 us -> 30.4 us  [call(): pl.pallas_call(run, grid_spec=spec, out_shape=outs, name=name, input_outp...]
    ppermute x39 -> x37, starting transfers between devices: 36.3 us -> 35.2 us  [swap(): return lax.ppermute(value, axis, [(i, i ^ bits) for i in range(size)])]
  transfers between devices with their start and end apart: 39 -> 37, of which waited for: 19 -> 15; matrix products, arithmetic and copies ran while one was open for 11% -> 9% of each run, Pallas kernels for 13% -> 18%
where the time goes in v3:
time: 140 us
  waiting for transfers between devices  57.7 us (41%)
  starting transfers between devices  35.2 us (25%)
  Pallas kernels  30.4 us (22%)
  matrix products  9.94 us (7%)
  other arithmetic  4.01 us (3%)
  between operations  2.41 us (2%)
    ppermute x37, waiting for transfers between devices, swap(): return lax.ppermute(value, axis, [(i, i ^ bits) for i in range(size)])  57.7 us
    ppermute x37, starting transfers between devices, swap(): return lax.ppermute(value, axis, [(i, i ^ bits) for i in range(size)])  35.2 us
    pallas_call x14, Pallas kernels, call(): pl.pallas_call(run, grid_spec=spec, out_shape=outs, name=name, input_outp...  30.4 us
    dot_general x1, matrix products, shards(): jnp.dot(tokens, base_weight, preferred_element_type=F32).astype(BF16)  6.05 us
    dot_general x2, matrix products, contract(): lax.dot_general(left, right, (((left_dim,), (right_dim,)), ((), ())), pre...  3.89 us
  transfers between devices with their start and end apart: 37, of which 15 were waited for; matrix products, arithmetic and copies ran while one was open for 9% of the time, Pallas kernels for 18%

profile of v3, /device:TPU:0, one launch (start us, length us, event | category | flops | bytes accessed | tf_op | source)
XLA Modules:
  0.0 140.1 jit_solution(10605490321300274965)
XLA Ops:
  0.6 1.0 message.1.refs_0_
  1.6 4.0 %collective-permute-start.3 = (bf16[272,512]{1,0:T(8,128)(2,1)S(1)}, bf16[272,512]{1,0:T(8,128)(2,1)S(1)}, u32[]{:S(2)}, u32[]{:S(2)}) collective-permute-start(bf16[272,512]{1,0:T(8,128)(2,1)S(1)} %message.1.refs_0_), channel_id=1, source_target_pairs={{0,6},{1,7},{2,4},{3,5},{4,2},{5,3},{6,0},{7,1},{8,14},{9,15},{10,... | collective-permute-start | bytes 835592 | tf_op jit(solution)/shard_map/ppermute | solution.py:163
  6.2 6.0 %convolution_convert_fusion.refs_4_.refs_0_ = bf16[256,2048]{1,0:T(8,128)(2,1)S(1)} fusion(bf16[256,2048]{1,0:T(8,128)(2,1)} %refs_0_.3, bf16[2048,2048]{1,0:T(8,128)(2,1)} %param.10), kind=kOutput, calls=%fused_computation | convolution fusion | flops 2148007936 | bytes 10485760 | tf_op jit(solution)/shard_map/dot_general | solution.py:425
  12.4 0.7 collective-permute-done.3.refs_2_
  13.1 5.1 %collective-permute-done.2.refs_1_ = bf16[272,512]{1,0:T(8,128)(2,1)S(1)} collective-permute-done((bf16[272,512]{1,0:T(8,128)(2,1)S(1)}, bf16[272,512]{1,0:T(8,128)(2,1)S(1)}, u32[]{:S(2)}, u32[]{:S(2)}) %collective-permute-start.2) | collective-permute-done | bytes 278560 | tf_op jit(solution)/shard_map/ppermute | solution.py:163
  19.0 1.5 %collective-permute-start.15 = (bf16[128,2048]{1,0:T(8,128)(2,1)S(1)}, bf16[128,2048]{1,0:T(8,128)(2,1)S(1)}, u32[]{:S(2)}, u32[]{:S(2)}) collective-permute-start(bf16[128,2048]{1,0:T(8,128)(2,1)S(1)} %get-tuple-element.55), channel_id=1, source_target_pairs={{0,2},{1,3},{2,0},{3,1},{4,6},{5,7},{6,4},{7,5},{8,10},{9,11},{10,... | collective-permute-start | bytes 1572872 | tf_op jit(solution)/shard_map/ppermute | solution.py:163
  23.5 1.5 %collective-permute-start.14 = (bf16[128,2048]{1,0:T(8,128)(2,1)S(1)}, bf16[128,2048]{1,0:T(8,128)(2,1)S(1)}, u32[]{:S(2)}, u32[]{:S(2)}) collective-permute-start(bf16[128,2048]{1,0:T(8,128)(2,1)S(1)} %get-tuple-element.98), channel_id=1, source_target_pairs={{0,4},{1,5},{2,6},{3,7},{4,0},{5,1},{6,2},{7,3},{8,12},{9,13},{10,... | collective-permute-start | bytes 1572872 | tf_op jit(solution)/shard_map/ppermute | solution.py:163
  25.5 2.6 %back_rows.1 = (bf16[8,128,512]{2,1,0:T(8,128)(2,1)S(1)}, f32[8,128,128]{2,1,0:T(8,128)S(1)}, bf16[8,256,128]{2,1,0:T(8,128)(2,1)S(1)}, bf16[4,256,128]{2,1,0:T(8,128)(2,1)S(1)}, f32[4,128,128]{2,1,0:T(8,128)S(1)}) custom-call(bf16[272,512]{1,0:T(8,128)(2,1)S(1)} %message.1.refs_0_, bf16[272,512]{1,0:T(8,128)(2,1)S(1)} %collective-permute-done.refs_1_, ...), custom_call_target="tpu_custom_call" | custom-call | flops 1024 | bytes 1024 | tf_op jit(solution)/shard_map/back_rows/pallas_call | solution.py:188
  28.2 5.7 %collective-permute-done.15.refs_4_.refs_1_ = bf16[128,2048]{1,0:T(8,128)(2,1)S(1)} collective-permute-done((bf16[128,2048]{1,0:T(8,128)(2,1)S(1)}, bf16[128,2048]{1,0:T(8,128)(2,1)S(1)}, u32[]{:S(2)}, u32[]{:S(2)}) %collective-permute-start.15) | collective-permute-done | bytes 524320 | tf_op jit(solution)/shard_map/ppermute | solution.py:163
  33.8 1.6 %collective-permute-start.7 = (bf16[512,128]{1,0:T(8,128)(2,1)S(1)}, bf16[512,128]{1,0:T(8,128)(2,1)S(1)}, u32[]{:S(2)}, u32[]{:S(2)}) collective-permute-start(bf16[512,128]{1,0:T(8,128)(2,1)S(1)} %bitcast_convert_fusion), channel_id=1, source_target_pairs={{0,8},{8,0},{16,24},{24,16},{1,9},{9,1},{17,25},{25,17},{2,10},{10... | collective-permute-start | bytes 393224 | tf_op jit(solution)/shard_map/ppermute | solution.py:163
  35.6 3.2 %collective-permute-done.7.refs_1_ = bf16[512,128]{1,0:T(8,128)(2,1)S(1)} collective-permute-done((bf16[512,128]{1,0:T(8,128)(2,1)S(1)}, bf16[512,128]{1,0:T(8,128)(2,1)S(1)}, u32[]{:S(2)}, u32[]{:S(2)}) %collective-permute-start.7) | collective-permute-done | bytes 131104 | tf_op jit(solution)/shard_map/ppermute | solution.py:163
  38.9 1.6 %low_rows.3 = (bf16[256,2048]{1,0:T(8,128)(2,1)S(1)}, f32[256,128]{1,0:T(8,128)S(1)}) custom-call(bf16[256,2048]{1,0:T(8,128)(2,1)S(1)} %copy-done.1, bf16[256,2048]{1,0:T(8,128)(2,1)S(1)} %collective-permute-done.8.refs_1_, bf16[8,256,128]{2,1,0:T(8,128)(2,1)S(1)} %get-tuple-element.52.refs_2_.refs_8_.refs_0_.refs_4_, ...), custom_call_target="tpu_custom_call" | custom-call | flops 1024 | bytes 1024 | tf_op jit(solution)/shard_map/low_rows/pallas_call | solution.py:188
  40.4 2.7 %collective-permute-start.18 = (bf16[512,128]{1,0:T(8,128)(2,1)S(1)}, bf16[512,128]{1,0:T(8,128)(2,1)S(1)}, u32[]{:S(2)}, u32[]{:S(2)}) collective-permute-start(bf16[512,128]{1,0:T(8,128)(2,1)S(1)} %tie.7), channel_id=1, source_target_pairs={{0,16},{8,24},{16,0},{24,8},{1,17},{9,25},{17,1},{25,9},{2,18},{10... | collective-permute-start | bytes 393224 | tf_op jit(solution)/shard_map/ppermute | solution.py:163
  43.2 1.6 %collective-permute-start.19 = (bf16[256,1024]{1,0:T(8,128)(2,1)S(1)}, bf16[256,1024]{1,0:T(8,128)(2,1)S(1)}, u32[]{:S(2)}, u32[]{:S(2)}) collective-permute-start(bf16[256,1024]{1,0:T(8,128)(2,1)S(1)} %pad_maximum_fusion.2), channel_id=1, source_target_pairs={{0,8},{8,0},{16,24},{24,16},{1,9},{9,1},{17,25},{25,17},{2,10},{10... | collective-permute-start | bytes 1572872 | tf_op jit(solution)/shard_map/ppermute | solution.py:163
  44.8 2.2 %collective-permute-done.18 = bf16[512,128]{1,0:T(8,128)(2,1)S(1)} collective-permute-done((bf16[512,128]{1,0:T(8,128)(2,1)S(1)}, bf16[512,128]{1,0:T(8,128)(2,1)S(1)}, u32[]{:S(2)}, u32[]{:S(2)}) %collective-permute-start.18) | collective-permute-done | bytes 131104 | tf_op jit(solution)/shard_map/ppermute | solution.py:163
  47.4 8.5 %collective-permute-done.19.refs_6_.refs_1_ = bf16[256,1024]{1,0:T(8,128)(2,1)S(1)} collective-permute-done((bf16[256,1024]{1,0:T(8,128)(2,1)S(1)}, bf16[256,1024]{1,0:T(8,128)(2,1)S(1)}, u32[]{:S(2)}, u32[]{:S(2)}) %collective-permute-start.19) | collective-permute-done | bytes 524320 | tf_op jit(solution)/shard_map/ppermute | solution.py:163
  55.8 3.6 %back_delta.2.refs_3_ = bf16[4,128,2048]{2,1,0:T(8,128)(2,1)S(1)} custom-call(bf16[1024,128]{1,0:T(8,128)(2,1)S(1)} %maximum_maximum_fusion.refs_0_.refs_3_, f32[8,128,128]{2,1,0:T(8,128)S(1)} %get-tuple-element.53.refs_3_.refs_9_.refs_1_.refs_5_, bf16[8,2048,128]{2,1,0:T(8,128)(2,1)S(1)} %copy-done, ...), custom_call_target="tpu_custom_call" | custom-call | flops 1024 | bytes 1024 | tf_op jit(solution)/shard_map/back_delta/pallas_call | solution.py:188
  60.2 1.6 %collective-permute-start.12 = (bf16[128,2048]{1,0:T(8,128)(2,1)S(1)}, bf16[128,2048]{1,0:T(8,128)(2,1)S(1)}, u32[]{:S(2)}, u32[]{:S(2)}) collective-permute-start(bf16[128,2048]{1,0:T(8,128)(2,1)S(1)} %collective-permute-done.11.refs_5_.refs_3_), channel_id=1, source_target_pairs={{0,4},{1,5},{2,6},{3,7},{4,0},{5,1},{6,2},{7,3},{8,12},{9,13},{10,... | collective-permute-start | bytes 1572872 | tf_op jit(solution)/shard_map/ppermute | solution.py:163
  61.8 0.7 collective-permute-start.10
  62.5 1.2 collective-permute-start.13
  63.7 3.6 %back_delta.3.refs_2_ = bf16[4,128,2048]{2,1,0:T(8,128)(2,1)S(1)} custom-call(bf16[1024,128]{1,0:T(8,128)(2,1)S(1)} %maximum_maximum_fusion.refs_0_.refs_3_, f32[8,128,128]{2,1,0:T(8,128)S(1)} %get-tuple-element.53.refs_3_.refs_9_.refs_1_.refs_5_, bf16[8,2048,128]{2,1,0:T(8,128)(2,1)S(1)} %copy-done, bf16[4,128,2048]{2,1,0:T(8,128)(2,1)S(1)} %back_delta.2.refs_3_), custom_call_target="tpu_custom_call" | custom-call | flops 1024 | bytes 1024 | tf_op jit(solution)/shard_map/back_delta/pallas_call | solution.py:188
  67.3 3.4 %low_rows.4 = (bf16[512,2048]{1,0:T(8,128)(2,1)S(1)}, f32[512,128]{1,0:T(8,128)S(1)}) custom-call(bf16[128,2048]{1,0:T(8,128)(2,1)S(1)} %collective-permute-done.9.refs_0_.refs_2_, bf16[128,2048]{1,0:T(8,128)(2,1)S(1)} %collective-permute-done.14.refs_1_.refs_4_, bf16[256,2048]{1,0:T(8,128)(2,1)S(1)} %collective-permute-done.16.refs_2_.refs_6_.refs_5_, ...), custom_call_target="tpu_custom_call" | custom-call | flops 1024 | bytes 1024 | tf_op jit(solution)/shard_map/low_rows/pallas_call | solution.py:188
  70.8 0.8 back_diag.1
  71.6 1.2 back_near.1
  72.8 4.0 %collective-permute-done.13.refs_2_ = bf16[256,512]{1,0:T(8,128)(2,1)S(1)} collective-permute-done((bf16[256,512]{1,0:T(8,128)(2,1)S(1)}, bf16[256,512]{1,0:T(8,128)(2,1)S(1)}, u32[]{:S(2)}, u32[]{:S(2)}) %collective-permute-start.13) | collective-permute-done | bytes 262176 | tf_op jit(solution)/shard_map/ppermute | solution.py:163
  77.6 1.3 collective-permute-start.24
  79.5 0.8 back_home.1.refs_3_
  80.3 1.8 %low_rows.5 = (bf16[256,2048]{1,0:T(8,128)(2,1)S(1)}, f32[256,128]{1,0:T(8,128)S(1)}) custom-call(bf16[128,2048]{1,0:T(8,128)(2,1)S(1)} %get-tuple-element.60.refs_0_, bf16[128,2048]{1,0:T(8,128)(2,1)S(1)} %get-tuple-element.61.refs_1_, bf16[128,2048]{1,0:T(8,128)(2,1)S(1)} %collective-permute-done.21.refs_2_, ...), custom_call_target="tpu_custom_call" | custom-call | flops 1024 | bytes 1024 | tf_op jit(solution)/shard_map/low_rows/pallas_call | solution.py:188
  82.5 2.6 %collective-permute-start.23 = (bf16[512,128]{1,0:T(8,128)(2,1)S(1)}, bf16[512,128]{1,0:T(8,128)(2,1)S(1)}, u32[]{:S(2)}, u32[]{:S(2)}) collective-permute-start(bf16[512,128]{1,0:T(8,128)(2,1)S(1)} %select_convert_fusion.1), channel_id=1, source_target_pairs={{0,16},{8,24},{16,0},{24,8},{1,17},{9,25},{17,1},{25,9},{2,18},{10... | collective-permute-start | bytes 393224 | tf_op jit(solution)/shard_map/ppermute | solution.py:163
  85.1 9.1 %collective-permute-done.26.refs_6_ = bf16[2,256,512]{2,1,0:T(8,128)(2,1)S(1)} collective-permute-done((bf16[2,256,512]{2,1,0:T(8,128)(2,1)S(1)}, bf16[2,256,512]{2,1,0:T(8,128)(2,1)S(1)}, u32[]{:S(2)}, u32[]{:S(2)}) %collective-permute-start.26) | collective-permute-done | bytes 524320 | tf_op jit(solution)/shard_map/ppermute | solution.py:163
  95.6 2.2 %collective-permute-start.27 = (bf16[256,512]{1,0:T(8,128)(2,1)S(1)}, bf16[256,512]{1,0:T(8,128)(2,1)S(1)}, u32[]{:S(2)}, u32[]{:S(2)}) collective-permute-start(bf16[256,512]{1,0:T(8,128)(2,1)S(1)} %select_convert_fusion), channel_id=1, source_target_pairs={{0,16},{8,24},{16,0},{24,8},{1,17},{9,25},{17,1},{25,9},{2,18},{10... | collective-permute-start | bytes 786440 | tf_op jit(solution)/shard_map/ppermute | solution.py:163
  97.8 1.2 collective-permute-start.29
  99.5 2.4 %fusion.1.refs_10_ = f32[256,2048]{1,0:T(8,128)S(1)} fusion(bf16[2048,2048]{1,0:T(8,128)(2,1)S(1)} %bitcast.52, bf16[256,512]{1,0:T(8,128)(2,1)S(1)} %get-tuple-element.95, bf16[256,512]{1,0:T(8,128)(2,1)S(1)} %get-tuple-element.94, bf16[256,512]{1,0:T(8,128)(2,1)S(1)} %get-tuple-element.93, bf16[256,512]{1,0:T(8,128)(2,1)S(1)} %get-tuple-element.92), kind=kOutput, calls=%fused_computation.6 | convolution fusion | flops 2151677952 | bytes 11534336 | tf_op jit(solution)/shard_map/dot_general | solution.py:156
  101.9 8.0 %down_grad.1 = (bf16[8,2048,128]{2,1,0:T(8,128)(2,1)}, f32[8,128]{1,0:T(8,128)S(1)}) custom-call(bf16[256,2048]{1,0:T(8,128)(2,1)S(1)} %get-tuple-element.72.refs_0_, bf16[256,2048]{1,0:T(8,128)(2,1)S(1)} %get-tuple-element.73.refs_1_, bf16[512,2048]{1,0:T(8,128)(2,1)S(1)} %get-tuple-element.74.refs_2_, ...), custom_call_target="tpu_custom_call" | custom-call | flops 1024 | bytes 1024 | tf_op jit(solution)/shard_map/down_grad/pallas_call | solution.py:188
  110.3 0.9 collective-permute-done.30.refs_5_
  111.2 1.0 up_delta.1
  112.3 0.9 collective-permute-start.35
  113.2 1.2 collective-permute-start.36
  114.4 1.5 %fusion = bf16[512,512]{1,0:T(8,128)(2,1)} fusion(bf16[1024,512]{1,0:T(8,128)(2,1)S(1)} %get-tuple-element.86, bf16[1024,512]{1,0:T(8,128)(2,1)S(1)} %bitcast.48), kind=kOutput, calls=%fused_computation.3 | convolution fusion | flops 537395200 | bytes 2621440 | tf_op jit(solution)/shard_map/dot_general | solution.py:156
  116.4 0.8 collective-permute-start.32
  117.3 1.2 collective-permute-start.33
  118.4 1.5 %collective-permute-start.34 = (bf16[256,512]{1,0:T(8,128)(2,1)S(1)}, bf16[256,512]{1,0:T(8,128)(2,1)S(1)}, u32[]{:S(2)}, u32[]{:S(2)}) collective-permute-start(bf16[256,512]{1,0:T(8,128)(2,1)S(1)} %get-tuple-element.81), channel_id=1, source_target_pairs={{0,6},{1,7},{2,4},{3,5},{4,2},{5,3},{6,0},{7,1},{8,14},{9,15},{10,... | collective-permute-start | bytes 786440 | tf_op jit(solution)/shard_map/ppermute | solution.py:163
  120.0 7.1 %collective-permute-done.35 = bf16[128,2048]{1,0:T(8,128)(2,1)S(1)} collective-permute-done((bf16[128,2048]{1,0:T(8,128)(2,1)S(1)}, bf16[128,2048]{1,0:T(8,128)(2,1)S(1)}, u32[]{:S(2)}, u32[]{:S(2)}) %collective-permute-start.35) | collective-permute-done | bytes 524320 | tf_op jit(solution)/shard_map/ppermute | solution.py:163
  127.1 0.9 collective-permute-done.36
  128.2 1.3 add_convert_fusion
  129.4 4.2 %collective-permute-done.32 = bf16[256,512]{1,0:T(8,128)(2,1)S(1)} collective-permute-done((bf16[256,512]{1,0:T(8,128)(2,1)S(1)}, bf16[256,512]{1,0:T(8,128)(2,1)S(1)}, u32[]{:S(2)}, u32[]{:S(2)}) %collective-permute-start.32) | collective-permute-done | bytes 262176 | tf_op jit(solution)/shard_map/ppermute | solution.py:163
  133.6 5.4 %collective-permute-done.34 = bf16[256,512]{1,0:T(8,128)(2,1)S(1)} collective-permute-done((bf16[256,512]{1,0:T(8,128)(2,1)S(1)}, bf16[256,512]{1,0:T(8,128)(2,1)S(1)}, u32[]{:S(2)}, u32[]{:S(2)}) %collective-permute-start.34) | collective-permute-done | bytes 262176 | tf_op jit(solution)/shard_map/ppermute | solution.py:163
  139.0 1.1 add_convert_fusion.1
  (86 shorter events, 9.7 us)
Async XLA Ops:
  1.6 10.7 %copy-start.1 = (bf16[256,2048]{1,0:T(8,128)(2,1)S(1)}, bf16[256,2048]{1,0:T(8,128)(2,1)}, u32[]{:S(2)}) copy-start(bf16[256,2048]{1,0:T(8,128)(2,1)} %refs_0_.3) | copy-start | bytes 3145732
  1.6 11.5 %collective-permute-start.3 = (bf16[272,512]{1,0:T(8,128)(2,1)S(1)}, bf16[272,512]{1,0:T(8,128)(2,1)S(1)}, u32[]{:S(2)}, u32[]{:S(2)}) collective-permute-start(bf16[272,512]{1,0:T(8,128)(2,1)S(1)} %message.1.refs_0_), channel_id=1, source_target_pairs={{0,6},{1,7},{2,4},{3,5},{4,2},{5,3},{6,0},{7,1},{8,14},{9,15},{10,... | collective-permute-start | bytes 835592 | tf_op jit(solution)/shard_map/ppermute | solution.py:163
  5.6 12.6 %collective-permute-start.2 = (bf16[272,512]{1,0:T(8,128)(2,1)S(1)}, bf16[272,512]{1,0:T(8,128)(2,1)S(1)}, u32[]{:S(2)}, u32[]{:S(2)}) collective-permute-start(bf16[272,512]{1,0:T(8,128)(2,1)S(1)} %message.1.refs_0_), channel_id=1, source_target_pairs={{0,4},{1,5},{2,6},{3,7},{4,0},{5,1},{6,2},{7,3},{8,12},{9,13},{10,... | collective-permute-start | bytes 835592 | tf_op jit(solution)/shard_map/ppermute | solution.py:163
  6.1 12.4 %collective-permute-start.1 = (bf16[272,512]{1,0:T(8,128)(2,1)S(1)}, bf16[272,512]{1,0:T(8,128)(2,1)S(1)}, u32[]{:S(2)}, u32[]{:S(2)}) collective-permute-start(bf16[272,512]{1,0:T(8,128)(2,1)S(1)} %message.1.refs_0_), channel_id=1, source_target_pairs={{0,2},{1,3},{2,0},{3,1},{4,6},{5,7},{6,4},{7,5},{8,10},{9,11},{10,... | collective-permute-start | bytes 835592 | tf_op jit(solution)/shard_map/ppermute | solution.py:163
  6.2 14.9 %collective-permute-start = (bf16[272,512]{1,0:T(8,128)(2,1)S(1)}, bf16[272,512]{1,0:T(8,128)(2,1)S(1)}, u32[]{:S(2)}, u32[]{:S(2)}) collective-permute-start(bf16[272,512]{1,0:T(8,128)(2,1)S(1)} %message.1.refs_0_), channel_id=1, source_target_pairs={{0,1},{1,0},{2,3},{3,2},{4,5},{5,4},{6,7},{7,6},{8,9},{9,8},{10,11... | collective-permute-start | bytes 835592 | tf_op jit(solution)/shard_map/ppermute | solution.py:163
  12.3 13.2 %copy-start.2 = (bf16[8,64,512]{2,1,0:T(8,128)(2,1)S(1)}, bf16[8,64,512]{2,1,0:T(8,128)(2,1)}, u32[]{:S(2)}) copy-start(bf16[8,64,512]{2,1,0:T(8,128)(2,1)} %refs_2_.5) | copy-start | bytes 1572868
  18.5 2.6 %collective-permute-start.4 = (bf16[272,512]{1,0:T(8,128)(2,1)S(1)}, bf16[272,512]{1,0:T(8,128)(2,1)S(1)}, u32[]{:S(2)}, u32[]{:S(2)}) collective-permute-start(bf16[272,512]{1,0:T(8,128)(2,1)S(1)} %get-tuple-element.48.refs_2_), channel_id=1, source_target_pairs={{0,1},{1,0},{2,3},{3,2},{4,5},{5,4},{6,7},{7,6},{8,9},{9,8},{10,11... | collective-permute-start | bytes 835592 | tf_op jit(solution)/shard_map/ppermute | solution.py:163
  18.5 20.3 %collective-permute-start.8 = (bf16[256,2048]{1,0:T(8,128)(2,1)S(1)}, bf16[256,2048]{1,0:T(8,128)(2,1)S(1)}, u32[]{:S(2)}, u32[]{:S(2)}) collective-permute-start(bf16[256,2048]{1,0:T(8,128)(2,1)S(1)} %copy-done.1), channel_id=1, source_target_pairs={{0,1},{1,0},{2,3},{3,2},{4,5},{5,4},{6,7},{7,6},{8,9},{9,8},{10,11... | collective-permute-start | bytes 3145736 | tf_op jit(solution)/shard_map/ppermute | solution.py:163
  19.0 14.8 %collective-permute-start.15 = (bf16[128,2048]{1,0:T(8,128)(2,1)S(1)}, bf16[128,2048]{1,0:T(8,128)(2,1)S(1)}, u32[]{:S(2)}, u32[]{:S(2)}) collective-permute-start(bf16[128,2048]{1,0:T(8,128)(2,1)S(1)} %get-tuple-element.55), channel_id=1, source_target_pairs={{0,2},{1,3},{2,0},{3,1},{4,6},{5,7},{6,4},{7,5},{8,10},{9,11},{10,... | collective-permute-start | bytes 1572872 | tf_op jit(solution)/shard_map/ppermute | solution.py:163
  20.5 14.9 %collective-permute-start.9 = (bf16[128,2048]{1,0:T(8,128)(2,1)S(1)}, bf16[128,2048]{1,0:T(8,128)(2,1)S(1)}, u32[]{:S(2)}, u32[]{:S(2)}) collective-permute-start(bf16[128,2048]{1,0:T(8,128)(2,1)S(1)} %get-tuple-element.55), channel_id=1, source_target_pairs={{0,4},{1,5},{2,6},{3,7},{4,0},{5,1},{6,2},{7,3},{8,12},{9,13},{10,... | collective-permute-start | bytes 1572872 | tf_op jit(solution)/shard_map/ppermute | solution.py:163
  21.1 2.3 %collective-permute-start.5 = (bf16[272,512]{1,0:T(8,128)(2,1)S(1)}, bf16[272,512]{1,0:T(8,128)(2,1)S(1)}, u32[]{:S(2)}, u32[]{:S(2)}) collective-permute-start(bf16[272,512]{1,0:T(8,128)(2,1)S(1)} %get-tuple-element.49.refs_4_), channel_id=1, source_target_pairs={{0,1},{1,0},{2,3},{3,2},{4,5},{5,4},{6,7},{7,6},{8,9},{9,8},{10,11... | collective-permute-start | bytes 835592 | tf_op jit(solution)/shard_map/ppermute | solution.py:163
  21.1 3.8 %collective-permute-start.6 = (bf16[272,512]{1,0:T(8,128)(2,1)S(1)}, bf16[272,512]{1,0:T(8,128)(2,1)S(1)}, u32[]{:S(2)}, u32[]{:S(2)}) collective-permute-start(bf16[272,512]{1,0:T(8,128)(2,1)S(1)} %get-tuple-element.50.refs_6_), channel_id=1, source_target_pairs={{0,1},{1,0},{2,3},{3,2},{4,5},{5,4},{6,7},{7,6},{8,9},{9,8},{10,11... | collective-permute-start | bytes 835592 | tf_op jit(solution)/shard_map/ppermute | solution.py:163
  23.5 23.9 %collective-permute-start.14 = (bf16[128,2048]{1,0:T(8,128)(2,1)S(1)}, bf16[128,2048]{1,0:T(8,128)(2,1)S(1)}, u32[]{:S(2)}, u32[]{:S(2)}) collective-permute-start(bf16[128,2048]{1,0:T(8,128)(2,1)S(1)} %get-tuple-element.98), channel_id=1, source_target_pairs={{0,4},{1,5},{2,6},{3,7},{4,0},{5,1},{6,2},{7,3},{8,12},{9,13},{10,... | collective-permute-start | bytes 1572872 | tf_op jit(solution)/shard_map/ppermute | solution.py:163
  25.0 22.4 %collective-permute-start.11 = (bf16[128,2048]{1,0:T(8,128)(2,1)S(1)}, bf16[128,2048]{1,0:T(8,128)(2,1)S(1)}, u32[]{:S(2)}, u32[]{:S(2)}) collective-permute-start(bf16[128,2048]{1,0:T(8,128)(2,1)S(1)} %get-tuple-element.98), channel_id=1, source_target_pairs={{0,2},{1,3},{2,0},{3,1},{4,6},{5,7},{6,4},{7,5},{8,10},{9,11},{10,... | collective-permute-start | bytes 1572872 | tf_op jit(solution)/shard_map/ppermute | solution.py:163
  28.1 10.7 %copy-start = (bf16[8,2048,128]{2,1,0:T(8,128)(2,1)S(1)}, bf16[8,2048,128]{2,1,0:T(8,128)(2,1)}, u32[]{:S(2)}) copy-start(bf16[8,2048,128]{2,1,0:T(8,128)(2,1)} %refs_6_.1) | copy-start | bytes 12582916
  33.8 5.0 %collective-permute-start.7 = (bf16[512,128]{1,0:T(8,128)(2,1)S(1)}, bf16[512,128]{1,0:T(8,128)(2,1)S(1)}, u32[]{:S(2)}, u32[]{:S(2)}) collective-permute-start(bf16[512,128]{1,0:T(8,128)(2,1)S(1)} %bitcast_convert_fusion), channel_id=1, source_target_pairs={{0,8},{8,0},{16,24},{24,16},{1,9},{9,1},{17,25},{25,17},{2,10},{10... | collective-permute-start | bytes 393224 | tf_op jit(solution)/shard_map/ppermute | solution.py:163
  35.5 20.4 %collective-permute-start.16 = (bf16[256,2048]{1,0:T(8,128)(2,1)S(1)}, bf16[256,2048]{1,0:T(8,128)(2,1)S(1)}, u32[]{:S(2)}, u32[]{:S(2)}) collective-permute-start(bf16[256,2048]{1,0:T(8,128)(2,1)S(1)} %pad_maximum_fusion), channel_id=1, source_target_pairs={{0,1},{1,0},{2,3},{3,2},{4,5},{5,4},{6,7},{7,6},{8,9},{9,8},{10,11... | collective-permute-start | bytes 3145736 | tf_op jit(solution)/shard_map/ppermute | solution.py:163
  40.4 6.6 %collective-permute-start.18 = (bf16[512,128]{1,0:T(8,128)(2,1)S(1)}, bf16[512,128]{1,0:T(8,128)(2,1)S(1)}, u32[]{:S(2)}, u32[]{:S(2)}) collective-permute-start(bf16[512,128]{1,0:T(8,128)(2,1)S(1)} %tie.7), channel_id=1, source_target_pairs={{0,16},{8,24},{16,0},{24,8},{1,17},{9,25},{17,1},{25,9},{2,18},{10... | collective-permute-start | bytes 393224 | tf_op jit(solution)/shard_map/ppermute | solution.py:163
  43.2 12.6 %collective-permute-start.19 = (bf16[256,1024]{1,0:T(8,128)(2,1)S(1)}, bf16[256,1024]{1,0:T(8,128)(2,1)S(1)}, u32[]{:S(2)}, u32[]{:S(2)}) collective-permute-start(bf16[256,1024]{1,0:T(8,128)(2,1)S(1)} %pad_maximum_fusion.2), channel_id=1, source_target_pairs={{0,8},{8,0},{16,24},{24,16},{1,9},{9,1},{17,25},{25,17},{2,10},{10... | collective-permute-start | bytes 1572872 | tf_op jit(solution)/shard_map/ppermute | solution.py:163
  59.5 3.1 %copy-start.3 = (bf16[256,512]{1,0:T(8,128)(2,1)S(1)}, bf16[256,512]{1,0:T(8,128)(2,1)}, u32[]{:S(2)}) copy-start(bf16[256,512]{1,0:T(8,128)(2,1)} %refs_0_.2) | copy-start | bytes 786436
  59.5 11.3 %collective-permute-start.20 = (bf16[4,128,2048]{2,1,0:T(8,128)(2,1)S(1)}, bf16[4,128,2048]{2,1,0:T(8,128)(2,1)S(1)}, u32[]{:S(2)}, u32[]{:S(2)}) collective-permute-start(bf16[4,128,2048]{2,1,0:T(8,128)(2,1)S(1)} %back_delta.2.refs_3_), channel_id=1, source_target_pairs={{0,1},{1,0},{2,3},{3,2},{4,5},{5,4},{6,7},{7,6},{8,9},{9,8},{10,11... | collective-permute-start | bytes 6291464 | tf_op jit(solution)/shard_map/ppermute | solution.py:163
  59.7 7.7 %collective-permute-start.17 = (bf16[256,2048]{1,0:T(8,128)(2,1)S(1)}, bf16[256,2048]{1,0:T(8,128)(2,1)S(1)}, u32[]{:S(2)}, u32[]{:S(2)}) collective-permute-start(bf16[256,2048]{1,0:T(8,128)(2,1)S(1)} %pad_maximum_fusion.1), channel_id=1, source_target_pairs={{0,1},{1,0},{2,3},{3,2},{4,5},{5,4},{6,7},{7,6},{8,9},{9,8},{10,11... | collective-permute-start | bytes 3145736 | tf_op jit(solution)/shard_map/ppermute | solution.py:163
  60.2 16.6 %collective-permute-start.12 = (bf16[128,2048]{1,0:T(8,128)(2,1)S(1)}, bf16[128,2048]{1,0:T(8,128)(2,1)S(1)}, u32[]{:S(2)}, u32[]{:S(2)}) collective-permute-start(bf16[128,2048]{1,0:T(8,128)(2,1)S(1)} %collective-permute-done.11.refs_5_.refs_3_), channel_id=1, source_target_pairs={{0,4},{1,5},{2,6},{3,7},{4,0},{5,1},{6,2},{7,3},{8,12},{9,13},{10,... | collective-permute-start | bytes 1572872 | tf_op jit(solution)/shard_map/ppermute | solution.py:163
  61.8 15.0 %collective-permute-start.10 = (bf16[128,2048]{1,0:T(8,128)(2,1)S(1)}, bf16[128,2048]{1,0:T(8,128)(2,1)S(1)}, u32[]{:S(2)}, u32[]{:S(2)}) collective-permute-start(bf16[128,2048]{1,0:T(8,128)(2,1)S(1)} %collective-permute-done.9.refs_0_.refs_2_), channel_id=1, source_target_pairs={{0,2},{1,3},{2,0},{3,1},{4,6},{5,7},{6,4},{7,5},{8,10},{9,11},{10,... | collective-permute-start | bytes 1572872 | tf_op jit(solution)/shard_map/ppermute | solution.py:163
  62.5 14.2 %collective-permute-start.13 = (bf16[256,512]{1,0:T(8,128)(2,1)S(1)}, bf16[256,512]{1,0:T(8,128)(2,1)S(1)}, u32[]{:S(2)}, u32[]{:S(2)}) collective-permute-start(bf16[256,512]{1,0:T(8,128)(2,1)S(1)} %copy-done.3), channel_id=1, source_target_pairs={{0,16},{8,24},{16,0},{24,8},{1,17},{9,25},{17,1},{25,9},{2,18},{10... | collective-permute-start | bytes 786440 | tf_op jit(solution)/shard_map/ppermute | solution.py:163
  76.8 3.5 %collective-permute-start.21 = (bf16[128,2048]{1,0:T(8,128)(2,1)S(1)}, bf16[128,2048]{1,0:T(8,128)(2,1)S(1)}, u32[]{:S(2)}, u32[]{:S(2)}) collective-permute-start(bf16[128,2048]{1,0:T(8,128)(2,1)S(1)} %get-tuple-element.60.refs_0_), channel_id=1, source_target_pairs={{0,1},{1,0},{2,3},{3,2},{4,5},{5,4},{6,7},{7,6},{8,9},{9,8},{10,11... | collective-permute-start | bytes 1572872 | tf_op jit(solution)/shard_map/ppermute | solution.py:163
  76.9 3.4 %collective-permute-start.22 = (bf16[128,2048]{1,0:T(8,128)(2,1)S(1)}, bf16[128,2048]{1,0:T(8,128)(2,1)S(1)}, u32[]{:S(2)}, u32[]{:S(2)}) collective-permute-start(bf16[128,2048]{1,0:T(8,128)(2,1)S(1)} %get-tuple-element.61.refs_1_), channel_id=1, source_target_pairs={{0,1},{1,0},{2,3},{3,2},{4,5},{5,4},{6,7},{7,6},{8,9},{9,8},{10,11... | collective-permute-start | bytes 1572872 | tf_op jit(solution)/shard_map/ppermute | solution.py:163
  77.4 16.8 %collective-permute-start.26 = (bf16[2,256,512]{2,1,0:T(8,128)(2,1)S(1)}, bf16[2,256,512]{2,1,0:T(8,128)(2,1)S(1)}, u32[]{:S(2)}, u32[]{:S(2)}) collective-permute-start(bf16[2,256,512]{2,1,0:T(8,128)(2,1)S(1)} %pad_maximum_fusion.3), channel_id=1, source_target_pairs={{0,8},{8,0},{16,24},{24,16},{1,9},{9,1},{17,25},{25,17},{2,10},{10... | collective-permute-start | bytes 1572872 | tf_op jit(solution)/shard_map/ppermute | solution.py:163
  77.6 16.7 %collective-permute-start.24 = (bf16[128,2048]{1,0:T(8,128)(2,1)S(1)}, bf16[128,2048]{1,0:T(8,128)(2,1)S(1)}, u32[]{:S(2)}, u32[]{:S(2)}) collective-permute-start(bf16[128,2048]{1,0:T(8,128)(2,1)S(1)} %get-tuple-element.58.refs_4_), channel_id=1, source_target_pairs={{0,2},{1,3},{2,0},{3,1},{4,6},{5,7},{6,4},{7,5},{8,10},{9,11},{10,... | collective-permute-start | bytes 1572872 | tf_op jit(solution)/shard_map/ppermute | solution.py:163
  79.0 15.5 %collective-permute-start.25 = (bf16[128,2048]{1,0:T(8,128)(2,1)S(1)}, bf16[128,2048]{1,0:T(8,128)(2,1)S(1)}, u32[]{:S(2)}, u32[]{:S(2)}) collective-permute-start(bf16[128,2048]{1,0:T(8,128)(2,1)S(1)} %get-tuple-element.66), channel_id=1, source_target_pairs={{0,4},{1,5},{2,6},{3,7},{4,0},{5,1},{6,2},{7,3},{8,12},{9,13},{10,... | collective-permute-start | bytes 1572872 | tf_op jit(solution)/shard_map/ppermute | solution.py:163
  80.3 19.2 %slice-start = ((s8[8388608]{0:T(1024)(128)(4,1)}), s8[4194304]{0:T(1024)(128)(4,1)S(1)}, s32[]{:S(2)}) async-start(s8[8388608]{0:T(1024)(128)(4,1)} %bitcast.51), calls=%async_computation | async-start | bytes 8388608
  82.4 17.1 %slice-start.1 = ((s8[8388608]{0:T(1024)(128)(4,1)}), s8[4194304]{0:T(1024)(128)(4,1)S(1)}, s32[]{:S(2)}) async-start(s8[8388608]{0:T(1024)(128)(4,1)} %bitcast.51), calls=%async_computation.1 | async-start | bytes 8388608
  82.5 12.1 %collective-permute-start.23 = (bf16[512,128]{1,0:T(8,128)(2,1)S(1)}, bf16[512,128]{1,0:T(8,128)(2,1)S(1)}, u32[]{:S(2)}, u32[]{:S(2)}) collective-permute-start(bf16[512,128]{1,0:T(8,128)(2,1)S(1)} %select_convert_fusion.1), channel_id=1, source_target_pairs={{0,16},{8,24},{16,0},{24,8},{1,17},{9,25},{17,1},{25,9},{2,18},{10... | collective-permute-start | bytes 393224 | tf_op jit(solution)/shard_map/ppermute | solution.py:163
  94.8 15.1 %collective-permute-start.28 = (bf16[512,128]{1,0:T(8,128)(2,1)S(1)}, bf16[512,128]{1,0:T(8,128)(2,1)S(1)}, u32[]{:S(2)}, u32[]{:S(2)}) collective-permute-start(bf16[512,128]{1,0:T(8,128)(2,1)S(1)} %get-tuple-element.69), channel_id=1, source_target_pairs={{0,8},{8,0},{16,24},{24,16},{1,9},{9,1},{17,25},{25,17},{2,10},{10... | collective-permute-start | bytes 393224 | tf_op jit(solution)/shard_map/ppermute | solution.py:163
  95.6 14.4 %collective-permute-start.27 = (bf16[256,512]{1,0:T(8,128)(2,1)S(1)}, bf16[256,512]{1,0:T(8,128)(2,1)S(1)}, u32[]{:S(2)}, u32[]{:S(2)}) collective-permute-start(bf16[256,512]{1,0:T(8,128)(2,1)S(1)} %select_convert_fusion), channel_id=1, source_target_pairs={{0,16},{8,24},{16,0},{24,8},{1,17},{9,25},{17,1},{25,9},{2,18},{10... | collective-permute-start | bytes 786440 | tf_op jit(solution)/shard_map/ppermute | solution.py:163
  97.8 12.5 %collective-permute-start.29 = (bf16[128,2048]{1,0:T(8,128)(2,1)S(1)}, bf16[128,2048]{1,0:T(8,128)(2,1)S(1)}, u32[]{:S(2)}, u32[]{:S(2)}) collective-permute-start(bf16[128,2048]{1,0:T(8,128)(2,1)S(1)} %get-tuple-element.70), channel_id=1, source_target_pairs={{0,4},{1,5},{2,6},{3,7},{4,0},{5,1},{6,2},{7,3},{8,12},{9,13},{10,... | collective-permute-start | bytes 1572872 | tf_op jit(solution)/shard_map/ppermute | solution.py:163
  99.0 12.2 %collective-permute-start.30 = (bf16[128,2048]{1,0:T(8,128)(2,1)S(1)}, bf16[128,2048]{1,0:T(8,128)(2,1)S(1)}, u32[]{:S(2)}, u32[]{:S(2)}) collective-permute-start(bf16[128,2048]{1,0:T(8,128)(2,1)S(1)} %get-tuple-element.71), channel_id=1, source_target_pairs={{0,2},{1,3},{2,0},{3,1},{4,6},{5,7},{6,4},{7,5},{8,10},{9,11},{10,... | collective-permute-start | bytes 1572872 | tf_op jit(solution)/shard_map/ppermute | solution.py:163
  112.2 3.8 %collective-permute-start.31 = (bf16[4,128,512]{2,1,0:T(8,128)(2,1)S(1)}, bf16[4,128,512]{2,1,0:T(8,128)(2,1)S(1)}, u32[]{:S(2)}, u32[]{:S(2)}) collective-permute-start(bf16[4,128,512]{2,1,0:T(8,128)(2,1)S(1)} %get-tuple-element.77), channel_id=1, source_target_pairs={{0,1},{1,0},{2,3},{3,2},{4,5},{5,4},{6,7},{7,6},{8,9},{9,8},{10,11... | collective-permute-start | bytes 1572872 | tf_op jit(solution)/shard_map/ppermute | solution.py:163
  112.3 14.8 %collective-permute-start.35 = (bf16[128,2048]{1,0:T(8,128)(2,1)S(1)}, bf16[128,2048]{1,0:T(8,128)(2,1)S(1)}, u32[]{:S(2)}, u32[]{:S(2)}) collective-permute-start(bf16[128,2048]{1,0:T(8,128)(2,1)S(1)} %get-tuple-element.83), channel_id=1, source_target_pairs={{0,4},{1,5},{2,6},{3,7},{4,0},{5,1},{6,2},{7,3},{8,12},{9,13},{10,... | collective-permute-start | bytes 1572872 | tf_op jit(solution)/shard_map/ppermute | solution.py:163
  113.2 14.8 %collective-permute-start.36 = (bf16[128,2048]{1,0:T(8,128)(2,1)S(1)}, bf16[128,2048]{1,0:T(8,128)(2,1)S(1)}, u32[]{:S(2)}, u32[]{:S(2)}) collective-permute-start(bf16[128,2048]{1,0:T(8,128)(2,1)S(1)} %get-tuple-element.84), channel_id=1, source_target_pairs={{0,2},{1,3},{2,0},{3,1},{4,6},{5,7},{6,4},{7,5},{8,10},{9,11},{10,... | collective-permute-start | bytes 1572872 | tf_op jit(solution)/shard_map/ppermute | solution.py:163
  116.4 17.2 %collective-permute-start.32 = (bf16[256,512]{1,0:T(8,128)(2,1)S(1)}, bf16[256,512]{1,0:T(8,128)(2,1)S(1)}, u32[]{:S(2)}, u32[]{:S(2)}) collective-permute-start(bf16[256,512]{1,0:T(8,128)(2,1)S(1)} %get-tuple-element.79), channel_id=1, source_target_pairs={{0,2},{1,3},{2,0},{3,1},{4,6},{5,7},{6,4},{7,5},{8,10},{9,11},{10,... | collective-permute-start | bytes 786440 | tf_op jit(solution)/shard_map/ppermute | solution.py:163
  117.3 16.3 %collective-permute-start.33 = (bf16[256,512]{1,0:T(8,128)(2,1)S(1)}, bf16[256,512]{1,0:T(8,128)(2,1)S(1)}, u32[]{:S(2)}, u32[]{:S(2)}) collective-permute-start(bf16[256,512]{1,0:T(8,128)(2,1)S(1)} %get-tuple-element.80), channel_id=1, source_target_pairs={{0,4},{1,5},{2,6},{3,7},{4,0},{5,1},{6,2},{7,3},{8,12},{9,13},{10,... | collective-permute-start | bytes 786440 | tf_op jit(solution)/shard_map/ppermute | solution.py:163
  118.4 20.6 %collective-permute-start.34 = (bf16[256,512]{1,0:T(8,128)(2,1)S(1)}, bf16[256,512]{1,0:T(8,128)(2,1)S(1)}, u32[]{:S(2)}, u32[]{:S(2)}) collective-permute-start(bf16[256,512]{1,0:T(8,128)(2,1)S(1)} %get-tuple-element.81), channel_id=1, source_target_pairs={{0,6},{1,7},{2,4},{3,5},{4,2},{5,3},{6,0},{7,1},{8,14},{9,15},{10,... | collective-permute-start | bytes 786440 | tf_op jit(solution)/shard_map/ppermute | solution.py:163

commit v4 on v3

--- a/solution.py
+++ b/solution.py
@@ -466,7 +466,7 @@
     x_a, low_a = low_rows(0, with_mates((tokens,)))
     back_half = (back_part + got1.astype(F32)).astype(BF16)
     (back_half,) = tie((back_half,), (x_top, y_top, low_a))
-    (base_partial,) = tie((base_partial,), (got1,))
+    base_partial, bottom = tie((base_partial, bottom), (got1,))
 
     back_other = swap(back_half, "fsdp", 2)
     x_bottom, y_bottom = swap(bottom, "adapter", 2), swap(bottom, "adapter", 4)

time: 140 us -> 140 us (level)
  waiting for transfers between devices: 57.7 us -> 56.3 us
where the time goes in v4:
time: 140 us
  waiting for transfers between devices  56.3 us (40%)
  starting transfers between devices  35.9 us (26%)
  Pallas kernels  30.6 us (22%)
  matrix products  9.93 us (7%)
  other arithmetic  3.97 us (3%)
  between operations  2.39 us (2%)
    ppermute x37, waiting for transfers between devices, swap(): return lax.ppermute(value, axis, [(i, i ^ bits) for i in range(size)])  56.3 us
    ppermute x37, starting transfers between devices, swap(): return lax.ppermute(value, axis, [(i, i ^ bits) for i in range(size)])  35.9 us
    pallas_call x14, Pallas kernels, call(): pl.pallas_call(run, grid_spec=spec, out_shape=outs, name=name, input_outp...  30.6 us
    dot_general x1, matrix products, shards(): jnp.dot(tokens, base_weight, preferred_element_type=F32).astype(BF16)  6.05 us
    dot_general x2, matrix products, contract(): lax.dot_general(left, right, (((left_dim,), (right_dim,)), ((), ())), pre...  3.89 us
  transfers between devices with their start and end apart: 37, of which 15 were waited for; matrix products, arithmetic and copies ran while one was open for 9% of the time, Pallas kernels for 18%

profile of v4, /device:TPU:0, one launch (start us, length us, event | category | flops | bytes accessed | tf_op | source)
XLA Modules:
  0.0 139.6 jit_solution(13020960129022314730)
XLA Ops:
  0.6 1.0 message.1.refs_0_
  1.6 4.0 %collective-permute-start.3 = (bf16[272,512]{1,0:T(8,128)(2,1)S(1)}, bf16[272,512]{1,0:T(8,128)(2,1)S(1)}, u32[]{:S(2)}, u32[]{:S(2)}) collective-permute-start(bf16[272,512]{1,0:T(8,128)(2,1)S(1)} %message.1.refs_0_), channel_id=1, source_target_pairs={{0,6},{1,7},{2,4},{3,5},{4,2},{5,3},{6,0},{7,1},{8,14},{9,15},{10,... | collective-permute-start | bytes 835592 | tf_op jit(solution)/shard_map/ppermute | solution.py:163
  6.2 6.0 %convolution_convert_fusion.refs_4_.refs_0_ = bf16[256,2048]{1,0:T(8,128)(2,1)S(1)} fusion(bf16[256,2048]{1,0:T(8,128)(2,1)} %refs_0_.3, bf16[2048,2048]{1,0:T(8,128)(2,1)} %param.10), kind=kOutput, calls=%fused_computation | convolution fusion | flops 2148007936 | bytes 10485760 | tf_op jit(solution)/shard_map/dot_general | solution.py:425
  12.4 0.7 collective-permute-done.3.refs_2_
  13.1 5.1 %collective-permute-done.2.refs_1_ = bf16[272,512]{1,0:T(8,128)(2,1)S(1)} collective-permute-done((bf16[272,512]{1,0:T(8,128)(2,1)S(1)}, bf16[272,512]{1,0:T(8,128)(2,1)S(1)}, u32[]{:S(2)}, u32[]{:S(2)}) %collective-permute-start.2) | collective-permute-done | bytes 278560 | tf_op jit(solution)/shard_map/ppermute | solution.py:163
  19.5 1.5 %collective-permute-start.15 = (bf16[128,2048]{1,0:T(8,128)(2,1)S(1)}, bf16[128,2048]{1,0:T(8,128)(2,1)S(1)}, u32[]{:S(2)}, u32[]{:S(2)}) collective-permute-start(bf16[128,2048]{1,0:T(8,128)(2,1)S(1)} %get-tuple-element.58), channel_id=1, source_target_pairs={{0,2},{1,3},{2,0},{3,1},{4,6},{5,7},{6,4},{7,5},{8,10},{9,11},{10,... | collective-permute-start | bytes 1572872 | tf_op jit(solution)/shard_map/ppermute | solution.py:163
  21.7 2.6 %back_rows.1 = (bf16[8,128,512]{2,1,0:T(8,128)(2,1)S(1)}, f32[8,128,128]{2,1,0:T(8,128)S(1)}, bf16[8,256,128]{2,1,0:T(8,128)(2,1)S(1)}, bf16[4,256,128]{2,1,0:T(8,128)(2,1)S(1)}, f32[4,128,128]{2,1,0:T(8,128)S(1)}) custom-call(bf16[272,512]{1,0:T(8,128)(2,1)S(1)} %message.1.refs_0_, bf16[272,512]{1,0:T(8,128)(2,1)S(1)} %collective-permute-done.refs_1_, ...), custom_call_target="tpu_custom_call" | custom-call | flops 1024 | bytes 1024 | tf_op jit(solution)/shard_map/back_rows/pallas_call | solution.py:188
  24.3 1.8 %collective-permute-start.7 = (bf16[512,128]{1,0:T(8,128)(2,1)S(1)}, bf16[512,128]{1,0:T(8,128)(2,1)S(1)}, u32[]{:S(2)}, u32[]{:S(2)}) collective-permute-start(bf16[512,128]{1,0:T(8,128)(2,1)S(1)} %bitcast_convert_fusion), channel_id=1, source_target_pairs={{0,8},{8,0},{16,24},{24,16},{1,9},{9,1},{17,25},{25,17},{2,10},{10... | collective-permute-start | bytes 393224 | tf_op jit(solution)/shard_map/ppermute | solution.py:163
  27.9 1.6 %collective-permute-done.7.refs_2_ = bf16[512,128]{1,0:T(8,128)(2,1)S(1)} collective-permute-done((bf16[512,128]{1,0:T(8,128)(2,1)S(1)}, bf16[512,128]{1,0:T(8,128)(2,1)S(1)}, u32[]{:S(2)}, u32[]{:S(2)}) %collective-permute-start.7) | collective-permute-done | bytes 131104 | tf_op jit(solution)/shard_map/ppermute | solution.py:163
  29.5 1.3 collective-permute-start.14
  30.8 0.8 collective-permute-start.11
  31.6 2.8 %collective-permute-done.15.refs_4_.refs_1_ = bf16[128,2048]{1,0:T(8,128)(2,1)S(1)} collective-permute-done((bf16[128,2048]{1,0:T(8,128)(2,1)S(1)}, bf16[128,2048]{1,0:T(8,128)(2,1)S(1)}, u32[]{:S(2)}, u32[]{:S(2)}) %collective-permute-start.15) | collective-permute-done | bytes 524320 | tf_op jit(solution)/shard_map/ppermute | solution.py:163
  34.3 1.5 %collective-permute-done.9.refs_0_.refs_2_ = bf16[128,2048]{1,0:T(8,128)(2,1)S(1)} collective-permute-done((bf16[128,2048]{1,0:T(8,128)(2,1)S(1)}, bf16[128,2048]{1,0:T(8,128)(2,1)S(1)}, u32[]{:S(2)}, u32[]{:S(2)}) %collective-permute-start.9) | collective-permute-done | bytes 524320 | tf_op jit(solution)/shard_map/ppermute | solution.py:163
  36.1 1.6 %low_rows.3 = (bf16[256,2048]{1,0:T(8,128)(2,1)S(1)}, f32[256,128]{1,0:T(8,128)S(1)}) custom-call(bf16[256,2048]{1,0:T(8,128)(2,1)S(1)} %copy-done.1, bf16[256,2048]{1,0:T(8,128)(2,1)S(1)} %collective-permute-done.8.refs_1_, bf16[8,256,128]{2,1,0:T(8,128)(2,1)S(1)} %get-tuple-element.55.refs_2_.refs_8_.refs_0_.refs_4_, ...), custom_call_target="tpu_custom_call" | custom-call | flops 1024 | bytes 1024 | tf_op jit(solution)/shard_map/low_rows/pallas_call | solution.py:188
  37.7 2.7 %collective-permute-start.18 = (bf16[512,128]{1,0:T(8,128)(2,1)S(1)}, bf16[512,128]{1,0:T(8,128)(2,1)S(1)}, u32[]{:S(2)}, u32[]{:S(2)}) collective-permute-start(bf16[512,128]{1,0:T(8,128)(2,1)S(1)} %tie.7), channel_id=1, source_target_pairs={{0,16},{8,24},{16,0},{24,8},{1,17},{9,25},{17,1},{25,9},{2,18},{10... | collective-permute-start | bytes 393224 | tf_op jit(solution)/shard_map/ppermute | solution.py:163
  40.4 1.6 %collective-permute-start.19 = (bf16[256,1024]{1,0:T(8,128)(2,1)S(1)}, bf16[256,1024]{1,0:T(8,128)(2,1)S(1)}, u32[]{:S(2)}, u32[]{:S(2)}) collective-permute-start(bf16[256,1024]{1,0:T(8,128)(2,1)S(1)} %pad_maximum_fusion.2), channel_id=1, source_target_pairs={{0,8},{8,0},{16,24},{24,16},{1,9},{9,1},{17,25},{25,17},{2,10},{10... | collective-permute-start | bytes 1572872 | tf_op jit(solution)/shard_map/ppermute | solution.py:163
  42.1 5.4 %collective-permute-done.18 = bf16[512,128]{1,0:T(8,128)(2,1)S(1)} collective-permute-done((bf16[512,128]{1,0:T(8,128)(2,1)S(1)}, bf16[512,128]{1,0:T(8,128)(2,1)S(1)}, u32[]{:S(2)}, u32[]{:S(2)}) %collective-permute-start.18) | collective-permute-done | bytes 131104 | tf_op jit(solution)/shard_map/ppermute | solution.py:163
  47.7 8.5 %collective-permute-done.19.refs_6_.refs_1_ = bf16[256,1024]{1,0:T(8,128)(2,1)S(1)} collective-permute-done((bf16[256,1024]{1,0:T(8,128)(2,1)S(1)}, bf16[256,1024]{1,0:T(8,128)(2,1)S(1)}, u32[]{:S(2)}, u32[]{:S(2)}) %collective-permute-start.19) | collective-permute-done | bytes 524320 | tf_op jit(solution)/shard_map/ppermute | solution.py:163
  56.2 3.8 %back_delta.2.refs_3_ = bf16[4,128,2048]{2,1,0:T(8,128)(2,1)S(1)} custom-call(bf16[1024,128]{1,0:T(8,128)(2,1)S(1)} %maximum_maximum_fusion.refs_0_.refs_3_, f32[8,128,128]{2,1,0:T(8,128)S(1)} %get-tuple-element.56.refs_3_.refs_9_.refs_1_.refs_5_, bf16[8,2048,128]{2,1,0:T(8,128)(2,1)S(1)} %copy-done, ...), custom_call_target="tpu_custom_call" | custom-call | flops 1024 | bytes 1024 | tf_op jit(solution)/shard_map/back_delta/pallas_call | solution.py:188
  61.2 1.5 %collective-permute-start.12 = (bf16[128,2048]{1,0:T(8,128)(2,1)S(1)}, bf16[128,2048]{1,0:T(8,128)(2,1)S(1)}, u32[]{:S(2)}, u32[]{:S(2)}) collective-permute-start(bf16[128,2048]{1,0:T(8,128)(2,1)S(1)} %collective-permute-done.11.refs_5_.refs_3_), channel_id=1, source_target_pairs={{0,4},{1,5},{2,6},{3,7},{4,0},{5,1},{6,2},{7,3},{8,12},{9,13},{10,... | collective-permute-start | bytes 1572872 | tf_op jit(solution)/shard_map/ppermute | solution.py:163
  62.7 1.1 collective-permute-start.13
  63.9 3.6 %back_delta.3.refs_2_ = bf16[4,128,2048]{2,1,0:T(8,128)(2,1)S(1)} custom-call(bf16[1024,128]{1,0:T(8,128)(2,1)S(1)} %maximum_maximum_fusion.refs_0_.refs_3_, f32[8,128,128]{2,1,0:T(8,128)S(1)} %get-tuple-element.56.refs_3_.refs_9_.refs_1_.refs_5_, bf16[8,2048,128]{2,1,0:T(8,128)(2,1)S(1)} %copy-done, bf16[4,128,2048]{2,1,0:T(8,128)(2,1)S(1)} %back_delta.2.refs_3_), custom_call_target="tpu_custom_call" | custom-call | flops 1024 | bytes 1024 | tf_op jit(solution)/shard_map/back_delta/pallas_call | solution.py:188
  67.5 3.4 %low_rows.4 = (bf16[512,2048]{1,0:T(8,128)(2,1)S(1)}, f32[512,128]{1,0:T(8,128)S(1)}) custom-call(bf16[128,2048]{1,0:T(8,128)(2,1)S(1)} %collective-permute-done.9.refs_0_.refs_2_, bf16[128,2048]{1,0:T(8,128)(2,1)S(1)} %collective-permute-done.14.refs_1_.refs_4_, bf16[256,2048]{1,0:T(8,128)(2,1)S(1)} %collective-permute-done.16.refs_2_.refs_6_.refs_5_, ...), custom_call_target="tpu_custom_call" | custom-call | flops 1024 | bytes 1024 | tf_op jit(solution)/shard_map/low_rows/pallas_call | solution.py:188
  70.9 0.8 back_diag.1
  71.7 1.2 back_near.1
  73.0 4.0 %collective-permute-done.13.refs_2_ = bf16[256,512]{1,0:T(8,128)(2,1)S(1)} collective-permute-done((bf16[256,512]{1,0:T(8,128)(2,1)S(1)}, bf16[256,512]{1,0:T(8,128)(2,1)S(1)}, u32[]{:S(2)}, u32[]{:S(2)}) %collective-permute-start.13) | collective-permute-done | bytes 262176 | tf_op jit(solution)/shard_map/ppermute | solution.py:163
  77.8 0.8 collective-permute-start.24
  78.6 1.4 collective-permute-start.25
  80.0 0.8 back_home.1.refs_3_
  80.8 1.8 %low_rows.5 = (bf16[256,2048]{1,0:T(8,128)(2,1)S(1)}, f32[256,128]{1,0:T(8,128)S(1)}) custom-call(bf16[128,2048]{1,0:T(8,128)(2,1)S(1)} %get-tuple-element.64.refs_0_, bf16[128,2048]{1,0:T(8,128)(2,1)S(1)} %get-tuple-element.65.refs_1_, bf16[128,2048]{1,0:T(8,128)(2,1)S(1)} %collective-permute-done.21.refs_2_, ...), custom_call_target="tpu_custom_call" | custom-call | flops 1024 | bytes 1024 | tf_op jit(solution)/shard_map/low_rows/pallas_call | solution.py:188
  83.0 2.7 %collective-permute-start.23 = (bf16[512,128]{1,0:T(8,128)(2,1)S(1)}, bf16[512,128]{1,0:T(8,128)(2,1)S(1)}, u32[]{:S(2)}, u32[]{:S(2)}) collective-permute-start(bf16[512,128]{1,0:T(8,128)(2,1)S(1)} %select_convert_fusion.1), channel_id=1, source_target_pairs={{0,16},{8,24},{16,0},{24,8},{1,17},{9,25},{17,1},{25,9},{2,18},{10... | collective-permute-start | bytes 393224 | tf_op jit(solution)/shard_map/ppermute | solution.py:163
  85.6 8.8 %collective-permute-done.26.refs_6_ = bf16[2,256,512]{2,1,0:T(8,128)(2,1)S(1)} collective-permute-done((bf16[2,256,512]{2,1,0:T(8,128)(2,1)S(1)}, bf16[2,256,512]{2,1,0:T(8,128)(2,1)S(1)}, u32[]{:S(2)}, u32[]{:S(2)}) %collective-permute-start.26) | collective-permute-done | bytes 524320 | tf_op jit(solution)/shard_map/ppermute | solution.py:163
  95.8 2.2 %collective-permute-start.27 = (bf16[256,512]{1,0:T(8,128)(2,1)S(1)}, bf16[256,512]{1,0:T(8,128)(2,1)S(1)}, u32[]{:S(2)}, u32[]{:S(2)}) collective-permute-start(bf16[256,512]{1,0:T(8,128)(2,1)S(1)} %select_convert_fusion), channel_id=1, source_target_pairs={{0,16},{8,24},{16,0},{24,8},{1,17},{9,25},{17,1},{25,9},{2,18},{10... | collective-permute-start | bytes 786440 | tf_op jit(solution)/shard_map/ppermute | solution.py:163
  98.5 1.6 %collective-permute-start.30 = (bf16[128,2048]{1,0:T(8,128)(2,1)S(1)}, bf16[128,2048]{1,0:T(8,128)(2,1)S(1)}, u32[]{:S(2)}, u32[]{:S(2)}) collective-permute-start(bf16[128,2048]{1,0:T(8,128)(2,1)S(1)} %get-tuple-element.75), channel_id=1, source_target_pairs={{0,2},{1,3},{2,0},{3,1},{4,6},{5,7},{6,4},{7,5},{8,10},{9,11},{10,... | collective-permute-start | bytes 1572872 | tf_op jit(solution)/shard_map/ppermute | solution.py:163
  100.1 2.4 %fusion.1.refs_10_ = f32[256,2048]{1,0:T(8,128)S(1)} fusion(bf16[2048,2048]{1,0:T(8,128)(2,1)S(1)} %bitcast.52, bf16[256,512]{1,0:T(8,128)(2,1)S(1)} %get-tuple-element.99, bf16[256,512]{1,0:T(8,128)(2,1)S(1)} %get-tuple-element.98, bf16[256,512]{1,0:T(8,128)(2,1)S(1)} %get-tuple-element.97, bf16[256,512]{1,0:T(8,128)(2,1)S(1)} %get-tuple-element.96), kind=kOutput, calls=%fused_computation.6 | convolution fusion | flops 2151677952 | bytes 11534336 | tf_op jit(solution)/shard_map/dot_general | solution.py:156
  102.4 8.0 %down_grad.1 = (bf16[8,2048,128]{2,1,0:T(8,128)(2,1)}, f32[8,128]{1,0:T(8,128)S(1)}) custom-call(bf16[256,2048]{1,0:T(8,128)(2,1)S(1)} %get-tuple-element.76.refs_0_, bf16[256,2048]{1,0:T(8,128)(2,1)S(1)} %get-tuple-element.77.refs_1_, bf16[512,2048]{1,0:T(8,128)(2,1)S(1)} %get-tuple-element.78.refs_2_, ...), custom_call_target="tpu_custom_call" | custom-call | flops 1024 | bytes 1024 | tf_op jit(solution)/shard_map/down_grad/pallas_call | solution.py:188
  110.7 1.0 up_delta.1
  111.8 1.5 %collective-permute-start.35 = (bf16[128,2048]{1,0:T(8,128)(2,1)S(1)}, bf16[128,2048]{1,0:T(8,128)(2,1)S(1)}, u32[]{:S(2)}, u32[]{:S(2)}) collective-permute-start(bf16[128,2048]{1,0:T(8,128)(2,1)S(1)} %get-tuple-element.87), channel_id=1, source_target_pairs={{0,4},{1,5},{2,6},{3,7},{4,0},{5,1},{6,2},{7,3},{8,12},{9,13},{10,... | collective-permute-start | bytes 1572872 | tf_op jit(solution)/shard_map/ppermute | solution.py:163
  113.3 0.8 collective-permute-start.36
  114.1 1.5 %fusion = bf16[512,512]{1,0:T(8,128)(2,1)} fusion(bf16[1024,512]{1,0:T(8,128)(2,1)S(1)} %get-tuple-element.90, bf16[1024,512]{1,0:T(8,128)(2,1)S(1)} %bitcast.48), kind=kOutput, calls=%fused_computation.3 | convolution fusion | flops 537395200 | bytes 2621440 | tf_op jit(solution)/shard_map/dot_general | solution.py:156
  116.1 1.3 collective-permute-start.32
  118.0 1.7 %collective-permute-start.34 = (bf16[256,512]{1,0:T(8,128)(2,1)S(1)}, bf16[256,512]{1,0:T(8,128)(2,1)S(1)}, u32[]{:S(2)}, u32[]{:S(2)}) collective-permute-start(bf16[256,512]{1,0:T(8,128)(2,1)S(1)} %get-tuple-element.85), channel_id=1, source_target_pairs={{0,6},{1,7},{2,4},{3,5},{4,2},{5,3},{6,0},{7,1},{8,14},{9,15},{10,... | collective-permute-start | bytes 786440 | tf_op jit(solution)/shard_map/ppermute | solution.py:163
  119.7 6.9 %collective-permute-done.35 = bf16[128,2048]{1,0:T(8,128)(2,1)S(1)} collective-permute-done((bf16[128,2048]{1,0:T(8,128)(2,1)S(1)}, bf16[128,2048]{1,0:T(8,128)(2,1)S(1)}, u32[]{:S(2)}, u32[]{:S(2)}) %collective-permute-start.35) | collective-permute-done | bytes 524320 | tf_op jit(solution)/shard_map/ppermute | solution.py:163
  126.6 1.5 %collective-permute-done.36 = bf16[128,2048]{1,0:T(8,128)(2,1)S(1)} collective-permute-done((bf16[128,2048]{1,0:T(8,128)(2,1)S(1)}, bf16[128,2048]{1,0:T(8,128)(2,1)S(1)}, u32[]{:S(2)}, u32[]{:S(2)}) %collective-permute-start.36) | collective-permute-done | bytes 524320 | tf_op jit(solution)/shard_map/ppermute | solution.py:163
  128.3 1.3 add_convert_fusion
  129.6 4.2 %collective-permute-done.32 = bf16[256,512]{1,0:T(8,128)(2,1)S(1)} collective-permute-done((bf16[256,512]{1,0:T(8,128)(2,1)S(1)}, bf16[256,512]{1,0:T(8,128)(2,1)S(1)}, u32[]{:S(2)}, u32[]{:S(2)}) %collective-permute-start.32) | collective-permute-done | bytes 262176 | tf_op jit(solution)/shard_map/ppermute | solution.py:163
  133.7 4.8 %collective-permute-done.34 = bf16[256,512]{1,0:T(8,128)(2,1)S(1)} collective-permute-done((bf16[256,512]{1,0:T(8,128)(2,1)S(1)}, bf16[256,512]{1,0:T(8,128)(2,1)S(1)}, u32[]{:S(2)}, u32[]{:S(2)}) %collective-permute-start.34) | collective-permute-done | bytes 262176 | tf_op jit(solution)/shard_map/ppermute | solution.py:163
  138.6 1.1 add_convert_fusion.1
  (86 shorter events, 9.5 us)
Async XLA Ops:
  1.6 10.7 %copy-start.1 = (bf16[256,2048]{1,0:T(8,128)(2,1)S(1)}, bf16[256,2048]{1,0:T(8,128)(2,1)}, u32[]{:S(2)}) copy-start(bf16[256,2048]{1,0:T(8,128)(2,1)} %refs_0_.3) | copy-start | bytes 3145732
  1.6 11.5 %collective-permute-start.3 = (bf16[272,512]{1,0:T(8,128)(2,1)S(1)}, bf16[272,512]{1,0:T(8,128)(2,1)S(1)}, u32[]{:S(2)}, u32[]{:S(2)}) collective-permute-start(bf16[272,512]{1,0:T(8,128)(2,1)S(1)} %message.1.refs_0_), channel_id=1, source_target_pairs={{0,6},{1,7},{2,4},{3,5},{4,2},{5,3},{6,0},{7,1},{8,14},{9,15},{10,... | collective-permute-start | bytes 835592 | tf_op jit(solution)/shard_map/ppermute | solution.py:163
  5.6 12.6 %collective-permute-start.2 = (bf16[272,512]{1,0:T(8,128)(2,1)S(1)}, bf16[272,512]{1,0:T(8,128)(2,1)S(1)}, u32[]{:S(2)}, u32[]{:S(2)}) collective-permute-start(bf16[272,512]{1,0:T(8,128)(2,1)S(1)} %message.1.refs_0_), channel_id=1, source_target_pairs={{0,4},{1,5},{2,6},{3,7},{4,0},{5,1},{6,2},{7,3},{8,12},{9,13},{10,... | collective-permute-start | bytes 835592 | tf_op jit(solution)/shard_map/ppermute | solution.py:163
  6.1 12.4 %collective-permute-start.1 = (bf16[272,512]{1,0:T(8,128)(2,1)S(1)}, bf16[272,512]{1,0:T(8,128)(2,1)S(1)}, u32[]{:S(2)}, u32[]{:S(2)}) collective-permute-start(bf16[272,512]{1,0:T(8,128)(2,1)S(1)} %message.1.refs_0_), channel_id=1, source_target_pairs={{0,2},{1,3},{2,0},{3,1},{4,6},{5,7},{6,4},{7,5},{8,10},{9,11},{10,... | collective-permute-start | bytes 835592 | tf_op jit(solution)/shard_map/ppermute | solution.py:163
  6.2 13.3 %collective-permute-start = (bf16[272,512]{1,0:T(8,128)(2,1)S(1)}, bf16[272,512]{1,0:T(8,128)(2,1)S(1)}, u32[]{:S(2)}, u32[]{:S(2)}) collective-permute-start(bf16[272,512]{1,0:T(8,128)(2,1)S(1)} %message.1.refs_0_), channel_id=1, source_target_pairs={{0,1},{1,0},{2,3},{3,2},{4,5},{5,4},{6,7},{7,6},{8,9},{9,8},{10,11... | collective-permute-start | bytes 835592 | tf_op jit(solution)/shard_map/ppermute | solution.py:163
  12.3 9.3 %copy-start.2 = (bf16[8,64,512]{2,1,0:T(8,128)(2,1)S(1)}, bf16[8,64,512]{2,1,0:T(8,128)(2,1)}, u32[]{:S(2)}) copy-start(bf16[8,64,512]{2,1,0:T(8,128)(2,1)} %refs_2_.5) | copy-start | bytes 1572868
  18.5 2.5 %collective-permute-start.4 = (bf16[272,512]{1,0:T(8,128)(2,1)S(1)}, bf16[272,512]{1,0:T(8,128)(2,1)S(1)}, u32[]{:S(2)}, u32[]{:S(2)}) collective-permute-start(bf16[272,512]{1,0:T(8,128)(2,1)S(1)} %get-tuple-element.50.refs_2_), channel_id=1, source_target_pairs={{0,1},{1,0},{2,3},{3,2},{4,5},{5,4},{6,7},{7,6},{8,9},{9,8},{10,11... | collective-permute-start | bytes 835592 | tf_op jit(solution)/shard_map/ppermute | solution.py:163
  18.5 3.1 %collective-permute-start.5 = (bf16[272,512]{1,0:T(8,128)(2,1)S(1)}, bf16[272,512]{1,0:T(8,128)(2,1)S(1)}, u32[]{:S(2)}, u32[]{:S(2)}) collective-permute-start(bf16[272,512]{1,0:T(8,128)(2,1)S(1)} %get-tuple-element.51.refs_4_), channel_id=1, source_target_pairs={{0,1},{1,0},{2,3},{3,2},{4,5},{5,4},{6,7},{7,6},{8,9},{9,8},{10,11... | collective-permute-start | bytes 835592 | tf_op jit(solution)/shard_map/ppermute | solution.py:163
  19.0 2.6 %collective-permute-start.6 = (bf16[272,512]{1,0:T(8,128)(2,1)S(1)}, bf16[272,512]{1,0:T(8,128)(2,1)S(1)}, u32[]{:S(2)}, u32[]{:S(2)}) collective-permute-start(bf16[272,512]{1,0:T(8,128)(2,1)S(1)} %get-tuple-element.52.refs_6_), channel_id=1, source_target_pairs={{0,1},{1,0},{2,3},{3,2},{4,5},{5,4},{6,7},{7,6},{8,9},{9,8},{10,11... | collective-permute-start | bytes 835592 | tf_op jit(solution)/shard_map/ppermute | solution.py:163
  19.0 17.0 %collective-permute-start.8 = (bf16[256,2048]{1,0:T(8,128)(2,1)S(1)}, bf16[256,2048]{1,0:T(8,128)(2,1)S(1)}, u32[]{:S(2)}, u32[]{:S(2)}) collective-permute-start(bf16[256,2048]{1,0:T(8,128)(2,1)S(1)} %copy-done.1), channel_id=1, source_target_pairs={{0,1},{1,0},{2,3},{3,2},{4,5},{5,4},{6,7},{7,6},{8,9},{9,8},{10,11... | collective-permute-start | bytes 3145736 | tf_op jit(solution)/shard_map/ppermute | solution.py:163
  19.5 14.8 %collective-permute-start.15 = (bf16[128,2048]{1,0:T(8,128)(2,1)S(1)}, bf16[128,2048]{1,0:T(8,128)(2,1)S(1)}, u32[]{:S(2)}, u32[]{:S(2)}) collective-permute-start(bf16[128,2048]{1,0:T(8,128)(2,1)S(1)} %get-tuple-element.58), channel_id=1, source_target_pairs={{0,2},{1,3},{2,0},{3,1},{4,6},{5,7},{6,4},{7,5},{8,10},{9,11},{10,... | collective-permute-start | bytes 1572872 | tf_op jit(solution)/shard_map/ppermute | solution.py:163
  21.0 14.8 %collective-permute-start.9 = (bf16[128,2048]{1,0:T(8,128)(2,1)S(1)}, bf16[128,2048]{1,0:T(8,128)(2,1)S(1)}, u32[]{:S(2)}, u32[]{:S(2)}) collective-permute-start(bf16[128,2048]{1,0:T(8,128)(2,1)S(1)} %get-tuple-element.58), channel_id=1, source_target_pairs={{0,4},{1,5},{2,6},{3,7},{4,0},{5,1},{6,2},{7,3},{8,12},{9,13},{10,... | collective-permute-start | bytes 1572872 | tf_op jit(solution)/shard_map/ppermute | solution.py:163
  24.3 5.2 %collective-permute-start.7 = (bf16[512,128]{1,0:T(8,128)(2,1)S(1)}, bf16[512,128]{1,0:T(8,128)(2,1)S(1)}, u32[]{:S(2)}, u32[]{:S(2)}) collective-permute-start(bf16[512,128]{1,0:T(8,128)(2,1)S(1)} %bitcast_convert_fusion), channel_id=1, source_target_pairs={{0,8},{8,0},{16,24},{24,16},{1,9},{9,1},{17,25},{25,17},{2,10},{10... | collective-permute-start | bytes 393224 | tf_op jit(solution)/shard_map/ppermute | solution.py:163
  29.5 6.6 %copy-start = (bf16[8,2048,128]{2,1,0:T(8,128)(2,1)S(1)}, bf16[8,2048,128]{2,1,0:T(8,128)(2,1)}, u32[]{:S(2)}) copy-start(bf16[8,2048,128]{2,1,0:T(8,128)(2,1)} %refs_6_.1) | copy-start | bytes 12582916
  29.5 26.7 %collective-permute-start.14 = (bf16[128,2048]{1,0:T(8,128)(2,1)S(1)}, bf16[128,2048]{1,0:T(8,128)(2,1)S(1)}, u32[]{:S(2)}, u32[]{:S(2)}) collective-permute-start(bf16[128,2048]{1,0:T(8,128)(2,1)S(1)} %get-tuple-element.59), channel_id=1, source_target_pairs={{0,4},{1,5},{2,6},{3,7},{4,0},{5,1},{6,2},{7,3},{8,12},{9,13},{10,... | collective-permute-start | bytes 1572872 | tf_op jit(solution)/shard_map/ppermute | solution.py:163
  30.8 25.5 %collective-permute-start.11 = (bf16[128,2048]{1,0:T(8,128)(2,1)S(1)}, bf16[128,2048]{1,0:T(8,128)(2,1)S(1)}, u32[]{:S(2)}, u32[]{:S(2)}) collective-permute-start(bf16[128,2048]{1,0:T(8,128)(2,1)S(1)} %get-tuple-element.59), channel_id=1, source_target_pairs={{0,2},{1,3},{2,0},{3,1},{4,6},{5,7},{6,4},{7,5},{8,10},{9,11},{10,... | collective-permute-start | bytes 1572872 | tf_op jit(solution)/shard_map/ppermute | solution.py:163
  35.9 20.3 %collective-permute-start.16 = (bf16[256,2048]{1,0:T(8,128)(2,1)S(1)}, bf16[256,2048]{1,0:T(8,128)(2,1)S(1)}, u32[]{:S(2)}, u32[]{:S(2)}) collective-permute-start(bf16[256,2048]{1,0:T(8,128)(2,1)S(1)} %pad_maximum_fusion), channel_id=1, source_target_pairs={{0,1},{1,0},{2,3},{3,2},{4,5},{5,4},{6,7},{7,6},{8,9},{9,8},{10,11... | collective-permute-start | bytes 3145736 | tf_op jit(solution)/shard_map/ppermute | solution.py:163
  37.7 9.8 %collective-permute-start.18 = (bf16[512,128]{1,0:T(8,128)(2,1)S(1)}, bf16[512,128]{1,0:T(8,128)(2,1)S(1)}, u32[]{:S(2)}, u32[]{:S(2)}) collective-permute-start(bf16[512,128]{1,0:T(8,128)(2,1)S(1)} %tie.7), channel_id=1, source_target_pairs={{0,16},{8,24},{16,0},{24,8},{1,17},{9,25},{17,1},{25,9},{2,18},{10... | collective-permute-start | bytes 393224 | tf_op jit(solution)/shard_map/ppermute | solution.py:163
  40.4 15.8 %collective-permute-start.19 = (bf16[256,1024]{1,0:T(8,128)(2,1)S(1)}, bf16[256,1024]{1,0:T(8,128)(2,1)S(1)}, u32[]{:S(2)}, u32[]{:S(2)}) collective-permute-start(bf16[256,1024]{1,0:T(8,128)(2,1)S(1)} %pad_maximum_fusion.2), channel_id=1, source_target_pairs={{0,8},{8,0},{16,24},{24,16},{1,9},{9,1},{17,25},{25,17},{2,10},{10... | collective-permute-start | bytes 1572872 | tf_op jit(solution)/shard_map/ppermute | solution.py:163
  60.0 2.7 %copy-start.3 = (bf16[256,512]{1,0:T(8,128)(2,1)S(1)}, bf16[256,512]{1,0:T(8,128)(2,1)}, u32[]{:S(2)}) copy-start(bf16[256,512]{1,0:T(8,128)(2,1)} %refs_0_.2) | copy-start | bytes 786436
  60.1 10.9 %collective-permute-start.20 = (bf16[4,128,2048]{2,1,0:T(8,128)(2,1)S(1)}, bf16[4,128,2048]{2,1,0:T(8,128)(2,1)S(1)}, u32[]{:S(2)}, u32[]{:S(2)}) collective-permute-start(bf16[4,128,2048]{2,1,0:T(8,128)(2,1)S(1)} %back_delta.2.refs_3_), channel_id=1, source_target_pairs={{0,1},{1,0},{2,3},{3,2},{4,5},{5,4},{6,7},{7,6},{8,9},{9,8},{10,11... | collective-permute-start | bytes 6291464 | tf_op jit(solution)/shard_map/ppermute | solution.py:163
  60.2 7.3 %collective-permute-start.17 = (bf16[256,2048]{1,0:T(8,128)(2,1)S(1)}, bf16[256,2048]{1,0:T(8,128)(2,1)S(1)}, u32[]{:S(2)}, u32[]{:S(2)}) collective-permute-start(bf16[256,2048]{1,0:T(8,128)(2,1)S(1)} %pad_maximum_fusion.1), channel_id=1, source_target_pairs={{0,1},{1,0},{2,3},{3,2},{4,5},{5,4},{6,7},{7,6},{8,9},{9,8},{10,11... | collective-permute-start | bytes 3145736 | tf_op jit(solution)/shard_map/ppermute | solution.py:163
  60.8 16.2 %collective-permute-start.10 = (bf16[128,2048]{1,0:T(8,128)(2,1)S(1)}, bf16[128,2048]{1,0:T(8,128)(2,1)S(1)}, u32[]{:S(2)}, u32[]{:S(2)}) collective-permute-start(bf16[128,2048]{1,0:T(8,128)(2,1)S(1)} %collective-permute-done.9.refs_0_.refs_2_), channel_id=1, source_target_pairs={{0,2},{1,3},{2,0},{3,1},{4,6},{5,7},{6,4},{7,5},{8,10},{9,11},{10,... | collective-permute-start | bytes 1572872 | tf_op jit(solution)/shard_map/ppermute | solution.py:163
  61.2 15.7 %collective-permute-start.12 = (bf16[128,2048]{1,0:T(8,128)(2,1)S(1)}, bf16[128,2048]{1,0:T(8,128)(2,1)S(1)}, u32[]{:S(2)}, u32[]{:S(2)}) collective-permute-start(bf16[128,2048]{1,0:T(8,128)(2,1)S(1)} %collective-permute-done.11.refs_5_.refs_3_), channel_id=1, source_target_pairs={{0,4},{1,5},{2,6},{3,7},{4,0},{5,1},{6,2},{7,3},{8,12},{9,13},{10,... | collective-permute-start | bytes 1572872 | tf_op jit(solution)/shard_map/ppermute | solution.py:163
  62.7 14.2 %collective-permute-start.13 = (bf16[256,512]{1,0:T(8,128)(2,1)S(1)}, bf16[256,512]{1,0:T(8,128)(2,1)S(1)}, u32[]{:S(2)}, u32[]{:S(2)}) collective-permute-start(bf16[256,512]{1,0:T(8,128)(2,1)S(1)} %copy-done.3), channel_id=1, source_target_pairs={{0,16},{8,24},{16,0},{24,8},{1,17},{9,25},{17,1},{25,9},{2,18},{10... | collective-permute-start | bytes 786440 | tf_op jit(solution)/shard_map/ppermute | solution.py:163
  77.0 3.8 %collective-permute-start.21 = (bf16[128,2048]{1,0:T(8,128)(2,1)S(1)}, bf16[128,2048]{1,0:T(8,128)(2,1)S(1)}, u32[]{:S(2)}, u32[]{:S(2)}) collective-permute-start(bf16[128,2048]{1,0:T(8,128)(2,1)S(1)} %get-tuple-element.64.refs_0_), channel_id=1, source_target_pairs={{0,1},{1,0},{2,3},{3,2},{4,5},{5,4},{6,7},{7,6},{8,9},{9,8},{10,11... | collective-permute-start | bytes 1572872 | tf_op jit(solution)/shard_map/ppermute | solution.py:163
  77.0 3.7 %collective-permute-start.22 = (bf16[128,2048]{1,0:T(8,128)(2,1)S(1)}, bf16[128,2048]{1,0:T(8,128)(2,1)S(1)}, u32[]{:S(2)}, u32[]{:S(2)}) collective-permute-start(bf16[128,2048]{1,0:T(8,128)(2,1)S(1)} %get-tuple-element.65.refs_1_), channel_id=1, source_target_pairs={{0,1},{1,0},{2,3},{3,2},{4,5},{5,4},{6,7},{7,6},{8,9},{9,8},{10,11... | collective-permute-start | bytes 1572872 | tf_op jit(solution)/shard_map/ppermute | solution.py:163
  77.6 16.8 %collective-permute-start.26 = (bf16[2,256,512]{2,1,0:T(8,128)(2,1)S(1)}, bf16[2,256,512]{2,1,0:T(8,128)(2,1)S(1)}, u32[]{:S(2)}, u32[]{:S(2)}) collective-permute-start(bf16[2,256,512]{2,1,0:T(8,128)(2,1)S(1)} %pad_maximum_fusion.3), channel_id=1, source_target_pairs={{0,8},{8,0},{16,24},{24,16},{1,9},{9,1},{17,25},{25,17},{2,10},{10... | collective-permute-start | bytes 1572872 | tf_op jit(solution)/shard_map/ppermute | solution.py:163
  77.8 16.7 %collective-permute-start.24 = (bf16[128,2048]{1,0:T(8,128)(2,1)S(1)}, bf16[128,2048]{1,0:T(8,128)(2,1)S(1)}, u32[]{:S(2)}, u32[]{:S(2)}) collective-permute-start(bf16[128,2048]{1,0:T(8,128)(2,1)S(1)} %get-tuple-element.62.refs_4_), channel_id=1, source_target_pairs={{0,2},{1,3},{2,0},{3,1},{4,6},{5,7},{6,4},{7,5},{8,10},{9,11},{10,... | collective-permute-start | bytes 1572872 | tf_op jit(solution)/shard_map/ppermute | solution.py:163
  78.6 16.0 %collective-permute-start.25 = (bf16[128,2048]{1,0:T(8,128)(2,1)S(1)}, bf16[128,2048]{1,0:T(8,128)(2,1)S(1)}, u32[]{:S(2)}, u32[]{:S(2)}) collective-permute-start(bf16[128,2048]{1,0:T(8,128)(2,1)S(1)} %get-tuple-element.70), channel_id=1, source_target_pairs={{0,4},{1,5},{2,6},{3,7},{4,0},{5,1},{6,2},{7,3},{8,12},{9,13},{10,... | collective-permute-start | bytes 1572872 | tf_op jit(solution)/shard_map/ppermute | solution.py:163
  80.8 19.3 %slice-start = ((s8[8388608]{0:T(1024)(128)(4,1)}), s8[4194304]{0:T(1024)(128)(4,1)S(1)}, s32[]{:S(2)}) async-start(s8[8388608]{0:T(1024)(128)(4,1)} %bitcast.51), calls=%async_computation | async-start | bytes 8388608
  82.9 17.1 %slice-start.1 = ((s8[8388608]{0:T(1024)(128)(4,1)}), s8[4194304]{0:T(1024)(128)(4,1)S(1)}, s32[]{:S(2)}) async-start(s8[8388608]{0:T(1024)(128)(4,1)} %bitcast.51), calls=%async_computation.1 | async-start | bytes 8388608
  83.0 11.8 %collective-permute-start.23 = (bf16[512,128]{1,0:T(8,128)(2,1)S(1)}, bf16[512,128]{1,0:T(8,128)(2,1)S(1)}, u32[]{:S(2)}, u32[]{:S(2)}) collective-permute-start(bf16[512,128]{1,0:T(8,128)(2,1)S(1)} %select_convert_fusion.1), channel_id=1, source_target_pairs={{0,16},{8,24},{16,0},{24,8},{1,17},{9,25},{17,1},{25,9},{2,18},{10... | collective-permute-start | bytes 393224 | tf_op jit(solution)/shard_map/ppermute | solution.py:163
  95.0 15.5 %collective-permute-start.28 = (bf16[512,128]{1,0:T(8,128)(2,1)S(1)}, bf16[512,128]{1,0:T(8,128)(2,1)S(1)}, u32[]{:S(2)}, u32[]{:S(2)}) collective-permute-start(bf16[512,128]{1,0:T(8,128)(2,1)S(1)} %get-tuple-element.73), channel_id=1, source_target_pairs={{0,8},{8,0},{16,24},{24,16},{1,9},{9,1},{17,25},{25,17},{2,10},{10... | collective-permute-start | bytes 393224 | tf_op jit(solution)/shard_map/ppermute | solution.py:163
  95.8 14.8 %collective-permute-start.27 = (bf16[256,512]{1,0:T(8,128)(2,1)S(1)}, bf16[256,512]{1,0:T(8,128)(2,1)S(1)}, u32[]{:S(2)}, u32[]{:S(2)}) collective-permute-start(bf16[256,512]{1,0:T(8,128)(2,1)S(1)} %select_convert_fusion), channel_id=1, source_target_pairs={{0,16},{8,24},{16,0},{24,8},{1,17},{9,25},{17,1},{25,9},{2,18},{10... | collective-permute-start | bytes 786440 | tf_op jit(solution)/shard_map/ppermute | solution.py:163
  98.0 12.6 %collective-permute-start.29 = (bf16[128,2048]{1,0:T(8,128)(2,1)S(1)}, bf16[128,2048]{1,0:T(8,128)(2,1)S(1)}, u32[]{:S(2)}, u32[]{:S(2)}) collective-permute-start(bf16[128,2048]{1,0:T(8,128)(2,1)S(1)} %get-tuple-element.74), channel_id=1, source_target_pairs={{0,4},{1,5},{2,6},{3,7},{4,0},{5,1},{6,2},{7,3},{8,12},{9,13},{10,... | collective-permute-start | bytes 1572872 | tf_op jit(solution)/shard_map/ppermute | solution.py:163
  98.5 12.2 %collective-permute-start.30 = (bf16[128,2048]{1,0:T(8,128)(2,1)S(1)}, bf16[128,2048]{1,0:T(8,128)(2,1)S(1)}, u32[]{:S(2)}, u32[]{:S(2)}) collective-permute-start(bf16[128,2048]{1,0:T(8,128)(2,1)S(1)} %get-tuple-element.75), channel_id=1, source_target_pairs={{0,2},{1,3},{2,0},{3,1},{4,6},{5,7},{6,4},{7,5},{8,10},{9,11},{10,... | collective-permute-start | bytes 1572872 | tf_op jit(solution)/shard_map/ppermute | solution.py:163
  111.7 3.9 %collective-permute-start.31 = (bf16[4,128,512]{2,1,0:T(8,128)(2,1)S(1)}, bf16[4,128,512]{2,1,0:T(8,128)(2,1)S(1)}, u32[]{:S(2)}, u32[]{:S(2)}) collective-permute-start(bf16[4,128,512]{2,1,0:T(8,128)(2,1)S(1)} %get-tuple-element.81), channel_id=1, source_target_pairs={{0,1},{1,0},{2,3},{3,2},{4,5},{5,4},{6,7},{7,6},{8,9},{9,8},{10,11... | collective-permute-start | bytes 1572872 | tf_op jit(solution)/shard_map/ppermute | solution.py:163
  111.8 14.8 %collective-permute-start.35 = (bf16[128,2048]{1,0:T(8,128)(2,1)S(1)}, bf16[128,2048]{1,0:T(8,128)(2,1)S(1)}, u32[]{:S(2)}, u32[]{:S(2)}) collective-permute-start(bf16[128,2048]{1,0:T(8,128)(2,1)S(1)} %get-tuple-element.87), channel_id=1, source_target_pairs={{0,4},{1,5},{2,6},{3,7},{4,0},{5,1},{6,2},{7,3},{8,12},{9,13},{10,... | collective-permute-start | bytes 1572872 | tf_op jit(solution)/shard_map/ppermute | solution.py:163
  113.3 14.8 %collective-permute-start.36 = (bf16[128,2048]{1,0:T(8,128)(2,1)S(1)}, bf16[128,2048]{1,0:T(8,128)(2,1)S(1)}, u32[]{:S(2)}, u32[]{:S(2)}) collective-permute-start(bf16[128,2048]{1,0:T(8,128)(2,1)S(1)} %get-tuple-element.88), channel_id=1, source_target_pairs={{0,2},{1,3},{2,0},{3,1},{4,6},{5,7},{6,4},{7,5},{8,10},{9,11},{10,... | collective-permute-start | bytes 1572872 | tf_op jit(solution)/shard_map/ppermute | solution.py:163
  116.1 17.6 %collective-permute-start.32 = (bf16[256,512]{1,0:T(8,128)(2,1)S(1)}, bf16[256,512]{1,0:T(8,128)(2,1)S(1)}, u32[]{:S(2)}, u32[]{:S(2)}) collective-permute-start(bf16[256,512]{1,0:T(8,128)(2,1)S(1)} %get-tuple-element.83), channel_id=1, source_target_pairs={{0,2},{1,3},{2,0},{3,1},{4,6},{5,7},{6,4},{7,5},{8,10},{9,11},{10,... | collective-permute-start | bytes 786440 | tf_op jit(solution)/shard_map/ppermute | solution.py:163
  117.4 16.3 %collective-permute-start.33 = (bf16[256,512]{1,0:T(8,128)(2,1)S(1)}, bf16[256,512]{1,0:T(8,128)(2,1)S(1)}, u32[]{:S(2)}, u32[]{:S(2)}) collective-permute-start(bf16[256,512]{1,0:T(8,128)(2,1)S(1)} %get-tuple-element.84), channel_id=1, source_target_pairs={{0,4},{1,5},{2,6},{3,7},{4,0},{5,1},{6,2},{7,3},{8,12},{9,13},{10,... | collective-permute-start | bytes 786440 | tf_op jit(solution)/shard_map/ppermute | solution.py:163
  118.0 20.6 %collective-permute-start.34 = (bf16[256,512]{1,0:T(8,128)(2,1)S(1)}, bf16[256,512]{1,0:T(8,128)(2,1)S(1)}, u32[]{:S(2)}, u32[]{:S(2)}) collective-permute-start(bf16[256,512]{1,0:T(8,128)(2,1)S(1)} %get-tuple-element.85), channel_id=1, source_target_pairs={{0,6},{1,7},{2,4},{3,5},{4,2},{5,3},{6,0},{7,1},{8,14},{9,15},{10,... | collective-permute-start | bytes 786440 | tf_op jit(solution)/shard_map/ppermute | solution.py:163
